TPU v7x, 32 devices: a whole 2x2x4 slice. The times are simulated.
32 devices in a mesh: seq: 8 (over z, core), fsdp: 4 (over y, x).
Axes of the slice: x: 2, y: 2, z: 4, core: 2. Of those that a mesh axis runs over, the one named last changes fastest.
Arguments:
- tokens: bfloat16 [4, 2048, 1024], P('fsdp', 'seq'), may hold values from -6 to 6
- seq_lengths: int32 [4, 4], P('fsdp'), may hold values from 1 to 1024, 2048 in all within a row
- seq_order: int32 [4, 2048], P('fsdp'), may hold values from 0 to 2047, each once within a row
- norm_one: bfloat16 [1024], P('fsdp'), may hold values from 0.5 to 1.5
- w_qkv: bfloat16 [1024, 3072], P('fsdp'), may hold values from -0.25 to 0.25
- w_out: bfloat16 [1024, 1024], P('fsdp'), may hold values from -0.75 to 0.75
- norm_two: bfloat16 [1024], P('fsdp'), may hold values from 0.5 to 1.5
- w_in: bfloat16 [1024, 5248], P('fsdp'), may hold values from -0.1875 to 0.1875
- w_down: bfloat16 [2624, 1024], P('fsdp'), may hold values from -0.15625 to 0.15625
- cotangent: bfloat16 [4, 2048, 1024], P('fsdp', 'seq'), may hold values from -6 to 6
Outputs:
- layer_out: bfloat16 [4, 2048, 1024], P('fsdp', 'seq')
- grad_tokens: bfloat16 [4, 2048, 1024], P('fsdp', 'seq')
- grad_norm_one: float32 [1024], P('fsdp')
- grad_w_qkv: float32 [1024, 3072], P('fsdp')
- grad_w_out: float32 [1024, 1024], P('fsdp')
- grad_norm_two: float32 [1024], P('fsdp')
- grad_w_in: float32 [1024, 5248], P('fsdp')
- grad_w_down: float32 [2624, 1024], P('fsdp')
Inputs may be any that keep to these rules, and one draw needn't show every extreme that they name: `seq_lengths`: each row holds the lengths of the 4 sequences packed one after another in a group; they sum to 2048 and the longest has exactly 1024 tokens. `seq_order`: each row holds every number of 0 to 2047 once.
All inputs are finite; a program needn't handle non-finite values.
Results may differ from a plain program's by a relative error of at most 0.017.
The roundings to bfloat16 on the way count: a program that leaves them out, or rounds other values in their place, can miss the bound.
Values may be sent and summed in bfloat16 or wider, within the bound.
No kernel may reach another device: no remote copies, remote signals or barrier semaphores. Data moves between devices by JAX's collectives and lax.ppermute only.
A program may use at most 192 MiB of HBM per device.

v0:
```python
import jax
import jax.numpy as jnp
from jax import lax
from jax.sharding import PartitionSpec as P

HD = 64


NORM_EPS = 1e-05
ROPE_BASE = 160000.0
MASKED = -1000000000.0


def norm_rows(values, gain):
    center = values - jnp.mean(values, axis=-1, keepdims=True)
    spread = jnp.mean(center * center, axis=-1, keepdims=True)
    return center * lax.rsqrt(spread + NORM_EPS) * gain


def rotate(values, places):
    full_width = values.shape[-1]
    half_width = full_width // 2
    index_half = jnp.arange(half_width, dtype=jnp.float32)
    inverse_freq = jnp.power(jnp.float32(ROPE_BASE), -2.0 * index_half / full_width)
    angles = places.astype(jnp.float32)[:, None] * inverse_freq[None, :]
    cosine = jnp.cos(angles)[:, None, :]
    sine = jnp.sin(angles)[:, None, :]
    first_half = values[..., :half_width]
    second_half = values[..., half_width:]
    return jnp.concatenate(
        [first_half * cosine - second_half * sine, second_half * cosine + first_half * sine],
        axis=-1,
    )


def seq_layout(lengths_row, row_count):
    ends = jnp.cumsum(lengths_row)
    indices = jnp.arange(row_count, dtype=jnp.int32)
    passed = (indices[:, None] >= ends[None, :]).astype(jnp.int32)
    segment = jnp.sum(passed, axis=1)
    starts = jnp.sum(passed * lengths_row[None, :], axis=1)
    return (segment, indices - starts)


def geglu(both_parts):
    half_width = both_parts.shape[-1] // 2
    return jax.nn.gelu(both_parts[:, :half_width], approximate=False) * both_parts[:, half_width:]


def block_scores(query_blk, seg_blk, key_all, seg_all):
    score_scale = query_blk.shape[-1] ** (-0.5)
    raw = jnp.einsum("qhd,khd->hqk", query_blk, key_all, preferred_element_type=jnp.float32)
    same_seq = seg_blk[None, :, None] == seg_all[None, None, :]
    return (jnp.where(same_seq, raw * score_scale, MASKED), same_seq, score_scale)


def forward_block(query_blk, seg_blk, key_all, value_all, seg_all):
    scores, same_seq, score_scale = block_scores(query_blk, seg_blk, key_all, seg_all)
    row_top = jnp.max(scores, axis=-1, keepdims=True)
    shifted = jnp.exp(scores - row_top)
    row_total = jnp.sum(shifted, axis=-1, keepdims=True)
    probs = (shifted / row_total).astype(jnp.bfloat16)
    attended = jnp.einsum("hqk,khd->qhd", probs, value_all, preferred_element_type=jnp.float32)
    return (attended.astype(jnp.bfloat16), row_top + jnp.log(row_total))


def attend(query, key_all, value_all, segment):
    group_rows = query.shape[0]
    block_rows = min(512, group_rows)
    block_count = group_rows // block_rows
    query_blocks = query.reshape(block_count, block_rows, query.shape[1], query.shape[2])
    seg_blocks = segment.reshape(block_count, block_rows)

    def one_block(paired):
        return forward_block(paired[0], paired[1], key_all, value_all, segment)

    attended, log_sums = lax.map(one_block, (query_blocks, seg_blocks))
    return (attended.reshape(query.shape), log_sums)


def attend_back(query, key_all, value_all, segment, log_sums, grad_out):
    group_rows = query.shape[0]
    block_rows = min(512, group_rows)
    block_count = group_rows // block_rows
    query_blocks = query.reshape(block_count, block_rows, query.shape[1], query.shape[2])
    seg_blocks = segment.reshape(block_count, block_rows)
    dout_blocks = grad_out.reshape(block_count, block_rows, query.shape[1], query.shape[2])

    def one_block(carried, inputs_blk):
        grad_key, grad_value = carried
        query_blk, seg_blk, lse_blk, dout_blk = inputs_blk
        scores, same_seq, score_scale = block_scores(query_blk, seg_blk, key_all, segment)
        probs = jnp.exp(scores - lse_blk)
        grad_probs = jnp.einsum(
            "qhd,khd->hqk", dout_blk, value_all, preferred_element_type=jnp.float32
        )
        centre = jnp.sum(probs * grad_probs, axis=-1, keepdims=True)
        grad_raw = jnp.where(same_seq, probs * (grad_probs - centre) * score_scale, 0.0).astype(
            jnp.bfloat16
        )
        grad_query = jnp.einsum(
            "hqk,khd->qhd", grad_raw, key_all, preferred_element_type=jnp.float32
        )
        grad_key = grad_key + jnp.einsum(
            "hqk,qhd->khd", grad_raw, query_blk, preferred_element_type=jnp.float32
        )
        grad_value = grad_value + jnp.einsum(
            "hqk,qhd->khd", probs.astype(jnp.bfloat16), dout_blk, preferred_element_type=jnp.float32
        )
        return ((grad_key, grad_value), grad_query)

    zeros_kv = jnp.zeros(key_all.shape, jnp.float32)
    sums_kv, grad_query = lax.scan(
        one_block, (zeros_kv, zeros_kv), (query_blocks, seg_blocks, log_sums, dout_blocks)
    )
    return (grad_query.reshape(query.shape), sums_kv[0], sums_kv[1])


def first_part(token_rows, gain_one, weight_qkv):
    normed_one = norm_rows(token_rows, gain_one.astype(jnp.float32)).astype(jnp.bfloat16)
    qkv = jnp.dot(normed_one, weight_qkv, preferred_element_type=jnp.float32).astype(jnp.bfloat16)
    return (normed_one, qkv)


def middle_part(heads_rows, lengths_row, order_row):
    group_rows = heads_rows.shape[0]
    head_width = heads_rows.shape[-1]
    local_heads = head_width // HD
    packed = jnp.take(heads_rows.reshape(group_rows, 3 * head_width), order_row, axis=0)
    packed = packed.reshape(group_rows, 3, local_heads, HD)
    segment, places = seq_layout(lengths_row, group_rows)
    query = rotate(packed[:, 0].astype(jnp.float32), places).astype(jnp.bfloat16)
    key_all = rotate(packed[:, 1].astype(jnp.float32), places).astype(jnp.bfloat16)
    value_all = packed[:, 2]
    attended, log_sums = attend(query, key_all, value_all, segment)
    inverse = (
        jnp.zeros((group_rows,), jnp.int32)
        .at[order_row]
        .set(jnp.arange(group_rows, dtype=jnp.int32))
    )
    arrival = jnp.take(attended.reshape(group_rows, head_width), inverse, axis=0)
    return (query, key_all, value_all, segment, places, inverse, log_sums, arrival)


def last_part(token_rows, attn_rows, weight_out, gain_two, weight_in, weight_down):
    middle = token_rows + jnp.dot(attn_rows, weight_out, preferred_element_type=jnp.float32)
    normed_two = norm_rows(middle, gain_two.astype(jnp.float32)).astype(jnp.bfloat16)
    both_parts = jnp.dot(normed_two, weight_in, preferred_element_type=jnp.float32)
    hidden = geglu(both_parts).astype(jnp.bfloat16)
    layer_rows = middle + jnp.dot(hidden, weight_down, preferred_element_type=jnp.float32)
    return (middle, normed_two, both_parts, hidden, layer_rows)


def local(
    tokens, seq_lengths, seq_order, norm_one, w_qkv, w_out, norm_two, w_in, w_down, cotangent
):
    seq_count = lax.axis_size("seq")
    token_rows = tokens[0].astype(jnp.float32)
    local_rows = token_rows.shape[0]
    lengths_row = seq_lengths[0]
    order_row = seq_order[0]
    gathered = (
        lax.all_gather(norm_one, "fsdp", axis=0, tiled=True),
        lax.all_gather(w_qkv, "fsdp", axis=0, tiled=True),
        lax.all_gather(w_out, "fsdp", axis=0, tiled=True),
        lax.all_gather(norm_two, "fsdp", axis=0, tiled=True),
        lax.all_gather(w_in, "fsdp", axis=0, tiled=True),
        lax.all_gather(w_down, "fsdp", axis=0, tiled=True),
    )
    normed_one, qkv = first_part(token_rows, gathered[0], gathered[1])
    heads_rows = lax.all_to_all(
        qkv.reshape(local_rows, 3, seq_count, -1), "seq", split_axis=2, concat_axis=0, tiled=True
    )
    query, key_all, value_all, segment, places, inverse, log_sums, arrival = middle_part(
        heads_rows, lengths_row, order_row
    )
    attn_rows = lax.all_to_all(
        arrival.reshape(arrival.shape[0], 1, -1), "seq", split_axis=0, concat_axis=1, tiled=True
    ).reshape(local_rows, -1)
    middle, normed_two, both_parts, hidden, layer_rows = last_part(
        token_rows, attn_rows, gathered[2], gathered[3], gathered[4], gathered[5]
    )
    layer_out = layer_rows.astype(jnp.bfloat16)[None]
    gathered = (
        lax.all_gather(norm_one, "fsdp", axis=0, tiled=True),
        lax.all_gather(w_qkv, "fsdp", axis=0, tiled=True),
        lax.all_gather(w_out, "fsdp", axis=0, tiled=True),
        lax.all_gather(norm_two, "fsdp", axis=0, tiled=True),
        lax.all_gather(w_in, "fsdp", axis=0, tiled=True),
        lax.all_gather(w_down, "fsdp", axis=0, tiled=True),
    )
    normed_one, qkv = first_part(token_rows, gathered[0], gathered[1])
    heads_rows = lax.all_to_all(
        qkv.reshape(local_rows, 3, seq_count, -1), "seq", split_axis=2, concat_axis=0, tiled=True
    )
    query, key_all, value_all, segment, places, inverse, log_sums, arrival = middle_part(
        heads_rows, lengths_row, order_row
    )
    attn_rows = lax.all_to_all(
        arrival.reshape(arrival.shape[0], 1, -1), "seq", split_axis=0, concat_axis=1, tiled=True
    ).reshape(local_rows, -1)
    middle, normed_two, both_parts, hidden, layer_rows = last_part(
        token_rows, attn_rows, gathered[2], gathered[3], gathered[4], gathered[5]
    )
    gain_one = gathered[0].astype(jnp.float32)
    weight_qkv = gathered[1]
    weight_out = gathered[2]
    gain_two = gathered[3].astype(jnp.float32)
    weight_in = gathered[4]
    weight_down = gathered[5]
    grad_out = cotangent[0]
    grad_wdown = jnp.einsum("tf,td->fd", hidden, grad_out, preferred_element_type=jnp.float32)
    grad_hidden = jnp.einsum("td,fd->tf", grad_out, weight_down, preferred_element_type=jnp.float32)
    grad_both = jax.vjp(geglu, both_parts)[1](grad_hidden)[0].astype(jnp.bfloat16)
    grad_win = jnp.einsum("td,tf->df", normed_two, grad_both, preferred_element_type=jnp.float32)
    grad_normed_two = jnp.einsum(
        "tf,df->td", grad_both, weight_in, preferred_element_type=jnp.float32
    )
    grad_mid_norm, grad_gain_two = jax.vjp(norm_rows, middle, gain_two)[1](grad_normed_two)
    grad_middle = grad_out.astype(jnp.float32) + grad_mid_norm
    grad_branch = grad_middle.astype(jnp.bfloat16)
    grad_wout = jnp.einsum("td,te->de", attn_rows, grad_branch, preferred_element_type=jnp.float32)
    grad_attn = jnp.einsum(
        "te,de->td", grad_branch, weight_out, preferred_element_type=jnp.float32
    ).astype(jnp.bfloat16)
    dout_rows = lax.all_to_all(
        grad_attn.reshape(local_rows, seq_count, -1), "seq", split_axis=1, concat_axis=0, tiled=True
    )
    group_rows = dout_rows.shape[0]
    dout_packed = jnp.take(dout_rows.reshape(group_rows, -1), order_row, axis=0).reshape(
        query.shape
    )
    grad_query_rot, grad_key_rot, grad_value = attend_back(
        query, key_all, value_all, segment, log_sums, dout_packed
    )

    def rotate_here(values):
        return rotate(values, places)

    rotate_back = jax.vjp(rotate_here, jnp.zeros(query.shape, jnp.float32))[1]
    grad_query = rotate_back(grad_query_rot)[0]
    grad_key = rotate_back(grad_key_rot)[0]
    grad_packed = jnp.stack([grad_query, grad_key, grad_value], axis=1).astype(jnp.bfloat16)
    grad_arrival = jnp.take(grad_packed.reshape(group_rows, -1), inverse, axis=0).reshape(
        group_rows, 3, 1, -1
    )
    grad_qkv = lax.all_to_all(grad_arrival, "seq", split_axis=0, concat_axis=2, tiled=True).reshape(
        local_rows, -1
    )
    grad_wqkv = jnp.einsum("td,te->de", normed_one, grad_qkv, preferred_element_type=jnp.float32)
    grad_normed_one = jnp.einsum(
        "te,de->td", grad_qkv, weight_qkv, preferred_element_type=jnp.float32
    )
    grad_rows_norm, grad_gain_one = jax.vjp(norm_rows, token_rows, gain_one)[1](grad_normed_one)
    grad_tokens = (grad_middle + grad_rows_norm).astype(jnp.bfloat16)[None]
    grad_gains = jnp.stack([grad_gain_one, grad_gain_two], axis=1)
    shares = (
        lax.psum_scatter(grad_gains, "fsdp", scatter_dimension=0, tiled=True),
        lax.psum_scatter(grad_wqkv, "fsdp", scatter_dimension=0, tiled=True),
        lax.psum_scatter(grad_wout, "fsdp", scatter_dimension=0, tiled=True),
        lax.psum_scatter(grad_win, "fsdp", scatter_dimension=0, tiled=True),
        lax.psum_scatter(grad_wdown, "fsdp", scatter_dimension=0, tiled=True),
    )
    owned = lax.psum((shares[0], shares[1], shares[2], shares[3], shares[4]), "seq")
    return (
        layer_out,
        grad_tokens,
        owned[0][:, 0],
        owned[1],
        owned[2],
        owned[0][:, 1],
        owned[3],
        owned[4],
    )


def solution(mesh):
    placed = (
        P("fsdp", "seq", None),
        P("fsdp", None),
        P("fsdp", None),
        P("fsdp"),
        P("fsdp", None),
        P("fsdp", None),
        P("fsdp"),
        P("fsdp", None),
        P("fsdp", None),
        P("fsdp", "seq", None),
    )
    return jax.shard_map(
        local,
        mesh=mesh,
        in_specs=placed,
        out_specs=(
            P("fsdp", "seq", None),
            P("fsdp", "seq", None),
            P("fsdp"),
            P("fsdp", None),
            P("fsdp", None),
            P("fsdp"),
            P("fsdp", None),
            P("fsdp", None),
        ),
        check_vma=False,
    )
```

profile of v0, /device:TPU:1, one launch (start us, length us, event | category | flops | bytes accessed | tf_op | source)
XLA Modules:
  0.0 1279.5 jit_solution(9339651831316924684)
XLA Ops:
  17.4 64.8 %all-gather.7.cloned.1.call-done = bf16[1024,3072]{1,0:T(8,128)(2,1)} async-done(((bf16[256,3072]{1,0:T(8,128)(2,1)}), bf16[1024,3072]{1,0:T(8,128)(2,1)}) %all-gather.7.cloned.1.call-update) | async-done | bytes 6291472 | tf_op jit(solution)/shard_map/all_gather | solution.py:164
  106.7 24.7 %all-to-all-done = bf16[256,3,8,128]{0,3,1,2:T(8,128)(2,1)S(1)} async-done(((bf16[256,3,8,128]{0,3,1,2:T(8,128)(2,1)}), bf16[256,3,8,128]{0,3,1,2:T(8,128)(2,1)S(1)}, u32[]{:S(2)}, u32[]{:S(2)}) %all-to-all-start) | async-done | bytes 1572896 | tf_op jit(solution)/shard_map/all_to_all | solution.py:171
  148.0 33.8 %while.38 = (s32[]{:T(128)}, bf16[4,512,2,64]{1,3,2,0:T(8,128)(2,1)S(1)}, f32[4,2,512,1]{2,1,3,0:T(2,128)}, s32[4,512]{1,0:T(4,128)S(1)}, s32[2048]{0:T(1024)S(1...) while((s32[]{:T(128)}, ...), condition=%wide.region_15.18_spmd, body=%wide.region_12.17_spmd.sunk | while | flops 563149824 | bytes 30718068 | solution.py:77
  183.1 51.3 %while.37 = (s32[]{:T(128)}, bf16[4,512,2,64]{1,3,2,0:T(8,128)(2,1)S(1)}, s32[4,512]{1,0:T(4,128)S(1)}, s32[2048]{0:T(1024)S(1)}, bf16[4,512,2,64]{1,3,2,0:T(8,1...) while((s32[]{:T(128)}, ...), condition=%wide.region_8.10_spmd, body=%wide.region_5.9_spmd.sunk | while | flops 550569984 | bytes 20207720 | solution.py:77
  278.1 9.0 fusion.228
  292.8 11.2 fusion.162
  326.1 9.4 fusion.139
  344.3 14.5 %all-to-all-done.3 = bf16[256,8,128]{2,0,1:T(8,128)(2,1)S(1)} async-done(((bf16[256,8,128]{2,0,1:T(8,128)(2,1)}), bf16[256,8,128]{2,0,1:T(8,128)(2,1)S(1)}, u32[]{:S(2)}, u32[]{:S(2)}) %all-to-all-start.3) | async-done | bytes 524320 | tf_op jit(solution)/shard_map/all_to_all | solution.py:226
  366.5 219.5 %while.39 = (s32[]{:T(128)}, f32[2048,2,64]{0,2,1:T(8,128)}, f32[2048,2,64]{0,2,1:T(8,128)}, f32[4,512,2,64]{1,0,3,2:T(4,128)}, bf16[4,512,2,64]{1,3,2,0:T(8,128...) while((s32[]{:T(128)}, f32[2048,2,64]{0,2,1:T(8,128)}, ...), condition=%wide.region_22.25_spmd.clone, body=%wide.region_20.24_spmd.clone.sunk | while | flops 1403000832 | bytes 88381616 | solution.py:113
  378.1 16.2 %fusion.312 = f32[2048,2,64]{0,2,1:T(8,128)} fusion(f32[2,512,2048]{2,1,0:T(8,128)} %fusion.310, f32[2,512,2048]{2,1,0:T(8,128)} %fusion.311, f32[2,512]{1,0:T(2,128)S(1)} %dynamic-slice_bitcast_fusion.2, pred[512,2048]{1,0:T(8,128)(4,1)S(1)} %broadcast_compare_fusion.8, f32[2048,2,64]{0,2,1:T(8,128)} %get-tuple-element.579, pred[]{:T(512)S(6)} %compare.9, ...), kind=kOutput, calls=%fused_computation.71.clone.1 | convolution fusion | flops 294128640 | bytes 37888004 | tf_op jit(solution)/shard_map/while/body/eval_jaxpr/hqk,qhd->khd/dot_general | solution.py:104
  401.2 14.6 %fusion.314 = f32[1,512,2,64]{1,3,2,0:T(8,128)S(1)} fusion(bf16[2048,2,64]{0,2,1:T(8,128)(2,1)S(1)} %get-tuple-element.598, f32[2,512,2048]{2,1,0:T(8,128)} %fusion.310, f32[2,512,2048]{2,1,0:T(8,128)} %fusion.311, f32[2,512]{1,0:T(2,128)S(1)} %dynamic-slice_bitcast_fusion.2, pred[512,2048]{1,0:T(8,128)(4,1)S(1)} %broadcast_compare_fusion.8), kind=kOutput, calls=%fused_computation.73.clone.1 | convolution fusion | flops 293604352 | bytes 18616320 | tf_op jit(solution)/shard_map/while/body/eval_jaxpr/hqk,khd->qhd/dot_general | solution.py:101
  433.6 15.9 %fusion.312 = f32[2048,2,64]{0,2,1:T(8,128)} fusion(f32[2,512,2048]{2,1,0:T(8,128)} %fusion.310, f32[2,512,2048]{2,1,0:T(8,128)} %fusion.311, f32[2,512]{1,0:T(2,128)S(1)} %dynamic-slice_bitcast_fusion.2, pred[512,2048]{1,0:T(8,128)(4,1)S(1)} %broadcast_compare_fusion.8, f32[2048,2,64]{0,2,1:T(8,128)} %get-tuple-element.579, pred[]{:T(512)S(6)} %compare.9, ...), kind=kOutput, calls=%fused_computation.71.clone.1 | convolution fusion | flops 294128640 | bytes 37888004 | tf_op jit(solution)/shard_map/while/body/eval_jaxpr/hqk,qhd->khd/dot_general | solution.py:104
  456.6 14.4 %fusion.314 = f32[1,512,2,64]{1,3,2,0:T(8,128)S(1)} fusion(bf16[2048,2,64]{0,2,1:T(8,128)(2,1)S(1)} %get-tuple-element.598, f32[2,512,2048]{2,1,0:T(8,128)} %fusion.310, f32[2,512,2048]{2,1,0:T(8,128)} %fusion.311, f32[2,512]{1,0:T(2,128)S(1)} %dynamic-slice_bitcast_fusion.2, pred[512,2048]{1,0:T(8,128)(4,1)S(1)} %broadcast_compare_fusion.8), kind=kOutput, calls=%fused_computation.73.clone.1 | convolution fusion | flops 293604352 | bytes 18616320 | tf_op jit(solution)/shard_map/while/body/eval_jaxpr/hqk,khd->qhd/dot_general | solution.py:101
  488.8 15.6 %fusion.312 = f32[2048,2,64]{0,2,1:T(8,128)} fusion(f32[2,512,2048]{2,1,0:T(8,128)} %fusion.310, f32[2,512,2048]{2,1,0:T(8,128)} %fusion.311, f32[2,512]{1,0:T(2,128)S(1)} %dynamic-slice_bitcast_fusion.2, pred[512,2048]{1,0:T(8,128)(4,1)S(1)} %broadcast_compare_fusion.8, f32[2048,2,64]{0,2,1:T(8,128)} %get-tuple-element.579, pred[]{:T(512)S(6)} %compare.9, ...), kind=kOutput, calls=%fused_computation.71.clone.1 | convolution fusion | flops 294128640 | bytes 37888004 | tf_op jit(solution)/shard_map/while/body/eval_jaxpr/hqk,qhd->khd/dot_general | solution.py:104
  511.5 13.7 %fusion.314 = f32[1,512,2,64]{1,3,2,0:T(8,128)S(1)} fusion(bf16[2048,2,64]{0,2,1:T(8,128)(2,1)S(1)} %get-tuple-element.598, f32[2,512,2048]{2,1,0:T(8,128)} %fusion.310, f32[2,512,2048]{2,1,0:T(8,128)} %fusion.311, f32[2,512]{1,0:T(2,128)S(1)} %dynamic-slice_bitcast_fusion.2, pred[512,2048]{1,0:T(8,128)(4,1)S(1)} %broadcast_compare_fusion.8), kind=kOutput, calls=%fused_computation.73.clone.1 | convolution fusion | flops 293604352 | bytes 18616320 | tf_op jit(solution)/shard_map/while/body/eval_jaxpr/hqk,khd->qhd/dot_general | solution.py:101
  542.9 15.6 %fusion.312 = f32[2048,2,64]{0,2,1:T(8,128)} fusion(f32[2,512,2048]{2,1,0:T(8,128)} %fusion.310, f32[2,512,2048]{2,1,0:T(8,128)} %fusion.311, f32[2,512]{1,0:T(2,128)S(1)} %dynamic-slice_bitcast_fusion.2, pred[512,2048]{1,0:T(8,128)(4,1)S(1)} %broadcast_compare_fusion.8, f32[2048,2,64]{0,2,1:T(8,128)} %get-tuple-element.579, pred[]{:T(512)S(6)} %compare.9, ...), kind=kOutput, calls=%fused_computation.71.clone.1 | convolution fusion | flops 294128640 | bytes 37888004 | tf_op jit(solution)/shard_map/while/body/eval_jaxpr/hqk,qhd->khd/dot_general | solution.py:104
  565.6 13.7 %fusion.314 = f32[1,512,2,64]{1,3,2,0:T(8,128)S(1)} fusion(bf16[2048,2,64]{0,2,1:T(8,128)(2,1)S(1)} %get-tuple-element.598, f32[2,512,2048]{2,1,0:T(8,128)} %fusion.310, f32[2,512,2048]{2,1,0:T(8,128)} %fusion.311, f32[2,512]{1,0:T(2,128)S(1)} %dynamic-slice_bitcast_fusion.2, pred[512,2048]{1,0:T(8,128)(4,1)S(1)} %broadcast_compare_fusion.8), kind=kOutput, calls=%fused_computation.73.clone.1 | convolution fusion | flops 293604352 | bytes 18616320 | tf_op jit(solution)/shard_map/while/body/eval_jaxpr/hqk,khd->qhd/dot_general | solution.py:101
  604.5 51.3 %all_to_all.80 = bf16[2048,3,1,128]{3,1,2,0:T(4,128)(2,1)S(1)} all-to-all(bf16[2048,3,1,128]{3,1,2,0:T(4,128)(2,1)S(1)} %copy.119), channel_id=1, replica_groups=mesh['seq'=8,'fsdp'=4] {'seq'}, dimensions={0} | all-to-all | bytes 3145728 | tf_op jit(solution)/shard_map/all_to_all | solution.py:247
  666.8 11.9 fusion.186
  686.3 98.6 %reduce-scatter.8.cloned.1.call-done = f32[256,3072]{1,0:T(8,128)} async-done(((f32[1024,3072]{1,0:T(8,128)}), f32[256,3072]{1,0:T(8,128)}) %reduce-scatter.8.cloned.1.call-update) | async-done | bytes 3145744 | tf_op jit(solution)/shard_map/reduce_scatter | solution.py:259
  784.9 195.5 %reduce-scatter.12.cloned.1.call-done = f32[256,5248]{1,0:T(8,128)} async-done(((f32[1024,5248]{1,0:T(8,128)}), f32[256,5248]{1,0:T(8,128)}) %reduce-scatter.12.cloned.1.call-update) | async-done | bytes 5373968 | tf_op jit(solution)/shard_map/reduce_scatter | solution.py:261
  982.6 19.6 %all_to_all.81 = bf16[8,2,16384]{2,1,0:T(2,128)(2,1)S(1)} all-to-all(bf16[8,2,16384]{2,1,0:T(2,128)(2,1)S(1)} %reshape.516), channel_id=1, replica_groups=mesh['seq'=8,'fsdp'=4] {'seq'}, dimensions={0} | all-to-all | bytes 1048576 | tf_op jit(solution)/shard_map/all_to_all | solution.py:177
  1022.9 14.3 %psum.35 = f32[256,2]{0,1:T(2,128)S(1)} all-reduce(f32[256,2]{0,1:T(2,128)S(1)} %copy.129), channel_id=1, replica_groups=mesh['seq'=8,'fsdp'=4] {'seq'}, use_global_device_ids=true, to_apply=%region_28.31 | all-reduce | flops 512 | bytes 4096 | tf_op jit(solution)/shard_map/psum | solution.py:264
  1037.8 223.1 %all-reduce.9.cloned.1.call-done = (f32[256,3072]{1,0:T(8,128)}, f32[256,1024]{1,0:T(8,128)}, f32[256,5248]{1,0:T(8,128)}, f32[656,1024]{1,0:T(8,128)}) async-done(((f32[256,3072]{1,0:T(8,128)}, f32[256,1024]{1,0:T(8,128)}, f32[256,5248]{1,0:T(8,128)}, f32[656,1024]{1,0:T(8,128)}), (f32[256,3072]{1,0:T(8,128)}, f32[256,1024]{1,0:T(8,128)}, f32[256,5248]{1,0:T(8,128)}, ...) | async-done | bytes 12255248 | tf_op jit(solution)/shard_map/psum | solution.py:264
  (336 shorter events, 395.3 us)
Async XLA Ops:
  7.2 75.0 %all-gather.7.cloned.1.call-start = ((), (), s32[]{:S(2)}) async-start(), calls=%async_computation.10 | async-start | bytes 7864320 | tf_op jit(solution)/shard_map/all_gather | solution.py:164
  7.9 267.2 %all-gather.9.cloned.1.call-start = ((), (), s32[]{:S(2)}) async-start(), calls=%async_computation.11 | async-start | bytes 2621440 | tf_op jit(solution)/shard_map/all_gather | solution.py:165
  8.7 269.4 %all-gather.11.cloned.1.call-start = ((), (), s32[]{:S(2)}) async-start(), calls=%async_computation.12 | async-start | bytes 13434880 | tf_op jit(solution)/shard_map/all_gather | solution.py:167
  16.3 65.8 %copy-start.33 = (f32[4,1,256]{2,1,0:T(1,128)}, f32[4,1,256]{2,1,0:T(1,128)S(1)}, u32[]{:S(2)}) copy-start(f32[4,1,256]{2,1,0:T(1,128)S(1)} %convert_element_type.150) | copy-start | bytes 12292
  16.5 65.7 %copy-start.44 = (f32[256]{0:T(256)}, f32[256]{0:T(256)S(1)}, u32[]{:S(2)}) copy-start(f32[256]{0:T(256)S(1)} %broadcast_multiply_fusion.2) | copy-start | bytes 3076
  17.4 64.8 %copy-start.46 = (f32[256]{0:T(256)}, f32[256]{0:T(256)S(1)}, u32[]{:S(2)}) copy-start(f32[256]{0:T(256)S(1)} %fusion.192) | copy-start | bytes 3076
  89.0 42.4 %all-to-all-start = ((bf16[256,3,8,128]{0,3,1,2:T(8,128)(2,1)}), bf16[256,3,8,128]{0,3,1,2:T(8,128)(2,1)S(1)}, u32[]{:S(2)}, u32[]{:S(2)}) async-start(bf16[256,3,8,128]{0,3,1,2:T(8,128)(2,1)} %copy.97), calls=%async_computation | async-start | bytes 3145728 | tf_op jit(solution)/shard_map/all_to_all | solution.py:171
  94.4 198.4 %all-gather.13.cloned.1.call-start = ((), (), s32[]{:S(2)}) async-start(), calls=%async_computation.13 | async-start | bytes 6717440 | tf_op jit(solution)/shard_map/all_gather | solution.py:168
  103.7 39.7 %copy-start.50 = (pred[2048]{0:T(1024)(128)(4,1)}, pred[2048]{0:T(1024)(128)(4,1)S(1)}, u32[]{:S(2)}) copy-start(pred[2048]{0:T(1024)(128)(4,1)S(1)} %compare_and_fusion.1) | copy-start | bytes 6148
  104.3 31.7 %copy-start.37 = (s32[2048]{0:T(1024)}, s32[2048]{0:T(1024)S(1)}, u32[]{:S(2)}) copy-start(s32[2048]{0:T(1024)S(1)} %fusion.188) | copy-start | bytes 24580
  255.0 18.7 %all-to-all-start.2 = ((bf16[8,2,16384]{2,1,0:T(2,128)(2,1)}), bf16[8,2,16384]{2,1,0:T(2,128)(2,1)S(1)}, u32[]{:S(2)}, u32[]{:S(2)}) async-start(bf16[8,2,16384]{2,1,0:T(2,128)(2,1)} %reshape.518), calls=%async_computation.2 | async-start | bytes 1048576 | tf_op jit(solution)/shard_map/all_to_all | solution.py:199
  259.2 427.1 %reduce-scatter.10.cloned.1.call-start = ((), (), s32[]{:S(2)}) async-start(), calls=%async_computation.15 | async-start | bytes 5242880 | tf_op jit(solution)/shard_map/reduce_scatter | solution.py:260
  266.0 51.8 %copy-start.31 = (f32[4,1,256]{2,1,0:T(1,128)}, f32[4,1,256]{2,1,0:T(1,128)S(1)}, u32[]{:S(2)}) copy-start(f32[4,1,256]{2,1,0:T(1,128)S(1)} %convert_element_type.151) | copy-start | bytes 12292
  277.7 40.0 %copy-start.40 = (f32[256]{0:T(256)}, f32[256]{0:T(256)S(1)}, u32[]{:S(2)}) copy-start(f32[256]{0:T(256)S(1)} %broadcast_multiply_fusion) | copy-start | bytes 3076
  278.0 39.8 %copy-start.42 = (f32[256]{0:T(256)}, f32[256]{0:T(256)S(1)}, u32[]{:S(2)}) copy-start(f32[256]{0:T(256)S(1)} %fusion.193) | copy-start | bytes 3076
  324.4 361.9 %reduce-scatter.14.cloned.1.call-start = ((), (), s32[]{:S(2)}) async-start(), calls=%async_computation.17 | async-start | bytes 13434880 | tf_op jit(solution)/shard_map/reduce_scatter | solution.py:262
  337.2 21.6 %copy-start.38 = (s32[2048]{0:T(1024)S(1)}, s32[2048]{0:T(1024)}, u32[]{:S(2)}) copy-start(s32[2048]{0:T(1024)} %copy-done.37) | copy-start | bytes 24580
  338.9 26.1 %copy-start.51 = (pred[2048]{0:T(1024)(128)(4,1)S(1)}, pred[2048]{0:T(1024)(128)(4,1)}, u32[]{:S(2)}) copy-start(pred[2048]{0:T(1024)(128)(4,1)} %copy-done.50) | copy-start | bytes 6148
  338.9 19.9 %all-to-all-start.3 = ((bf16[256,8,128]{2,0,1:T(8,128)(2,1)}), bf16[256,8,128]{2,0,1:T(8,128)(2,1)S(1)}, u32[]{:S(2)}, u32[]{:S(2)}) async-start(bf16[256,8,128]{2,0,1:T(8,128)(2,1)} %bitcast.216), calls=%async_computation.3 | async-start | bytes 1048576 | tf_op jit(solution)/shard_map/all_to_all | solution.py:226
  344.3 440.6 %reduce-scatter.8.cloned.1.call-start = ((), (), s32[]{:S(2)}) async-start(), calls=%async_computation.14 | async-start | bytes 15728640 | tf_op jit(solution)/shard_map/reduce_scatter | solution.py:259
  366.5 221.5 %copy-start.24 = (f32[2048,32]{0,1:T(8,128)S(1)}, f32[2048,32]{0,1:T(8,128)}, u32[]{:S(2)}) copy-start(f32[2048,32]{0,1:T(8,128)} %get-tuple-element.331) | copy-start | bytes 786436
  665.6 314.8 %reduce-scatter.12.cloned.1.call-start = ((), (), s32[]{:S(2)}) async-start(), calls=%async_computation.16 | async-start | bytes 26869760 | tf_op jit(solution)/shard_map/reduce_scatter | solution.py:261
  678.7 343.2 %reduce-scatter.16.cloned.1.call-start = ((), (), s32[]{:S(2)}) async-start(), calls=%async_computation.18 | async-start | bytes 655360
  686.2 574.7 %all-reduce.9.cloned.1.call-start = ((), (), s32[]{:S(2)}) async-start(), calls=%async_computation.19 | async-start | bytes 24510464 | tf_op jit(solution)/shard_map/psum | solution.py:264
  (51 other events, 250.7 us)
Sparse Core Ops, SparseCore 0:
  9.9 72.2 all-gather.6
  84.0 35.2 all-gather.8
  121.2 107.2 all-gather.10
  230.2 62.5 all-gather.12
  324.5 52.6 reduce-scatter.9
  380.5 105.6 reduce-scatter.13
  665.8 119.1 reduce-scatter.7
  788.4 192.0 reduce-scatter.11
  983.9 24.6 reduce-scatter.15
  1011.2 249.6 all-reduce.8
where the time goes:
time: 1290 us; the launch traced here: 1280 us
  waiting for transfers between devices  637 us (49%)
  matrix products  343 us (27%)
  local copies, waits for them, and re-layouts  129 us (10%)
  blocking collectives  98.9 us (8%)
  other arithmetic  39.4 us (3%)
  between operations  15.4 us (1%)
  starting transfers between devices  15.3 us (1%)
    psum x1, waiting for transfers between devices, local(): lax.psum((shares[0], shares[1], shares[2], shares[3], shares[4]), 'seq')  223 us
    reduce_scatter x1, waiting for transfers between devices, local(): lax.psum_scatter(grad_win, 'fsdp', scatter_dimension=0, tiled=True)  196 us
    reduce_scatter x1, waiting for transfers between devices, local(): lax.psum_scatter(grad_wqkv, 'fsdp', scatter_dimension=0, tiled=True)  98.6 us
    all_gather x1, waiting for transfers between devices, local(): lax.all_gather(w_qkv, 'fsdp', axis=0, tiled=True)  64.8 us
    dot_general x4, matrix products, one_block(): jnp.einsum('hqk,qhd->khd', grad_raw, query_blk, preferred_element_type=jn...  63.2 us
    dot_general x4, matrix products, one_block(): jnp.einsum('hqk,khd->qhd', grad_raw, key_all, preferred_element_type=jnp....  56.4 us
    all_to_all x1, blocking collectives, local(): lax.all_to_all(grad_arrival, 'seq', split_axis=0, concat_axis=2, tiled=True)  51.3 us
    unnamed x142, local copies, waits for them, and re-layouts  33.4 us
  transfers between devices with their start and end apart: 13, of which 8 were waited for; matrix products, arithmetic and copies ran while one was open for 36% of the time, Pallas kernels for 0%

commit v1 on v0

v1 whole, which is shorter than its diff:
```python
import functools
import math

import jax
import jax.numpy as jnp
from jax import lax
from jax.experimental import pallas as pl
from jax.experimental.pallas import tpu as pltpu
from jax.sharding import PartitionSpec as P

HD = 64
NORM_EPS = 1e-05
ROPE_BASE = 160000.0
BLOCK = 256
LOG2E = math.log2(math.e)
AXES = ("seq", "fsdp")
F32 = jnp.float32
BF16 = jnp.bfloat16
VMEM_LIMIT = 60 * 1024 * 1024


def core_swap(value, seq_count):
    return lax.ppermute(value, "seq", [(i, i ^ 1) for i in range(seq_count)])


def plane_bit(core, phase, levels):
    return (phase + core * (levels // 2)) % levels


def plane_mask(core, key, levels):
    mask = 0
    for phase in range(levels):
        if key >> phase & 1:
            mask |= 1 << plane_bit(core, phase, levels)
    return mask


def plane_swap(value, phase, seq_count, fsdp_count):
    levels = fsdp_count.bit_length() - 1
    pairs = []
    for s in range(seq_count):
        step = 1 << plane_bit(s & 1, phase, levels)
        for f in range(fsdp_count):
            pairs.append((s * fsdp_count + f, s * fsdp_count + (f ^ step)))
    return lax.ppermute(value, AXES, pairs)


def plane_gather(piece, seq_count, fsdp_count):
    pieces = [piece]
    for phase in range(fsdp_count.bit_length() - 1):
        pieces = pieces + [plane_swap(p, phase, seq_count, fsdp_count) for p in pieces]
    return pieces


def plane_reduce(blocks, seq_count, fsdp_count):
    blocks = list(blocks)
    for phase in reversed(range(fsdp_count.bit_length() - 1)):
        got = [
            plane_swap(blocks[(1 << phase) + key], phase, seq_count, fsdp_count)
            for key in range(1 << phase)
        ]
        blocks = [
            (blocks[key].astype(F32) + got[key].astype(F32)).astype(BF16)
            for key in range(1 << phase)
        ]
    return blocks[0]


def line_swap(value, level, seq_count):
    return lax.ppermute(value, "seq", [(i, i ^ (2 << level)) for i in range(seq_count)])


def line_levels(seq_count):
    return (seq_count // 2).bit_length() - 1


def line_reduce(block, place_z, seq_count):
    for level in range(line_levels(seq_count)):
        half = block.shape[0] // 2
        bit = (place_z >> level) & 1
        sent = lax.dynamic_slice_in_dim(block, (1 - bit) * half, half, 0)
        kept = lax.dynamic_slice_in_dim(block, bit * half, half, 0)
        got = line_swap(sent, level, seq_count)
        block = (kept.astype(F32) + got.astype(F32)).astype(BF16)
    return block


def ordered(bit, mine, other):
    first = jnp.where(bit == 0, mine, other)
    second = jnp.where(bit == 0, other, mine)
    return jnp.concatenate([first, second], axis=0)


def line_gather(block, place_z, seq_count):
    for level in reversed(range(line_levels(seq_count))):
        bit = (place_z >> level) & 1
        block = ordered(bit, block, line_swap(block, level, seq_count))
    return block


def any_spec():
    return pl.BlockSpec(memory_space=pl.ANY)


def vmem_spec():
    return pl.BlockSpec(memory_space=pltpu.VMEM)


def smem_spec():
    return pl.BlockSpec(memory_space=pltpu.SMEM)


def params():
    return pltpu.CompilerParams(vmem_limit_bytes=VMEM_LIMIT)


def cost(flops, moved):
    return pl.CostEstimate(flops=int(flops), bytes_accessed=int(moved), transcendentals=0)


def nt_dot(a, b):
    return lax.dot_general(a, b, (((1,), (1,)), ((), ())), preferred_element_type=F32)


def nn_dot(a, b):
    return jnp.dot(a, b, preferred_element_type=F32)


def row_copies(place_ref, own, mine, others, full, sems, rows):
    count = len(mine) + 1
    half = rows // 2
    core = place_ref[2 * count - 1]
    copies = [
        pltpu.make_async_copy(
            own, full.at[pl.ds(pl.multiple_of(place_ref[0] * rows, 16), rows), :], sems.at[0]
        )
    ]
    for which, (refs, side) in enumerate(((mine, core), (others, 1 - core))):
        for i, ref in enumerate(refs):
            at = 1 + which * (count - 1) + i
            base = pl.multiple_of(place_ref[at] * rows + side * half, 16)
            copies.append(
                pltpu.make_async_copy(ref, full.at[pl.ds(base, half), :], sems.at[at])
            )
    return copies


def column_copies(place_ref, own, mine, others, full, sems, rows):
    count = len(mine) + 1
    half = full.shape[1] // 2
    core = place_ref[2 * count - 1]
    copies = [
        pltpu.make_async_copy(
            own, full.at[pl.ds(pl.multiple_of(place_ref[0] * rows, 16), rows), :], sems.at[0]
        )
    ]
    for which, (refs, side) in enumerate(((mine, core), (others, 1 - core))):
        for i, ref in enumerate(refs):
            at = 1 + which * (count - 1) + i
            base = pl.multiple_of(place_ref[at] * rows, 16)
            left = pl.multiple_of(side * half, 128)
            copies.append(
                pltpu.make_async_copy(
                    ref, full.at[pl.ds(base, rows), pl.ds(left, half)], sems.at[at]
                )
            )
    return copies


def down_copies(place_ref, refs, full, sems, count, hidden):
    if len(refs) == 1:
        return [pltpu.make_async_copy(refs[0], full.at[pl.ds(0, hidden), :], sems.at[0])]
    return column_copies(
        place_ref, refs[0], refs[1 : 1 + count], refs[1 + count :], full, sems, hidden // (count + 1)
    )


def seg_rows(value, start, stop):
    return value[start:stop]


def attention_forward(
    seq_count, heads, group, low_ref, high_ref, x_ref, gain_ref, w_ref, order_ref, start_ref, end_ref,
    cos_ref, sin_ref, normed_ref, packed_ref, att_ref, out_ref, lse_ref, qkv_t, k_rows, o_rows,
):
    width = heads * HD
    rows = group // seq_count
    blocks = group // BLOCK

    def project(i, carry):
        x = x_ref[i].astype(F32)
        center = x - jnp.mean(x, axis=-1, keepdims=True)
        spread = jnp.mean(center * center, axis=-1, keepdims=True)
        normed = (center * lax.rsqrt(spread + NORM_EPS) * gain_ref[...]).astype(BF16)
        normed_ref[i] = normed
        qkv = nn_dot(normed, w_ref[...]).astype(BF16)
        qkv_t[i] = qkv.T
        return carry

    lax.fori_loop(0, seq_count, project, 0)

    def pack(i, carry):
        at = pl.ds(pl.multiple_of(i * BLOCK, BLOCK), BLOCK)
        order = order_ref[:, at]
        total = jnp.zeros((3 * width, BLOCK), F32)
        for s in range(seq_count):
            here = lax.broadcasted_iota(jnp.int32, (rows, BLOCK), 0) + s * rows
            hot = jnp.where(here == order, 1.0, 0.0).astype(BF16)
            total = total + nn_dot(qkv_t[s], hot)
        cos = cos_ref[:, at]
        sin = sin_ref[:, at]
        half = HD // 2
        for part in range(2):
            for h in range(heads):
                base = part * width + h * HD
                first = total[base : base + half]
                second = total[base + half : base + HD]
                turned = jnp.concatenate(
                    [first * cos - second * sin, second * cos + first * sin], axis=0
                ).astype(BF16)
                packed_ref[base : base + HD, at] = turned
                if part == 1:
                    k_rows[h, at, :] = turned.T
        packed_ref[2 * width :, at] = total[2 * width :].astype(BF16)
        return carry

    lax.fori_loop(0, blocks, pack, 0)
    scale = HD**-0.5 * LOG2E

    def attend(i, carry):
        at = pl.ds(pl.multiple_of(i * BLOCK, BLOCK), BLOCK)
        start = start_ref[:, at]
        end = end_ref[:, at]
        queries = [packed_ref[h * HD : (h + 1) * HD, at] for h in range(heads)]

        def step(j, state):
            there = pl.ds(pl.multiple_of(j * BLOCK, BLOCK), BLOCK)
            where = lax.broadcasted_iota(jnp.int32, (BLOCK, BLOCK), 0) + j * BLOCK
            same = jnp.logical_and(where >= start, where < end)
            following = []
            for h in range(heads):
                top, total, acc = state[h]
                scores = nn_dot(k_rows[h, there, :], queries[h]) * scale
                scores = jnp.where(same, scores, -1e30)
                new_top = jnp.maximum(top, jnp.max(scores, axis=0, keepdims=True))
                shrink = jnp.exp2(top - new_top)
                probs = jnp.exp2(scores - new_top)
                total = total * shrink + jnp.sum(probs, axis=0, keepdims=True)
                base = 2 * width + h * HD
                acc = acc * shrink + nn_dot(packed_ref[base : base + HD, there], probs.astype(BF16))
                following.append((new_top, total, acc))
            return tuple(following)

        first = tuple(
            (
                jnp.full((1, BLOCK), -1e30, F32),
                jnp.zeros((1, BLOCK), F32),
                jnp.zeros((HD, BLOCK), F32),
            )
            for _ in range(heads)
        )
        last = lax.fori_loop(low_ref[i], high_ref[i], step, first)
        outs = []
        for h in range(heads):
            top, total, acc = last[h]
            out = acc / total
            out_ref[h * HD : (h + 1) * HD, at] = out
            lse_ref[h : h + 1, at] = top + jnp.log2(total)
            outs.append(out)
        o_rows[at, :] = jnp.concatenate(outs, axis=0).astype(BF16).T
        return carry

    lax.fori_loop(0, blocks, attend, 0)

    def arrive(i, carry):
        here = lax.broadcasted_iota(jnp.int32, (rows, group), 0) + i * rows
        hot = jnp.where(here == order_ref[...], 1.0, 0.0).astype(BF16)
        att_ref[i] = nn_dot(hot, o_rows[...]).astype(BF16)
        return carry

    lax.fori_loop(0, seq_count, arrive, 0)


def run_attention_forward(x_all, gain, w_heads, layout, heads):
    seq_count, rows, dim = x_all.shape
    group = seq_count * rows
    width = heads * HD
    low, high, order, start, end, cos, sin = layout
    return pl.pallas_call(
        functools.partial(attention_forward, seq_count, heads, group),
        name="attention_forward",
        out_shape=(
            jax.ShapeDtypeStruct((seq_count, rows, dim), BF16),
            jax.ShapeDtypeStruct((3 * width, group), BF16),
            jax.ShapeDtypeStruct((seq_count, rows, width), BF16),
            jax.ShapeDtypeStruct((width, group), F32),
            jax.ShapeDtypeStruct((heads, group), F32),
        ),
        in_specs=[smem_spec()] * 2 + [vmem_spec()] * 8,
        out_specs=[vmem_spec()] * 5,
        scratch_shapes=[
            pltpu.VMEM((seq_count, 3 * width, rows), BF16),
            pltpu.VMEM((heads, group, HD), BF16),
            pltpu.VMEM((group, width), BF16),
        ],
        compiler_params=params(),
        cost_estimate=cost(24e9, 20e6),
    )(low, high, x_all, gain, w_heads, order, start, end, cos, sin)


def attention_backward(
    seq_count, heads, group, low_ref, high_ref, dout_ref, packed_ref, out_ref, lse_ref, order_ref,
    start_ref, end_ref, cos_ref, sin_ref, grad_ref, dout_t, dpack_t, drows, qrows, krows, vrows,
    delta_ref, dq_t, grows,
):
    width = heads * HD
    rows = group // seq_count
    blocks = group // BLOCK
    scale = HD**-0.5

    def turn(i, carry):
        dout_t[i] = dout_ref[i].T
        return carry

    lax.fori_loop(0, seq_count, turn, 0)

    def pack(i, carry):
        at = pl.ds(pl.multiple_of(i * BLOCK, BLOCK), BLOCK)
        order = order_ref[:, at]
        total = jnp.zeros((width, BLOCK), F32)
        for s in range(seq_count):
            here = lax.broadcasted_iota(jnp.int32, (rows, BLOCK), 0) + s * rows
            hot = jnp.where(here == order, 1.0, 0.0).astype(BF16)
            total = total + nn_dot(dout_t[s], hot)
        dpack_t[:, at] = total.astype(BF16)
        for h in range(heads):
            mine = total[h * HD : (h + 1) * HD]
            delta_ref[h : h + 1, at] = jnp.sum(
                mine * out_ref[h * HD : (h + 1) * HD, at], axis=0, keepdims=True
            )
            drows[h, at, :] = mine.T.astype(BF16)
            for part, ref in enumerate((qrows, krows, vrows)):
                base = part * width + h * HD
                ref[h, at, :] = packed_ref[base : base + HD, at].T
        dq_t[:, at] = jnp.zeros((width, BLOCK), F32)
        return carry

    lax.fori_loop(0, blocks, pack, 0)

    def keys(j, carry):
        there = pl.ds(pl.multiple_of(j * BLOCK, BLOCK), BLOCK)
        where = lax.broadcasted_iota(jnp.int32, (BLOCK, BLOCK), 0) + j * BLOCK

        def queries(i, state):
            at = pl.ds(pl.multiple_of(i * BLOCK, BLOCK), BLOCK)
            same = jnp.logical_and(where >= start_ref[:, at], where < end_ref[:, at])
            following = []
            for h in range(heads):
                dk, dv = state[h]
                base = h * HD
                key_rows = krows[h, there, :]
                query_t = packed_ref[base : base + HD, at]
                scores = nn_dot(key_rows, query_t) * (scale * LOG2E)
                scores = jnp.where(same, scores, -1e30)
                probs = jnp.exp2(scores - lse_ref[h : h + 1, at])
                dprobs = nn_dot(vrows[h, there, :], dpack_t[base : base + HD, at])
                raw = (probs * (dprobs - delta_ref[h : h + 1, at]) * scale).astype(BF16)
                dv = dv + nn_dot(probs.astype(BF16), drows[h, at, :])
                dk = dk + nn_dot(raw, qrows[h, at, :])
                key_t = packed_ref[width + base : width + base + HD, there]
                dq_t[base : base + HD, at] += nn_dot(key_t, raw)
                following.append((dk, dv))
            return tuple(following)

        zero = jnp.zeros((BLOCK, HD), F32)
        last = lax.fori_loop(low_ref[j], high_ref[j], queries, tuple((zero, zero) for _ in range(heads)))
        cos = cos_ref[:, there]
        sin = sin_ref[:, there]
        half = HD // 2
        turned = []
        for h in range(heads):
            dk_t = last[h][0].T
            first, second = dk_t[:half], dk_t[half:]
            turned.append(first * cos + second * sin)
            turned.append(second * cos - first * sin)
        grows[there, width : 2 * width] = jnp.concatenate(turned, axis=0).T.astype(BF16)
        grows[there, 2 * width :] = jnp.concatenate([last[h][1] for h in range(heads)], axis=1).astype(BF16)
        return carry

    lax.fori_loop(0, blocks, keys, 0)

    def finish(i, carry):
        at = pl.ds(pl.multiple_of(i * BLOCK, BLOCK), BLOCK)
        cos = cos_ref[:, at]
        sin = sin_ref[:, at]
        half = HD // 2
        turned = []
        for h in range(heads):
            first = dq_t[h * HD : h * HD + half, at]
            second = dq_t[h * HD + half : (h + 1) * HD, at]
            turned.append(first * cos + second * sin)
            turned.append(second * cos - first * sin)
        grows[at, :width] = jnp.concatenate(turned, axis=0).T.astype(BF16)
        return carry

    lax.fori_loop(0, blocks, finish, 0)

    def arrive(i, carry):
        here = lax.broadcasted_iota(jnp.int32, (rows, group), 0) + i * rows
        hot = jnp.where(here == order_ref[...], 1.0, 0.0).astype(BF16)
        grad_ref[i] = nn_dot(hot, grows[...]).astype(BF16)
        return carry

    lax.fori_loop(0, seq_count, arrive, 0)


def run_attention_backward(dout, packed, out_t, lse, layout, heads):
    seq_count, rows, width = dout.shape
    group = seq_count * rows
    low, high, order, start, end, cos, sin = layout
    return pl.pallas_call(
        functools.partial(attention_backward, seq_count, heads, group),
        name="attention_backward",
        out_shape=jax.ShapeDtypeStruct((seq_count, rows, 3 * width), BF16),
        in_specs=[smem_spec()] * 2 + [vmem_spec()] * 9,
        out_specs=vmem_spec(),
        scratch_shapes=[
            pltpu.VMEM((seq_count, width, rows), BF16),
            pltpu.VMEM((width, group), BF16),
            pltpu.VMEM((heads, group, HD), BF16),
            pltpu.VMEM((heads, group, HD), BF16),
            pltpu.VMEM((heads, group, HD), BF16),
            pltpu.VMEM((heads, group, HD), BF16),
            pltpu.VMEM((heads, group), F32),
            pltpu.VMEM((width, group), F32),
            pltpu.VMEM((group, 3 * width), BF16),
        ],
        compiler_params=params(),
        cost_estimate=cost(30e9, 10e6),
    )(low, high, dout, packed, out_t, lse, order, start, end, cos, sin)


def qkv_weight_grad(seq_count, normed_ref, grad_ref, gw_ref, total):
    total[...] = jnp.zeros_like(total)

    def step(i, carry):
        total[...] += nn_dot(grad_ref[i].T, normed_ref[i])
        return carry

    lax.fori_loop(0, seq_count, step, 0)
    gw_ref[...] = total[...].T.astype(BF16)


def run_qkv_weight_grad(normed, grad):
    seq_count, rows, dim = normed.shape
    width = grad.shape[-1]
    return pl.pallas_call(
        functools.partial(qkv_weight_grad, seq_count),
        name="qkv_weight_grad",
        out_shape=jax.ShapeDtypeStruct((dim, width), BF16),
        in_specs=[vmem_spec()] * 2,
        out_specs=vmem_spec(),
        scratch_shapes=[pltpu.VMEM((width, dim), F32)],
        compiler_params=params(),
        cost_estimate=cost(3e9, 6e6),
    )(normed, grad)


def padded(hidden):
    return -(-hidden // 128) * 128


def hidden_grad(count, hidden, place_ref, cot_ref, *refs):
    downs, (out_ref, full, sems) = refs[:-3], refs[-3:]
    copies = down_copies(place_ref, downs, full, sems, count, hidden)
    for copy in copies:
        copy.start()
    tail = padded(hidden) - hidden
    if tail:
        full[pl.ds(hidden, tail), :] = jnp.zeros((tail, full.shape[1]), BF16)
    for copy in copies:
        copy.wait()
    cot = cot_ref[...]
    tiles = padded(hidden) // 128

    def step(i, carry):
        at = pl.multiple_of(i * 128, 128)
        out_ref[:, pl.ds(at, 128)] = nt_dot(cot, full[pl.ds(at, 128), :])
        return carry

    lax.fori_loop(0, tiles, step, 0)


def run_hidden_grad(place, cot, downs, count, hidden):
    rows, dim = cot.shape
    return pl.pallas_call(
        functools.partial(hidden_grad, count, hidden),
        name="hidden_grad",
        out_shape=jax.ShapeDtypeStruct((rows, padded(hidden)), F32),
        in_specs=[smem_spec(), vmem_spec()] + [any_spec()] * len(downs),
        out_specs=vmem_spec(),
        scratch_shapes=[
            pltpu.VMEM((padded(hidden), dim), BF16),
            pltpu.SemaphoreType.DMA((2 * count + 1,)),
        ],
        compiler_params=params(),
        cost_estimate=cost(4e9, 9e6),
    )(place, cot, *downs)


def layer_result(count, hidden, place_ref, mid_ref, hid_ref, *refs):
    downs, (out_ref, full, sems) = refs[:-3], refs[-3:]
    copies = down_copies(place_ref, downs, full, sems, count, hidden)
    for copy in copies:
        copy.start()
    tail = padded(hidden) - hidden
    if tail:
        full[pl.ds(hidden, tail), :] = jnp.zeros((tail, full.shape[1]), BF16)
    for copy in copies:
        copy.wait()

    def step(i, carry):
        at = pl.ds(pl.multiple_of(i * 256, 256), 256)
        out_ref[:, at] = (mid_ref[:, at] + nn_dot(hid_ref[...], full[:, at])).astype(BF16)
        return carry

    lax.fori_loop(0, out_ref.shape[1] // 256, step, 0)


def run_layer_result(place, middle, hidden_rows, downs, count, hidden):
    rows, dim = middle.shape
    return pl.pallas_call(
        functools.partial(layer_result, count, hidden),
        name="layer_result",
        out_shape=jax.ShapeDtypeStruct((rows, dim), BF16),
        in_specs=[smem_spec()] + [vmem_spec()] * 2 + [any_spec()] * len(downs),
        out_specs=vmem_spec(),
        scratch_shapes=[
            pltpu.VMEM((padded(hidden), dim), BF16),
            pltpu.SemaphoreType.DMA((2 * count + 1,)),
        ],
        compiler_params=params(),
        cost_estimate=cost(4e9, 9e6),
    )(place, middle, hidden_rows, *downs)


def feed_forward(
    count, hidden, heads_width, place_ref, x_ref, att_ref, cot_ref, gain_ref, gh_ref, *refs
):
    outs_w, refs = refs[: 2 * count + 1], refs[2 * count + 1 :]
    ins_w, refs = refs[: 2 * count + 1], refs[2 * count + 1 :]
    (mid_ref, gmid_ref, nt_ref, gboth_ref, hid_ref, gbr_ref, ga_ref, att_all_ref) = refs[:8]
    wo, wi, both, early, late, sem_o, sem_i = refs[8:]
    dim = x_ref.shape[1]
    rows = dim // (count + 1)
    copies_o = row_copies(place_ref, outs_w[0], outs_w[1 : 1 + count], outs_w[1 + count :], wo, sem_o, rows)
    copies_i = row_copies(place_ref, ins_w[0], ins_w[1 : 1 + count], ins_w[1 + count :], wi, sem_i, rows)
    for copy in copies_o:
        copy.start()
    for copy in copies_i:
        copy.start()
    att = jnp.concatenate([att_ref[s] for s in range(att_ref.shape[0])], axis=1)
    att_all_ref[...] = att
    for copy in copies_o:
        copy.wait()

    def branch(i, carry):
        at = pl.ds(pl.multiple_of(i * 256, 256), 256)
        mid_ref[:, at] = x_ref[:, at].astype(F32) + nn_dot(att_all_ref[...], wo[:, at])
        return carry

    lax.fori_loop(0, dim // 256, branch, 0)
    middle = mid_ref[...]
    center = middle - jnp.mean(middle, axis=-1, keepdims=True)
    spread = jnp.mean(center * center, axis=-1, keepdims=True)
    scale = lax.rsqrt(spread + NORM_EPS)
    nt_ref[...] = (center * scale * gain_ref[...]).astype(BF16)
    for copy in copies_i:
        copy.wait()
    wide = 2 * hidden // 128

    def expand(i, carry):
        at = pl.ds(pl.multiple_of(i * 256, 256), 256)
        both[:, at] = nn_dot(nt_ref[...], wi[:, at])
        return carry

    lax.fori_loop(0, wide // 2, expand, 0)
    if wide % 2:
        both[:, pl.ds(128 * (wide - 1), 128)] = nn_dot(nt_ref[...], wi[:, pl.ds(128 * (wide - 1), 128)])
    both[:, pl.ds(128 * wide, 128)] = jnp.zeros((both.shape[0], 128), F32)
    tiles = padded(hidden) // 128
    whole = hidden // 128
    lanes = lax.broadcasted_iota(jnp.int32, (both.shape[0], 128), 1)
    shift = hidden % 128

    def tile(i):
        return pl.ds(pl.multiple_of(i * 128, 128), 128)

    def gates(i):
        a = both[:, tile(i)]
        if shift:
            left = pltpu.roll(both[:, tile(whole + i)], 128 - shift, 1)
            right = pltpu.roll(both[:, tile(whole + i + 1)], 128 - shift, 1)
            b = jnp.where(lanes < 128 - shift, left, right)
        else:
            b = both[:, tile(whole + i)]
        gh = gh_ref[:, tile(i)]
        phi = 0.5 * (1.0 + lax.erf(a * (0.5**0.5)))
        gelu = a * phi
        slope = phi + a * ((0.5 / math.pi) ** 0.5 * jnp.exp(-0.5 * a * a))
        hid_ref[:, tile(i)] = (gelu * b).astype(BF16)
        return gh * b * slope, gh * gelu

    if shift:
        first_a, first_b = gates(0)
        gboth_ref[:, tile(0)] = first_a.astype(BF16)
        early[...] = pltpu.roll(first_b, shift, 1)
        late[...] = early[...]

        def inner(i, carry):
            ga, gb = gates(i)
            turned = pltpu.roll(gb, shift, 1)
            gboth_ref[:, tile(i)] = ga.astype(BF16)
            gboth_ref[:, tile(whole + i)] = jnp.where(lanes < shift, late[...], turned).astype(BF16)
            late[...] = turned
            return carry

        lax.fori_loop(1, tiles - 1, inner, 0)
        ga, gb = gates(tiles - 1)
        turned = pltpu.roll(gb, shift, 1)
        gboth_ref[:, tile(whole)] = jnp.where(lanes < shift, ga, early[...]).astype(BF16)
        gboth_ref[:, tile(2 * whole)] = jnp.where(lanes < shift, late[...], turned).astype(BF16)
    else:

        def inner(i, carry):
            ga, gb = gates(i)
            gboth_ref[:, tile(i)] = ga.astype(BF16)
            gboth_ref[:, tile(whole + i)] = gb.astype(BF16)
            return carry

        lax.fori_loop(0, tiles, inner, 0)

    def back(i, carry):
        at = pl.multiple_of(i * 128, 128)
        both[:, pl.ds(at, 128)] = nt_dot(gboth_ref[...], wi[pl.ds(at, 128), :])
        return carry

    lax.fori_loop(0, dim // 128, back, 0)
    middle = mid_ref[...]
    center = middle - jnp.mean(middle, axis=-1, keepdims=True)
    spread = jnp.mean(center * center, axis=-1, keepdims=True)
    scale = lax.rsqrt(spread + NORM_EPS)
    normal = center * scale
    e = both[:, pl.ds(0, dim)] * gain_ref[...]
    pull = e - jnp.mean(e, axis=-1, keepdims=True) - normal * jnp.mean(e * normal, axis=-1, keepdims=True)
    gmid = cot_ref[...].astype(F32) + scale * pull
    gmid_ref[...] = gmid
    gbr_ref[...] = gmid.astype(BF16)

    def spread_out(i, carry):
        at = pl.multiple_of(i * 128, 128)
        both[:, pl.ds(at, 128)] = nt_dot(gbr_ref[...], wo[pl.ds(at, 128), :])
        return carry

    lax.fori_loop(0, dim // 128, spread_out, 0)
    for s in range(att_ref.shape[0]):
        ga_ref[s] = both[:, s * heads_width : (s + 1) * heads_width].astype(BF16)


def run_feed_forward(place, x, att, cot, gain, grad_hidden, w_out, w_in, count, hidden):
    rows, dim = x.shape
    seq_count, _, heads_width = att.shape
    return pl.pallas_call(
        functools.partial(feed_forward, count, hidden, heads_width),
        name="feed_forward",
        out_shape=(
            jax.ShapeDtypeStruct((rows, dim), F32),
            jax.ShapeDtypeStruct((rows, dim), F32),
            jax.ShapeDtypeStruct((rows, dim), BF16),
            jax.ShapeDtypeStruct((rows, 2 * hidden), BF16),
            jax.ShapeDtypeStruct((rows, padded(hidden)), BF16),
            jax.ShapeDtypeStruct((rows, dim), BF16),
            jax.ShapeDtypeStruct((seq_count, rows, heads_width), BF16),
            jax.ShapeDtypeStruct((rows, dim), BF16),
        ),
        in_specs=[smem_spec()] + [vmem_spec()] * 5 + [any_spec()] * (len(w_out) + len(w_in)),
        out_specs=[vmem_spec()] * 8,
        scratch_shapes=[
            pltpu.VMEM((dim, dim), BF16),
            pltpu.VMEM((dim, 2 * hidden), BF16),
            pltpu.VMEM((rows, 2 * hidden + 128), F32),
            pltpu.VMEM((rows, 128), F32),
            pltpu.VMEM((rows, 128), F32),
            pltpu.SemaphoreType.DMA((2 * count + 1,)),
            pltpu.SemaphoreType.DMA((2 * count + 1,)),
        ],
        compiler_params=params(),
        cost_estimate=cost(16e9, 24e6),
    )(place, x, att, cot, gain, grad_hidden, *w_out, *w_in)


def row_grad(count, rows, place_ref, left_ref, left_other_ref, right_ref, right_other_ref, out_ref, turned, picked):
    half = rows // 2
    tokens = left_ref.shape[0]

    @pl.when(pl.program_id(0) == 0)
    def _():
        turned[:, :tokens] = left_ref[...].T
        turned[:, tokens:] = left_other_ref[...].T
        core = place_ref[2 * count + 1]
        for key in range(count + 1):
            base = pl.multiple_of(place_ref[key] * rows + core * half, 16)
            picked[key * half : (key + 1) * half, :] = turned[pl.ds(base, half), :]

    right = jnp.concatenate([right_ref[...], right_other_ref[...]], axis=0)
    result = nn_dot(picked[...], right).astype(BF16)
    for key in range(count + 1):
        out_ref[key] = result[key * half : (key + 1) * half]


def run_row_grad(name, place, left, left_other, right, right_other, count):
    tokens, features = left.shape
    columns = right.shape[1]
    rows = features // (count + 1)
    wide = 1024 if columns % 1024 == 0 else 896
    steps = pl.cdiv(columns, wide)
    return pl.pallas_call(
        functools.partial(row_grad, count, rows),
        name=name,
        out_shape=jax.ShapeDtypeStruct((count + 1, rows // 2, columns), BF16),
        grid=(steps,),
        in_specs=[
            smem_spec(),
            pl.BlockSpec((tokens, features), lambda i: (0, 0)),
            pl.BlockSpec((tokens, features), lambda i: (0, 0)),
            pl.BlockSpec((tokens, wide), lambda i: (0, i)),
            pl.BlockSpec((tokens, wide), lambda i: (0, i)),
        ],
        out_specs=pl.BlockSpec((count + 1, rows // 2, wide), lambda i: (0, 0, i)),
        scratch_shapes=[
            pltpu.VMEM((features, 2 * tokens), BF16),
            pltpu.VMEM((features // 2, 2 * tokens), BF16),
        ],
        compiler_params=params(),
        cost_estimate=cost(2.0 * 2 * tokens * features * columns, 4 * tokens * columns + features * columns),
    )(place, left, left_other, right, right_other)


def down_grad(count, hidden, place_ref, hid_ref, hid_other_ref, cot_ref, cot_other_ref, out_ref, turned, picked):
    tokens = hid_ref.shape[0]
    half = cot_ref.shape[1] // 2
    rows = hidden // (count + 1)

    @pl.when(pl.program_id(0) == 0)
    def _():
        turned[:, :tokens] = hid_ref[...].T
        turned[:, tokens:] = hid_other_ref[...].T
        left = pl.ds(pl.multiple_of(place_ref[2 * count + 1] * half, 128), half)
        picked[:tokens] = cot_ref[:, left]
        picked[tokens:] = cot_other_ref[:, left]

    if rows % 16 == 0:
        base = pl.multiple_of(place_ref[pl.program_id(0)] * rows, 16)
        out_ref[0] = nn_dot(turned[pl.ds(base, rows), :], picked[...]).astype(BF16)
    else:
        out_ref[0] = nn_dot(turned[:hidden, :], picked[...]).astype(BF16)


def run_down_grad(place, hid, hid_other, cot, cot_other, count, hidden):
    tokens, dim = cot.shape
    rows = hidden // (count + 1)
    steps, rows = (count + 1, rows) if rows % 16 == 0 else (1, hidden)
    whole = lambda i: (0, 0)
    return pl.pallas_call(
        functools.partial(down_grad, count, hidden),
        name="down_grad",
        out_shape=jax.ShapeDtypeStruct((steps, rows, dim // 2), BF16),
        grid=(steps,),
        in_specs=[
            smem_spec(),
            pl.BlockSpec(hid.shape, whole),
            pl.BlockSpec(hid.shape, whole),
            pl.BlockSpec(cot.shape, whole),
            pl.BlockSpec(cot.shape, whole),
        ],
        out_specs=pl.BlockSpec((1, rows, dim // 2), lambda i: (i, 0, 0)),
        scratch_shapes=[
            pltpu.VMEM((hid.shape[1], 2 * tokens), BF16),
            pltpu.VMEM((2 * tokens, dim // 2), BF16),
        ],
        compiler_params=params(),
        cost_estimate=cost(3e9, 6e6),
    )(place, hid, hid_other, cot, cot_other)


def input_grad(count, place_ref, x_ref, gmid_ref, gain_ref, g_ref, *refs):
    weights, (out_ref, full, grad, total, sems) = refs[:-5], refs[-5:]
    seq_count, _, width = g_ref.shape
    width //= 3
    dim = x_ref.shape[1]
    rows = dim // (count + 1)
    copies = row_copies(place_ref, weights[0], weights[1 : 1 + count], weights[1 + count :], full, sems, rows)
    for copy in copies:
        copy.start()
    grad[...] = jnp.concatenate(
        [g_ref[s][:, part * width : (part + 1) * width] for part in range(3) for s in range(seq_count)],
        axis=1,
    )
    for copy in copies:
        copy.wait()

    def step(i, carry):
        at = pl.multiple_of(i * 128, 128)
        total[:, pl.ds(at, 128)] = nt_dot(grad[...], full[pl.ds(at, 128), :])
        return carry

    lax.fori_loop(0, dim // 128, step, 0)
    x = x_ref[...].astype(F32)
    center = x - jnp.mean(x, axis=-1, keepdims=True)
    spread = jnp.mean(center * center, axis=-1, keepdims=True)
    scale = lax.rsqrt(spread + NORM_EPS)
    normal = center * scale
    e = total[...] * gain_ref[...]
    pull = e - jnp.mean(e, axis=-1, keepdims=True) - normal * jnp.mean(e * normal, axis=-1, keepdims=True)
    out_ref[...] = (gmid_ref[...] + scale * pull).astype(BF16)


def run_input_grad(place, x, gmid, gain, grads, weights, count):
    rows, dim = x.shape
    columns = weights[0].shape[1]
    return pl.pallas_call(
        functools.partial(input_grad, count),
        name="input_grad",
        out_shape=jax.ShapeDtypeStruct((rows, dim), BF16),
        in_specs=[smem_spec()] + [vmem_spec()] * 4 + [any_spec()] * len(weights),
        out_specs=vmem_spec(),
        scratch_shapes=[
            pltpu.VMEM((dim, columns), BF16),
            pltpu.VMEM((rows, columns), BF16),
            pltpu.VMEM((rows, dim), F32),
            pltpu.SemaphoreType.DMA((2 * count + 1,)),
        ],
        compiler_params=params(),
        cost_estimate=cost(4e9, 10e6),
    )(place, x, gmid, gain, grads, *weights)


def sequence_layout(lengths, order, group):
    ends = jnp.cumsum(lengths)
    starts = ends - lengths
    index = jnp.arange(group, dtype=jnp.int32)
    passed = index[:, None] >= ends[None, :]
    start = jnp.sum(jnp.where(passed, lengths[None, :], 0), axis=1).astype(jnp.int32)
    inside = jnp.logical_and(index[:, None] >= starts[None, :], jnp.logical_not(passed))
    end = jnp.sum(jnp.where(inside, ends[None, :], 0), axis=1).astype(jnp.int32)
    places = index - start
    half = HD // 2
    speeds = jnp.power(F32(ROPE_BASE), -2.0 * jnp.arange(half, dtype=F32) / HD)
    angles = speeds[:, None] * places.astype(F32)[None, :]
    low = start[::BLOCK] // BLOCK
    high = (end[BLOCK - 1 :: BLOCK] + BLOCK - 1) // BLOCK
    return (low, high, order[None, :], start[None, :], end[None, :], jnp.cos(angles), jnp.sin(angles))


def local(tokens, seq_lengths, seq_order, norm_one, w_qkv, w_out, norm_two, w_in, w_down, cotangent):
    seq_count = lax.axis_size("seq")
    fsdp_count = lax.axis_size("fsdp")
    levels = fsdp_count.bit_length() - 1
    count = fsdp_count - 1
    seq_at = lax.axis_index("seq")
    fsdp_at = lax.axis_index("fsdp")
    core = seq_at % 2
    place_z = seq_at // 2
    x = tokens[0]
    cot = cotangent[0]
    rows, dim = x.shape
    group = rows * seq_count
    heads = dim // HD // seq_count
    width = heads * HD
    hidden = w_in.shape[1] // 2
    gather = functools.partial(plane_gather, seq_count=seq_count, fsdp_count=fsdp_count)
    swap = functools.partial(core_swap, seq_count=seq_count)

    keys = [jnp.array([plane_mask(c, key, levels) for key in range(1, fsdp_count)], jnp.int32) for c in (0, 1)]
    mine = fsdp_at ^ jnp.where(core == 0, keys[0], keys[1])
    other = fsdp_at ^ jnp.where(core == 0, keys[1], keys[0])
    place = jnp.concatenate([fsdp_at[None], mine, other, core[None]]).astype(jnp.int32)

    def half_rows(weight):
        half = weight.shape[0] // 2
        return lax.dynamic_slice_in_dim(weight, core * half, half, 0)

    def half_columns(weight):
        half = weight.shape[1] // 2
        return lax.dynamic_slice_in_dim(weight, core * half, half, 1)

    def spread_weight(weight, piece):
        pieces = gather(piece)[1:]
        return [weight] + pieces + [swap(p) for p in pieces]

    x_all = lax.all_gather(x, "seq", axis=0, tiled=False)
    own_heads = lax.dynamic_slice_in_dim(w_qkv.reshape(w_qkv.shape[0], 3, dim), seq_at * width, width, 2)
    w_heads = lax.all_gather(own_heads.reshape(w_qkv.shape[0], 3 * width), "fsdp", axis=0, tiled=True)
    gains = lax.all_gather(jnp.stack([norm_one, norm_two]), "fsdp", axis=1, tiled=True).astype(F32)
    gain_one, gain_two = gains[0:1], gains[1:2]
    outs = spread_weight(w_out, half_rows(w_out))
    if w_down.shape[0] % 16 == 0:
        downs = spread_weight(w_down, half_columns(w_down))
    else:
        downs = [lax.all_gather(w_down, "fsdp", axis=0, tiled=True)]
    ins = spread_weight(w_in, half_rows(w_in))
    qkvs = spread_weight(w_qkv, half_rows(w_qkv))
    cot_other = swap(cot)

    layout = sequence_layout(seq_lengths[0], seq_order[0], group)
    normed, packed, att, out_t, lse = run_attention_forward(x_all, gain_one, w_heads, layout, heads)
    att = lax.all_to_all(att, "seq", split_axis=0, concat_axis=0, tiled=True)
    grad_hidden = run_hidden_grad(place, cot, downs, count, hidden)
    middle, gmid, normed_two, gboth, hid, gbranch, gatt, att_all = run_feed_forward(
        place, x, att, cot, gain_two, grad_hidden, outs, ins, count, hidden
    )
    dout = lax.all_to_all(gatt, "seq", split_axis=0, concat_axis=0, tiled=True)
    layer_out = run_layer_result(place, middle, hid, downs, count, hidden)

    def finish(block):
        block = line_gather(line_reduce(block, place_z, seq_count), place_z, seq_count)
        return block

    reduce = functools.partial(plane_reduce, seq_count=seq_count, fsdp_count=fsdp_count)
    gw_in = run_row_grad("in_grad", place, normed_two, swap(normed_two), gboth, swap(gboth), count)
    gw_in = finish(reduce([gw_in[k] for k in range(fsdp_count)]))
    gw_in = ordered(core, gw_in, swap(gw_in)).astype(F32)
    gw_down = run_down_grad(place, hid, swap(hid), cot, cot_other, count, hidden)
    if w_down.shape[0] % 16 == 0:
        gw_down = [gw_down[k] for k in range(fsdp_count)]
    else:
        each = w_down.shape[0]
        gw_down = [lax.dynamic_slice_in_dim(gw_down[0], place[k] * each, each, 0) for k in range(fsdp_count)]
    gw_down = reduce(gw_down).T
    gw_down = finish(gw_down)
    gw_down = ordered(core, gw_down, swap(gw_down)).T.astype(F32)
    gw_out = run_row_grad("out_grad", place, att_all, swap(att_all), gbranch, swap(gbranch), count)
    gw_out = finish(reduce([gw_out[k] for k in range(fsdp_count)]))
    gw_out = ordered(core, gw_out, swap(gw_out)).astype(F32)

    grads = run_attention_backward(dout, packed, out_t, lse, layout, heads)
    grad_rows = lax.all_to_all(grads, "seq", split_axis=0, concat_axis=0, tiled=True)
    gw_heads = run_qkv_weight_grad(normed, grads)
    each = w_qkv.shape[0]
    gw_heads = reduce([lax.dynamic_slice_in_dim(gw_heads, place[k] * each, each, 0) for k in range(fsdp_count)])
    block = gw_heads[None]
    block = ordered(core, block, swap(block))[None]
    block = line_gather(block, place_z, seq_count)
    index = []
    for z in range(seq_count // 2):
        at = 0
        for level in range(line_levels(seq_count)):
            at = at * 2 + (z >> level & 1)
        index.append(at)
    block = jnp.stack([block[at] for at in index]).reshape(seq_count, each, 3, width)
    gw_qkv = block.transpose(1, 2, 0, 3).reshape(each, 3 * dim).astype(F32)
    grad_tokens = run_input_grad(place, x, gmid, gain_one, grad_rows, qkvs, count)

    grad_one = jnp.sum(gw_qkv * w_qkv.astype(F32), axis=1) / norm_one.astype(F32)
    grad_two = jnp.sum(gw_in * w_in.astype(F32), axis=1) / norm_two.astype(F32)
    return (layer_out[None], grad_tokens[None], grad_one, gw_qkv, gw_out, grad_two, gw_in, gw_down)


def solution(mesh):
    tokens = P("fsdp", "seq", None)
    rows = P("fsdp", None)
    return jax.shard_map(
        local,
        mesh=mesh,
        in_specs=(tokens, rows, rows, P("fsdp"), rows, rows, P("fsdp"), rows, rows, tokens),
        out_specs=(tokens, tokens, P("fsdp"), rows, rows, P("fsdp"), rows, rows),
        check_vma=False,
    )
```

time: 1290 us -> 532 us (0.41)
  waiting for transfers between devices: 637 us -> 150 us
  matrix products: 343 us -> 0 us
  Pallas kernels: 0 us -> 160 us
  local copies, waits for them, and re-layouts: 129 us -> 27.1 us
  starting transfers between devices: 15.3 us -> 75.4 us
  blocking collectives: 98.9 us -> 63.9 us
    dot_general x46 -> x0, matrix products: 314 us -> none  [the longest x4 63.2 us: one_block(): jnp.einsum('hqk,qhd->khd', grad_raw, query_blk, preferred_element_type=jn...]
    reduce_scatter x4 -> x0, waiting for transfers between devices: 294 us -> none  [the longest x1 196 us: local(): lax.psum_scatter(grad_win, 'fsdp', scatter_dimension=0, tiled=True)]
    psum x1 -> x0, waiting for transfers between devices: 223 us -> none  [local(): lax.psum((shares[0], shares[1], shares[2], shares[3], shares[4]), 'seq')]
    pallas_call x0 -> x10, Pallas kernels: none -> 160 us  [the longest x1 39.2 us: run_attention_forward(): pl.pallas_call(functools.partial(attention_forward, seq_count, heads, gro...]
    ppermute x0 -> x60, waiting for transfers between devices: none -> 144 us  [the longest x14 103 us: line_swap(): lax.ppermute(value, 'seq', [(i, i ^ 2 << level) for i in range(seq_count)])]
    all_to_all x2 -> x0, blocking collectives: 70.9 us -> none  [the longest x1 51.3 us: local(): lax.all_to_all(grad_arrival, 'seq', split_axis=0, concat_axis=2, tiled=True)]
    all_gather x4 -> x1, waiting for transfers between devices: 70.5 us -> 0.01 us  [local(): x_all = lax.all_gather(x, 'seq', axis=0, tiled=False)]
    ppermute x0 -> x60, starting transfers between devices: none -> 60 us  [the longest x22 28.7 us: core_swap(): return lax.ppermute(value, 'seq', [(i, i ^ 1) for i in range(seq_count)])]
  transfers between devices with their start and end apart: 13 -> 64, of which waited for: 8 -> 22; matrix products, arithmetic and copies ran while one was open for 36% -> 10% of each run, Pallas kernels for 0% -> 24%
where the time goes in v1:
time: 532 us; the launch traced here: 526 us
  Pallas kernels  160 us (30%)
  waiting for transfers between devices  150 us (28%)
  starting transfers between devices  75.4 us (14%)
  blocking collectives  63.9 us (12%)
  other arithmetic  33.5 us (6%)
  local copies, waits for them, and re-layouts  27.1 us (5%)
  between operations  16.8 us (3%)
    ppermute x14, waiting for transfers between devices, line_swap(): lax.ppermute(value, 'seq', [(i, i ^ 2 << level) for i in range(seq_count)])  103 us
    all_gather x1, blocking collectives, local(): lax.all_gather(own_heads.reshape(w_qkv.shape[0], 3 * width), 'fsdp', axis...  45.4 us
    ppermute x24, waiting for transfers between devices, plane_swap(): return lax.ppermute(value, AXES, pairs)  41 us
    pallas_call x1, Pallas kernels, run_attention_forward(): pl.pallas_call(functools.partial(attention_forward, seq_count, heads, gro...  39.2 us
    pallas_call x1, Pallas kernels, run_attention_backward(): pl.pallas_call(functools.partial(attention_backward, seq_count, heads, gr...  34.4 us
    pallas_call x1, Pallas kernels, run_feed_forward(): pl.pallas_call(functools.partial(feed_forward, count, hidden, heads_width...  31 us
    ppermute x22, starting transfers between devices, core_swap(): return lax.ppermute(value, 'seq', [(i, i ^ 1) for i in range(seq_count)])  28.7 us
    ppermute x24, starting transfers between devices, plane_swap(): return lax.ppermute(value, AXES, pairs)  18.6 us
  transfers between devices with their start and end apart: 64, of which 22 were waited for; matrix products, arithmetic and copies ran while one was open for 10% of the time, Pallas kernels for 24%

profile of v1, /device:TPU:1, one launch (start us, length us, event | category | flops | bytes accessed | tf_op | source)
XLA Modules:
  0.0 526.1 jit_solution(10380401233897511637)
XLA Ops:
  19.2 45.4 %all_gather.11.w_ref = bf16[1024,384]{1,0:T(8,128)(2,1)} all-gather(bf16[256,384]{1,0:T(8,128)(2,1)S(1)} %copy.37), channel_id=1, replica_groups=mesh['seq'=8,'fsdp'=4] {'fsdp'}, dimensions={0}, use_global_device_ids=true | all-gather | bytes 983040 | tf_op jit(solution)/shard_map/all_gather | solution.py:903
  65.7 18.4 %all_gather.10 = bf16[2,1024]{1,0:T(2,128)(2,1)S(1)} all-gather(bf16[2,256]{1,0:T(2,128)(2,1)S(1)} %pad_maximum_fusion.7), channel_id=1, replica_groups=mesh['seq'=8,'fsdp'=4] {'fsdp'}, dimensions={1}, use_global_device_ids=true | all-gather | bytes 5120 | tf_op jit(solution)/shard_map/all_gather | solution.py:904
  113.1 39.2 %attention_forward.1 = (bf16[8,256,1024]{2,1,0:T(8,128)(2,1)}, bf16[384,2048]{1,0:T(8,128)(2,1)}, bf16[8,256,128]{2,1,0:T(8,128)(2,1)}, f32[128,2048]{1,0:T(8,128)}, f32[2,2048]{1,0:T(2,128)}) custom-call(s32[8]{0:T(128)} %get-tuple-element.108.low_ref, s32[8]{0:T(128)} %get-tuple-element.107.high_ref, ...), custom_call_target="tpu_custom_call" | custom-call | flops 24000000000 | bytes 20000000 | tf_op jit(solution)/shard_map/attention_forward/pallas_call | solution.py:289
  152.3 5.3 %all-to-all-start = ((bf16[8,256,128]{2,1,0:T(8,128)(2,1)}), bf16[8,256,128]{2,1,0:T(8,128)(2,1)S(1)}, u32[]{:S(2)}, u32[]{:S(2)}) async-start(bf16[8,256,128]{2,1,0:T(8,128)(2,1)} %get-tuple-element.21), calls=%async_computation | async-start | bytes 1048576 | tf_op jit(solution)/shard_map/all_to_all | solution.py:917
  158.8 11.5 %hidden_grad.1.gh_ref = f32[256,2688]{1,0:T(8,128)} custom-call(s32[8]{0:T(128)} %pad_add_fusion.place_ref, bf16[256,1024]{1,0:T(8,128)(2,1)} %bitcast.12.cot_ref, bf16[656,1024]{1,0:T(8,128)(2,1)} %refs_0_.6, bf16[656,512]{1,0:T(8,128)(2,1)} %collective-permute-done.refs_1_, bf16[656,512]{1,0:T(8,128)(2,1)} %collective-permute-done.1.refs_2_, ...), custom_call_target="tpu_custom_call" | custom-call | flops 4000000000 | bytes 9000000 | tf_op jit(solution)/shard_map/hidden_grad/pallas_call | solution.py:496
  172.9 31.0 %feed_forward.1 = (f32[256,1024]{1,0:T(8,128)}, f32[256,1024]{1,0:T(8,128)}, bf16[256,1024]{1,0:T(8,128)(2,1)}, bf16[256,5248]{1,0:T(8,128)(2,1)}, bf16[256,2688...) custom-call(s32[8]{0:T(128)} %pad_add_fusion.place_ref, ...), custom_call_target="tpu_custom_call" | custom-call | flops 16000000000 | bytes 24000000 | tf_op jit(solution)/shard_map/feed_forward/pallas_call | solution.py:673
  226.8 34.4 %attention_backward.1.grad_ref = bf16[8,256,384]{2,1,0:T(8,128)(2,1)} custom-call(s32[8]{0:T(128)} %get-tuple-element.108.low_ref, s32[8]{0:T(128)} %get-tuple-element.107.high_ref, bf16[8,256,128]{2,1,0:T(8,128)(2,1)} %copy-done.22, bf16[384,2048]{1,0:T(8,128)(2,1)} %get-tuple-element.26.packed_ref, f32[128,2048]{1,0:T(8,128)} %get-tuple-element.27.out_ref, ...), custom_call_target="tpu_custom_call" | custom-call | flops 30000001024 | bytes 10000000 | tf_op jit(solution)/shard_map/attention_backward/pallas_call | solution.py:421
  261.4 7.1 %qkv_weight_grad.1 = bf16[1024,384]{1,0:T(8,128)(2,1)} custom-call(bf16[8,256,1024]{2,1,0:T(8,128)(2,1)} %get-tuple-element.29.normed_ref, bf16[8,256,384]{2,1,0:T(8,128)(2,1)} %attention_backward.1.grad_ref), custom_call_target="tpu_custom_call" | custom-call | flops 3000000000 | bytes 6000000 | tf_op jit(solution)/shard_map/qkv_weight_grad/pallas_call | solution.py:457
  289.8 8.8 %in_grad.1 = bf16[4,128,5248]{2,1,0:T(8,128)(2,1)} custom-call(s32[8]{0:T(128)} %pad_add_fusion.place_ref, bf16[256,1024]{1,0:T(8,128)(2,1)} %get-tuple-element.32.left_ref, bf16[256,1024]{1,0:T(8,128)(2,1)} %collective-permute-done.40.left_other_ref, bf16[256,5248]{1,0:T(8,128)(2,1)} %get-tuple-element.33.right_ref, ...), custom_call_target="tpu_custom_call" | custom-call | flops 5502926848 | bytes 10747904 | tf_op jit(solution)/shard_map/in_grad/pallas_call | solution.py:727
  303.1 6.1 %down_grad.1 = bf16[4,656,512]{2,1,0:T(8,128)(2,1)} custom-call(s32[8]{0:T(128)} %pad_add_fusion.place_ref, bf16[256,2688]{1,0:T(8,128)(2,1)} %get-tuple-element.23.hid_ref, bf16[256,2688]{1,0:T(8,128)(2,1)} %collective-permute-done.50.hid_other_ref, bf16[256,1024]{1,0:T(8,128)(2,1)} %bitcast.12.cot_ref, bf16[256,1024]{1,0:T(8,128)(2,1)} %collective-permute-done.51.cot_other_ref), custom_call_target="tpu_custom_call" | custom-call | flops 3000000000 | bytes 6000000 | tf_op jit(solution)/shard_map/down_grad/pallas_call | solution.py:774
  314.5 12.0 %collective-permute-done.53 = bf16[656,512]{1,0:T(8,128)(2,1)S(1)} collective-permute-done((bf16[656,512]{1,0:T(8,128)(2,1)S(1)}, bf16[656,512]{1,0:T(8,128)(2,1)S(1)}, u32[]{:S(2)}, u32[]{:S(2)}) %collective-permute-start.53) | collective-permute-done | bytes 671776 | tf_op jit(solution)/shard_map/ppermute | solution.py:45
  334.4 11.1 %collective-permute-done.28 = bf16[1,2,256,384]{3,2,1,0:T(8,128)(2,1)S(1)} collective-permute-done((bf16[1,2,256,384]{3,2,1,0:T(8,128)(2,1)S(1)}, bf16[1,2,256,384]{3,2,1,0:T(8,128)(2,1)S(1)}, u32[]{:S(2)}, u32[]{:S(2)}) %collective-permute-start.28) | collective-permute-done | bytes 393248 | tf_op jit(solution)/shard_map/ppermute | solution.py:70
  347.3 7.3 %layer_result.1 = bf16[256,1024]{1,0:T(8,128)(2,1)} custom-call(s32[8]{0:T(128)} %pad_add_fusion.place_ref, f32[256,1024]{1,0:T(8,128)} %get-tuple-element.22.mid_ref, bf16[256,2688]{1,0:T(8,128)(2,1)} %get-tuple-element.23.hid_ref, bf16[656,1024]{1,0:T(8,128)(2,1)} %refs_0_.6, bf16[656,512]{1,0:T(8,128)(2,1)} %collective-permute-done.refs_1_, ...), custom_call_target="tpu_custom_call" | custom-call | flops 4000000000 | bytes 9000000 | tf_op jit(solution)/shard_map/layer_result/pallas_call | solution.py:532
  354.6 6.4 %all-to-all-start.2 = ((bf16[8,256,384]{2,1,0:T(8,128)(2,1)}), bf16[8,256,384]{2,1,0:T(8,128)(2,1)}, u32[]{:S(2)}, u32[]{:S(2)}) async-start(bf16[8,256,384]{2,1,0:T(8,128)(2,1)} %attention_backward.1.grad_ref), calls=%async_computation.2 | async-start | bytes 3145728 | tf_op jit(solution)/shard_map/all_to_all | solution.py:947
  368.0 6.3 %collective-permute-done.44 = bf16[128,5248]{1,0:T(8,128)(2,1)} collective-permute-done((bf16[128,5248]{1,0:T(8,128)(2,1)}, bf16[128,5248]{1,0:T(8,128)(2,1)}, u32[]{:S(2)}, u32[]{:S(2)}) %collective-permute-start.44) | collective-permute-done | bytes 1343520 | tf_op jit(solution)/shard_map/ppermute | solution.py:45
  379.6 8.0 %collective-permute-done.20.refs_3_ = bf16[128,3072]{1,0:T(8,128)(2,1)} collective-permute-done((bf16[128,3072]{1,0:T(8,128)(2,1)}, bf16[128,3072]{1,0:T(8,128)(2,1)}, u32[]{:S(2)}, u32[]{:S(2)}) %collective-permute-start.20) | collective-permute-done | bytes 786464 | tf_op jit(solution)/shard_map/ppermute | solution.py:45
  388.0 17.5 %collective-permute-done.29 = bf16[2,2,256,384]{3,2,1,0:T(8,128)(2,1)S(1)} collective-permute-done((bf16[2,2,256,384]{3,2,1,0:T(8,128)(2,1)S(1)}, bf16[2,2,256,384]{3,2,1,0:T(8,128)(2,1)S(1)}, u32[]{:S(2)}, u32[]{:S(2)}) %collective-permute-start.29) | collective-permute-done | bytes 786464 | tf_op jit(solution)/shard_map/ppermute | solution.py:70
  407.1 5.7 %collective-permute-done.55 = bf16[256,656]{0,1:T(8,128)(2,1)S(1)} collective-permute-done((bf16[256,656]{0,1:T(8,128)(2,1)S(1)}, bf16[256,656]{0,1:T(8,128)(2,1)S(1)}, u32[]{:S(2)}, u32[]{:S(2)}) %collective-permute-start.55) | collective-permute-done | bytes 335904 | tf_op jit(solution)/shard_map/ppermute | solution.py:70
  415.1 15.6 %collective-permute-done.45 = bf16[64,5248]{1,0:T(8,128)(2,1)S(1)} collective-permute-done((bf16[64,5248]{1,0:T(8,128)(2,1)S(1)}, bf16[64,5248]{1,0:T(8,128)(2,1)S(1)}, u32[]{:S(2)}, u32[]{:S(2)}) %collective-permute-start.45) | collective-permute-done | bytes 671776 | tf_op jit(solution)/shard_map/ppermute | solution.py:70
  433.6 18.8 %collective-permute-done.46 = bf16[32,5248]{1,0:T(8,128)(2,1)S(1)} collective-permute-done((bf16[32,5248]{1,0:T(8,128)(2,1)S(1)}, bf16[32,5248]{1,0:T(8,128)(2,1)S(1)}, u32[]{:S(2)}, u32[]{:S(2)}) %collective-permute-start.46) | collective-permute-done | bytes 335904 | tf_op jit(solution)/shard_map/ppermute | solution.py:70
  452.5 10.6 %collective-permute-done.57 = bf16[128,656]{0,1:T(8,128)(2,1)S(1)} collective-permute-done((bf16[128,656]{0,1:T(8,128)(2,1)S(1)}, bf16[128,656]{0,1:T(8,128)(2,1)S(1)}, u32[]{:S(2)}, u32[]{:S(2)}) %collective-permute-start.57) | collective-permute-done | bytes 167968 | tf_op jit(solution)/shard_map/ppermute | solution.py:70
  464.0 6.4 %collective-permute-done.47 = bf16[32,5248]{1,0:T(8,128)(2,1)S(1)} collective-permute-done((bf16[32,5248]{1,0:T(8,128)(2,1)S(1)}, bf16[32,5248]{1,0:T(8,128)(2,1)S(1)}, u32[]{:S(2)}, u32[]{:S(2)}) %collective-permute-start.47) | collective-permute-done | bytes 335904 | tf_op jit(solution)/shard_map/ppermute | solution.py:70
  480.3 11.7 %collective-permute-done.48 = bf16[64,5248]{1,0:T(8,128)(2,1)} collective-permute-done((bf16[64,5248]{1,0:T(8,128)(2,1)}, bf16[64,5248]{1,0:T(8,128)(2,1)}, u32[]{:S(2)}, u32[]{:S(2)}) %collective-permute-start.48) | collective-permute-done | bytes 671776 | tf_op jit(solution)/shard_map/ppermute | solution.py:70
  499.3 10.8 %input_grad.1 = bf16[256,1024]{1,0:T(8,128)(2,1)} custom-call(s32[8]{0:T(128)} %pad_add_fusion.place_ref, bf16[256,1024]{1,0:T(8,128)(2,1)} %bitcast.90, f32[256,1024]{1,0:T(8,128)} %get-tuple-element.24.gmid_ref, f32[1,1024]{1,0:T(1,128)} %get-tuple-element.101.gain_ref, bf16[8,256,384]{2,1,0:T(8,128)(2,1)} %all-to-all-done.2.g_ref, ...), custom_call_target="tpu_custom_call" | custom-call | flops 4000000000 | bytes 10000000 | tf_op jit(solution)/shard_map/input_grad/pallas_call | solution.py:831
  (278 shorter events, 153.8 us)
Async XLA Ops:
  7.2 105.9 %all-gather.2.cloned.1.call-start = ((), (), s32[]{:S(2)}) async-start(), calls=%async_computation.3 | async-start | bytes 4718592 | tf_op jit(solution)/shard_map/all_gather | solution.py:901
  10.6 54.1 %collective-permute-start.12 = (bf16[128,5248]{1,0:T(8,128)(2,1)}, bf16[128,5248]{1,0:T(8,128)(2,1)}, u32[]{:S(2)}, u32[]{:S(2)}) collective-permute-start(bf16[128,5248]{1,0:T(8,128)(2,1)} %constant_dynamic-slice_fusion.8), channel_id=1, source_target_pairs={{0,1},{1,0},{2,3},{3,2},{4,6},{5,7},{6,4},{7,5},{8,9},{9,8},{10,11... | collective-permute-start | bytes 4030472 | tf_op jit(solution)/shard_map/ppermute | solution.py:45
  12.6 99.8 %collective-permute-start.13 = (bf16[128,5248]{1,0:T(8,128)(2,1)}, bf16[128,5248]{1,0:T(8,128)(2,1)}, u32[]{:S(2)}, u32[]{:S(2)}) collective-permute-start(bf16[128,5248]{1,0:T(8,128)(2,1)} %constant_dynamic-slice_fusion.8), channel_id=1, source_target_pairs={{0,2},{1,3},{2,0},{3,1},{4,5},{5,4},{6,7},{7,6},{8,10},{9,11},{10,... | collective-permute-start | bytes 4030472 | tf_op jit(solution)/shard_map/ppermute | solution.py:45
  14.6 70.1 %collective-permute-start.6 = (bf16[128,1024]{1,0:T(8,128)(2,1)}, bf16[128,1024]{1,0:T(8,128)(2,1)}, u32[]{:S(2)}, u32[]{:S(2)}) collective-permute-start(bf16[128,1024]{1,0:T(8,128)(2,1)} %constant_dynamic-slice_fusion.9), channel_id=1, source_target_pairs={{0,1},{1,0},{2,3},{3,2},{4,6},{5,7},{6,4},{7,5},{8,9},{9,8},{10,11... | collective-permute-start | bytes 786440 | tf_op jit(solution)/shard_map/ppermute | solution.py:45
  14.8 70.5 %collective-permute-start.7 = (bf16[128,1024]{1,0:T(8,128)(2,1)}, bf16[128,1024]{1,0:T(8,128)(2,1)}, u32[]{:S(2)}, u32[]{:S(2)}) collective-permute-start(bf16[128,1024]{1,0:T(8,128)(2,1)} %constant_dynamic-slice_fusion.9), channel_id=1, source_target_pairs={{0,2},{1,3},{2,0},{3,1},{4,5},{5,4},{6,7},{7,6},{8,10},{9,11},{10,... | collective-permute-start | bytes 786440 | tf_op jit(solution)/shard_map/ppermute | solution.py:45
  15.7 75.0 %collective-permute-start = (bf16[656,512]{1,0:T(8,128)(2,1)}, bf16[656,512]{1,0:T(8,128)(2,1)}, u32[]{:S(2)}, u32[]{:S(2)}) collective-permute-start(bf16[656,512]{1,0:T(8,128)(2,1)} %constant_dynamic-slice_fusion.10), channel_id=1, source_target_pairs={{0,1},{1,0},{2,3},{3,2},{4,6},{5,7},{6,4},{7,5},{8,9},{9,8},{10,11... | collective-permute-start | bytes 2015240 | tf_op jit(solution)/shard_map/ppermute | solution.py:45
  64.6 48.3 %collective-permute-start.14 = (bf16[128,5248]{1,0:T(8,128)(2,1)}, bf16[128,5248]{1,0:T(8,128)(2,1)}, u32[]{:S(2)}, u32[]{:S(2)}) collective-permute-start(bf16[128,5248]{1,0:T(8,128)(2,1)} %collective-permute-done.12.refs_8_), channel_id=1, source_target_pairs={{0,2},{1,3},{2,0},{3,1},{4,5},{5,4},{6,7},{7,6},{8,10},{9,11},{10,... | collective-permute-start | bytes 4030472 | tf_op jit(solution)/shard_map/ppermute | solution.py:45
  100.4 58.0 %collective-permute-start.4 = (bf16[656,512]{1,0:T(8,128)(2,1)}, bf16[656,512]{1,0:T(8,128)(2,1)}, u32[]{:S(2)}, u32[]{:S(2)}) collective-permute-start(bf16[656,512]{1,0:T(8,128)(2,1)} %collective-permute-done.1.refs_2_), channel_id=1, source_target_pairs={{0,4},{4,0},{8,12},{12,8},{16,20},{20,16},{24,28},{28,24},{1,5},{5... | collective-permute-start | bytes 2015240 | tf_op jit(solution)/shard_map/ppermute | solution.py:23
  107.6 62.8 %collective-permute-start.15 = (bf16[128,5248]{1,0:T(8,128)(2,1)}, bf16[128,5248]{1,0:T(8,128)(2,1)}, u32[]{:S(2)}, u32[]{:S(2)}) collective-permute-start(bf16[128,5248]{1,0:T(8,128)(2,1)} %collective-permute-done.12.refs_8_), channel_id=1, source_target_pairs={{0,4},{4,0},{8,12},{12,8},{16,20},{20,16},{24,28},{28,24},{1,5},{5... | collective-permute-start | bytes 4030472 | tf_op jit(solution)/shard_map/ppermute | solution.py:23
  112.5 45.9 %collective-permute-start.5 = (bf16[656,512]{1,0:T(8,128)(2,1)}, bf16[656,512]{1,0:T(8,128)(2,1)}, u32[]{:S(2)}, u32[]{:S(2)}) collective-permute-start(bf16[656,512]{1,0:T(8,128)(2,1)} %collective-permute-done.2.refs_3_), channel_id=1, source_target_pairs={{0,4},{4,0},{8,12},{12,8},{16,20},{20,16},{24,28},{28,24},{1,5},{5... | collective-permute-start | bytes 2015240 | tf_op jit(solution)/shard_map/ppermute | solution.py:23
  112.5 58.0 %collective-permute-start.16 = (bf16[128,5248]{1,0:T(8,128)(2,1)}, bf16[128,5248]{1,0:T(8,128)(2,1)}, u32[]{:S(2)}, u32[]{:S(2)}) collective-permute-start(bf16[128,5248]{1,0:T(8,128)(2,1)} %collective-permute-done.13.refs_9_), channel_id=1, source_target_pairs={{0,4},{4,0},{8,12},{12,8},{16,20},{20,16},{24,28},{28,24},{1,5},{5... | collective-permute-start | bytes 4030472 | tf_op jit(solution)/shard_map/ppermute | solution.py:23
  113.0 57.5 %collective-permute-start.17 = (bf16[128,5248]{1,0:T(8,128)(2,1)}, bf16[128,5248]{1,0:T(8,128)(2,1)}, u32[]{:S(2)}, u32[]{:S(2)}) collective-permute-start(bf16[128,5248]{1,0:T(8,128)(2,1)} %collective-permute-done.14.refs_10_), channel_id=1, source_target_pairs={{0,4},{4,0},{8,12},{12,8},{16,20},{20,16},{24,28},{28,24},{1,5},{5... | collective-permute-start | bytes 4030472 | tf_op jit(solution)/shard_map/ppermute | solution.py:23
  205.0 97.1 %collective-permute-start.51 = (bf16[256,1024]{1,0:T(8,128)(2,1)}, bf16[256,1024]{1,0:T(8,128)(2,1)}, u32[]{:S(2)}, u32[]{:S(2)}) collective-permute-start(bf16[256,1024]{1,0:T(8,128)(2,1)} %bitcast.12.cot_ref), channel_id=1, source_target_pairs={{0,4},{4,0},{8,12},{12,8},{16,20},{20,16},{24,28},{28,24},{1,5},{5... | collective-permute-start | bytes 1572872 | tf_op jit(solution)/shard_map/ppermute | solution.py:23
  218.4 71.3 %collective-permute-start.41 = (bf16[256,5248]{1,0:T(8,128)(2,1)}, bf16[256,5248]{1,0:T(8,128)(2,1)}, u32[]{:S(2)}, u32[]{:S(2)}) collective-permute-start(bf16[256,5248]{1,0:T(8,128)(2,1)} %get-tuple-element.33.right_ref), channel_id=1, source_target_pairs={{0,4},{4,0},{8,12},{12,8},{16,20},{20,16},{24,28},{28,24},{1,5},{5... | collective-permute-start | bytes 8060936 | tf_op jit(solution)/shard_map/ppermute | solution.py:23
  218.8 70.8 %collective-permute-start.40 = (bf16[256,1024]{1,0:T(8,128)(2,1)}, bf16[256,1024]{1,0:T(8,128)(2,1)}, u32[]{:S(2)}, u32[]{:S(2)}) collective-permute-start(bf16[256,1024]{1,0:T(8,128)(2,1)} %get-tuple-element.32.left_ref), channel_id=1, source_target_pairs={{0,4},{4,0},{8,12},{12,8},{16,20},{20,16},{24,28},{28,24},{1,5},{5... | collective-permute-start | bytes 1572872 | tf_op jit(solution)/shard_map/ppermute | solution.py:23
  218.9 42.3 %collective-permute-start.32 = (bf16[128,1024]{1,0:T(8,128)(2,1)S(1)}, bf16[128,1024]{1,0:T(8,128)(2,1)S(1)}, u32[]{:S(2)}, u32[]{:S(2)}) collective-permute-start(bf16[128,1024]{1,0:T(8,128)(2,1)S(1)} %get-tuple-element.74), channel_id=1, source_target_pairs={{0,2},{1,3},{2,0},{3,1},{4,5},{5,4},{6,7},{7,6},{8,10},{9,11},{10,... | collective-permute-start | bytes 786440 | tf_op jit(solution)/shard_map/ppermute | solution.py:45
  281.0 82.3 %collective-permute-start.18 = (bf16[128,3072]{1,0:T(8,128)(2,1)}, bf16[128,3072]{1,0:T(8,128)(2,1)}, u32[]{:S(2)}, u32[]{:S(2)}) collective-permute-start(bf16[128,3072]{1,0:T(8,128)(2,1)} %constant_dynamic-slice_fusion.7), channel_id=1, source_target_pairs={{0,1},{1,0},{2,3},{3,2},{4,6},{5,7},{6,4},{7,5},{8,9},{9,8},{10,11... | collective-permute-start | bytes 2359304 | tf_op jit(solution)/shard_map/ppermute | solution.py:45
  312.0 51.8 %collective-permute-start.52 = (bf16[656,512]{1,0:T(8,128)(2,1)}, bf16[656,512]{1,0:T(8,128)(2,1)}, u32[]{:S(2)}, u32[]{:S(2)}) collective-permute-start(bf16[656,512]{1,0:T(8,128)(2,1)} %get-tuple-element.64), channel_id=1, source_target_pairs={{0,2},{1,3},{2,0},{3,1},{4,5},{5,4},{6,7},{7,6},{8,10},{9,11},{10,... | collective-permute-start | bytes 2015240 | tf_op jit(solution)/shard_map/ppermute | solution.py:45
  354.6 144.7 %all-to-all-start.2 = ((bf16[8,256,384]{2,1,0:T(8,128)(2,1)}), bf16[8,256,384]{2,1,0:T(8,128)(2,1)}, u32[]{:S(2)}, u32[]{:S(2)}) async-start(bf16[8,256,384]{2,1,0:T(8,128)(2,1)} %attention_backward.1.grad_ref), calls=%async_computation.2 | async-start | bytes 3145728 | tf_op jit(solution)/shard_map/all_to_all | solution.py:947
  367.9 44.9 %collective-permute-start.55 = (bf16[256,656]{0,1:T(8,128)(2,1)S(1)}, bf16[256,656]{0,1:T(8,128)(2,1)S(1)}, u32[]{:S(2)}, u32[]{:S(2)}) collective-permute-start(bf16[256,656]{0,1:T(8,128)(2,1)S(1)} %dynamic-slice_bitcast_fusion), channel_id=1, source_target_pairs={{0,8},{4,12},{8,0},{12,4},{16,24},{20,28},{24,16},{28,20},{1,9},{5... | collective-permute-start | bytes 1007624 | tf_op jit(solution)/shard_map/ppermute | solution.py:70
  377.0 53.8 %collective-permute-start.45 = (bf16[64,5248]{1,0:T(8,128)(2,1)S(1)}, bf16[64,5248]{1,0:T(8,128)(2,1)S(1)}, u32[]{:S(2)}, u32[]{:S(2)}) collective-permute-start(bf16[64,5248]{1,0:T(8,128)(2,1)S(1)} %constant_dynamic-slice_fusion.2), channel_id=1, source_target_pairs={{0,8},{4,12},{8,0},{12,4},{16,24},{20,28},{24,16},{28,20},{1,9},{5... | collective-permute-start | bytes 2015240 | tf_op jit(solution)/shard_map/ppermute | solution.py:70
  379.5 119.8 %collective-permute-start.21 = (bf16[128,3072]{1,0:T(8,128)(2,1)}, bf16[128,3072]{1,0:T(8,128)(2,1)}, u32[]{:S(2)}, u32[]{:S(2)}) collective-permute-start(bf16[128,3072]{1,0:T(8,128)(2,1)} %collective-permute-done.18.refs_1_), channel_id=1, source_target_pairs={{0,4},{4,0},{8,12},{12,8},{16,20},{20,16},{24,28},{28,24},{1,5},{5... | collective-permute-start | bytes 2359304 | tf_op jit(solution)/shard_map/ppermute | solution.py:23
  387.6 111.7 %collective-permute-start.22 = (bf16[128,3072]{1,0:T(8,128)(2,1)}, bf16[128,3072]{1,0:T(8,128)(2,1)}, u32[]{:S(2)}, u32[]{:S(2)}) collective-permute-start(bf16[128,3072]{1,0:T(8,128)(2,1)} %collective-permute-done.19.refs_2_), channel_id=1, source_target_pairs={{0,4},{4,0},{8,12},{12,8},{16,20},{20,16},{24,28},{28,24},{1,5},{5... | collective-permute-start | bytes 2359304 | tf_op jit(solution)/shard_map/ppermute | solution.py:23
  405.5 93.8 %collective-permute-start.23 = (bf16[128,3072]{1,0:T(8,128)(2,1)}, bf16[128,3072]{1,0:T(8,128)(2,1)}, u32[]{:S(2)}, u32[]{:S(2)}) collective-permute-start(bf16[128,3072]{1,0:T(8,128)(2,1)} %collective-permute-done.20.refs_3_), channel_id=1, source_target_pairs={{0,4},{4,0},{8,12},{12,8},{16,20},{20,16},{24,28},{28,24},{1,5},{5... | collective-permute-start | bytes 2359304 | tf_op jit(solution)/shard_map/ppermute | solution.py:23
  (81 other events, 1369.5 us)
Sparse Core Ops, SparseCore 0:
  9.6 49.6 all-gather.1

commit v2 on v1

v2 whole, which is shorter than its diff:
```python
import functools
import math

import jax
import jax.numpy as jnp
from jax import lax
from jax.experimental import pallas as pl
from jax.experimental.pallas import tpu as pltpu
from jax.sharding import PartitionSpec as P

HD = 64
NORM_EPS = 1e-05
ROPE_BASE = 160000.0
BLOCK = 256
WIDE = 512
LOG2E = math.log2(math.e)
AXES = ("seq", "fsdp")
F32 = jnp.float32
BF16 = jnp.bfloat16
VMEM_LIMIT = 60 * 1024 * 1024


def core_swap(value, seq_count):
    return lax.ppermute(value, "seq", [(i, i ^ 1) for i in range(seq_count)])


def plane_bit(core, phase, levels):
    return (phase + core * (levels // 2)) % levels


def plane_mask(core, key, levels):
    mask = 0
    for phase in range(levels):
        if key >> phase & 1:
            mask |= 1 << plane_bit(core, phase, levels)
    return mask


def plane_swap(value, phase, seq_count, fsdp_count):
    levels = fsdp_count.bit_length() - 1
    pairs = []
    for s in range(seq_count):
        step = 1 << plane_bit(s & 1, phase, levels)
        for f in range(fsdp_count):
            pairs.append((s * fsdp_count + f, s * fsdp_count + (f ^ step)))
    return lax.ppermute(value, AXES, pairs)


def after(value, *others):
    return lax.optimization_barrier((value, *others))[0]


def plane_gather(piece, seq_count, fsdp_count, *others):
    pieces = [piece]
    for phase in range(fsdp_count.bit_length() - 1):
        if phase == 1:
            pieces[0] = after(piece, pieces[1], *others)
        pieces = pieces + [plane_swap(p, phase, seq_count, fsdp_count) for p in pieces]
    return pieces[1:]


def added(*values):
    return sum(v.astype(F32) for v in values).astype(BF16)


def plane_reduce(first, b, c, seq_count, fsdp_count):
    second = plane_swap(added(b[0], first[1]), 0, seq_count, fsdp_count)
    return c[0], first[0], second


def line_swap(value, level, seq_count):
    return lax.ppermute(value, "seq", [(i, i ^ (2 << level)) for i in range(seq_count)])


def line_reduce(parts, seq_count):
    got = line_swap(added(*(p[2:] for p in parts)), 0, seq_count)
    last = line_swap(added(*(p[1] for p in parts), got[1]), 1, seq_count)
    return added(*(p[0] for p in parts), got[0], last)


def line_gather(block, seq_count):
    pair = jnp.stack([block, line_swap(block, 1, seq_count)])
    rest = line_swap(pair, 0, seq_count)
    return [pair, rest, core_swap(pair, seq_count), core_swap(rest, seq_count)]


def any_spec():
    return pl.BlockSpec(memory_space=pl.ANY)


def vmem_spec():
    return pl.BlockSpec(memory_space=pltpu.VMEM)


def smem_spec():
    return pl.BlockSpec(memory_space=pltpu.SMEM)


def params():
    return pltpu.CompilerParams(vmem_limit_bytes=VMEM_LIMIT)


def cost(flops, moved):
    return pl.CostEstimate(flops=int(flops), bytes_accessed=int(moved), transcendentals=0)


def nt_dot(a, b):
    return lax.dot_general(a, b, (((1,), (1,)), ((), ())), preferred_element_type=F32)


def nn_dot(a, b):
    return jnp.dot(a, b, preferred_element_type=F32)


def own_copy(place_ref, own, full, sems, rows):
    base = pl.multiple_of(place_ref[0] * rows, 16)
    return pltpu.make_async_copy(own, full.at[pl.ds(base, rows), :], sems.at[0])


def row_copies(place_ref, own, mine, others, left, full, sems):
    count = len(mine)
    rows = own.shape[0]
    half = rows // 2
    core = place_ref[2 * count + 1]
    copies = [own_copy(place_ref, own, full, sems, rows)]
    for which, (refs, side) in enumerate(((mine, core), (others, 1 - core))):
        for i, ref in enumerate(refs):
            at = 1 + which * count + i
            base = pl.multiple_of(place_ref[at] * rows + side * half, 16)
            copies.append(
                pltpu.make_async_copy(
                    ref.at[:, pl.ds(left, full.shape[1])], full.at[pl.ds(base, half), :], sems.at[at]
                )
            )
    return copies


def down_blocks(rows, tall):
    return [(start, min(tall, rows - start)) for start in range(0, rows, tall)]


def down_copies(place_ref, own, mine, others, left, full, sems, hidden):
    if not mine:
        return [pltpu.make_async_copy(own, full.at[pl.ds(0, hidden), :], sems.at[0])]
    count = len(mine)
    rows = own.shape[0]
    half = own.shape[1] // 2
    core = place_ref[2 * count + 1]
    blocks = down_blocks(rows, mine[0].shape[0])
    copies = [own_copy(place_ref, own, full, sems, rows)]
    for which, (refs, side) in enumerate(((mine, core), (others, 1 - core))):
        for i, ref in enumerate(refs):
            at = 1 + which * count + i
            side_at = pl.multiple_of(side * half, 128)
            for k, (start, tall) in enumerate(blocks):
                base = pl.multiple_of(place_ref[at] * rows + start, 16)
                copies.append(
                    pltpu.make_async_copy(
                        ref.at[pl.ds(0, tall), pl.ds(left + k * half, half)],
                        full.at[pl.ds(base, tall), pl.ds(side_at, half)],
                        sems.at[1 + (at - 1) * len(blocks) + k],
                    )
                )
    return copies


def pack_pieces(place_ref, in_ref, out_ref, down_ref, packed_ref, sems):
    half = in_ref.shape[0] // 2
    core = place_ref[place_ref.shape[0] - 2]
    base = pl.multiple_of(core * half, 16)
    wide, also = in_ref.shape[1], out_ref.shape[1]
    copies = [
        pltpu.make_async_copy(
            in_ref.at[pl.ds(base, half), :], packed_ref.at[:, pl.ds(0, wide)], sems.at[0]
        ),
        pltpu.make_async_copy(
            out_ref.at[pl.ds(base, half), :], packed_ref.at[:, pl.ds(wide, also)], sems.at[1]
        ),
    ]
    if packed_ref.shape[1] > wide + also:
        columns = down_ref.shape[1] // 2
        side = pl.multiple_of(core * columns, 128)
        for k, (start, tall) in enumerate(down_blocks(down_ref.shape[0], half)):
            copies.append(
                pltpu.make_async_copy(
                    down_ref.at[pl.ds(start, tall), pl.ds(side, columns)],
                    packed_ref.at[pl.ds(0, tall), pl.ds(wide + also + k * columns, columns)],
                    sems.at[2 + k],
                )
            )
    for copy in copies:
        copy.start()
    for copy in copies:
        copy.wait()


def run_pack_pieces(place, w_in, w_out, w_down, regular):
    half = w_in.shape[0] // 2
    blocks = len(down_blocks(w_down.shape[0], half)) if regular else 0
    wide = w_in.shape[1] + w_out.shape[1] + blocks * (w_down.shape[1] // 2)
    return pl.pallas_call(
        pack_pieces,
        name="pack_pieces",
        out_shape=jax.ShapeDtypeStruct((half, wide), BF16),
        in_specs=[smem_spec()] + [any_spec()] * 3,
        out_specs=vmem_spec(),
        scratch_shapes=[pltpu.SemaphoreType.DMA((2 + blocks,))],
        compiler_params=params(),
        cost_estimate=cost(1e6, 5e6),
    )(place, w_in, w_out, w_down)


def attention_forward(
    seq_count, heads, group, low_ref, high_ref, place_ref, x_hbm, order_ref, start_ref, end_ref,
    cos_ref, sin_ref, *refs,
):
    pieces, refs = refs[:-15], refs[-15:]
    gains_ref, normed_hbm, packed_ref, att_ref, out_ref, lse_ref = refs[:6]
    w_ref, x_ref, normed_ref, qkv_t, k_rows, o_rows, scores_ref, x_sems, normed_sems = refs[6:15]
    width = heads * HD
    rows = group // seq_count
    blocks = group // BLOCK
    fetches = [pltpu.make_async_copy(x_hbm.at[i], x_ref.at[i], x_sems.at[i]) for i in range(seq_count)]
    stores = [
        pltpu.make_async_copy(normed_ref.at[i], normed_hbm.at[i], normed_sems.at[i]) for i in range(seq_count)
    ]
    for fetch in fetches:
        fetch.start()
    if len(pieces) == 2:
        w_ref[...] = pieces[0][...]
        gains_ref[...] = pieces[1][...]
    else:
        tall = w_ref.shape[0] // len(pieces)
        for mask, piece in enumerate(pieces):
            base = pl.multiple_of((place_ref[0] ^ mask) * tall, 128)
            w_ref[pl.ds(base, tall), :] = piece[:tall]
            gains_ref[:, pl.ds(base, tall)] = piece[tall : tall + 2, :tall].astype(F32)
    gain_ref = gains_ref.at[pl.ds(0, 1), :]

    def project(i):
        x = x_ref[i].astype(F32)
        center = x - jnp.mean(x, axis=-1, keepdims=True)
        spread = jnp.mean(center * center, axis=-1, keepdims=True)
        normed = (center * lax.rsqrt(spread + NORM_EPS) * gain_ref[...]).astype(BF16)
        normed_ref[i] = normed
        qkv = nn_dot(normed, w_ref[...]).astype(BF16)
        qkv_t[i] = qkv.T

    for i in range(seq_count):
        fetches[i].wait()
        project(i)
        stores[i].start()

    def pack(i, carry):
        at = pl.ds(pl.multiple_of(i * BLOCK, BLOCK), BLOCK)
        order = order_ref[:, at]
        total = jnp.zeros((3 * width, BLOCK), F32)
        for s in range(seq_count):
            here = lax.broadcasted_iota(jnp.int32, (rows, BLOCK), 0) + s * rows
            hot = jnp.where(here == order, 1.0, 0.0).astype(BF16)
            total = total + nn_dot(qkv_t[s], hot)
        cos = cos_ref[:, at]
        sin = sin_ref[:, at]
        half = HD // 2
        for part in range(2):
            for h in range(heads):
                base = part * width + h * HD
                first = total[base : base + half]
                second = total[base + half : base + HD]
                turned = jnp.concatenate(
                    [first * cos - second * sin, second * cos + first * sin], axis=0
                ).astype(BF16)
                packed_ref[base : base + HD, at] = turned
                if part == 1:
                    k_rows[h, at, :] = turned.T
        packed_ref[2 * width :, at] = total[2 * width :].astype(BF16)
        return carry

    lax.fori_loop(0, blocks, pack, 0)
    scale = HD**-0.5 * LOG2E

    def attend(i, carry):
        at = pl.ds(pl.multiple_of(i * WIDE, WIDE), WIDE)
        start = start_ref[:, at]
        end = end_ref[:, at]
        queries = [packed_ref[h * HD : (h + 1) * HD, at] for h in range(heads)]

        low, high = low_ref[i], high_ref[i]

        def score(j, tops):
            there = pl.ds(pl.multiple_of(j * BLOCK, BLOCK), BLOCK)
            where = lax.broadcasted_iota(jnp.int32, (BLOCK, WIDE), 0) + j * BLOCK
            same = jnp.logical_and(where >= start, where < end)
            following = []
            for h in range(heads):
                scores = jnp.where(same, nn_dot(k_rows[h, there, :], queries[h]) * scale, -1e30)
                scores_ref[j, h] = scores
                following.append(jnp.maximum(tops[h], jnp.max(scores.reshape(-1, 8, WIDE), axis=0)))
            return tuple(following)

        tops = lax.fori_loop(low, high, score, tuple(jnp.full((8, WIDE), -1e30, F32) for _ in range(heads)))
        tops = [jnp.max(top, axis=0, keepdims=True) for top in tops]

        def weigh(j, state):
            there = pl.ds(pl.multiple_of(j * BLOCK, BLOCK), BLOCK)
            following = []
            for h in range(heads):
                total, acc = state[h]
                probs = jnp.exp2(scores_ref[j, h] - tops[h])
                total = total + jnp.sum(probs.reshape(-1, 8, WIDE), axis=0)
                base = 2 * width + h * HD
                acc = acc + nn_dot(packed_ref[base : base + HD, there], probs.astype(BF16))
                following.append((total, acc))
            return tuple(following)

        first = tuple((jnp.zeros((8, WIDE), F32), jnp.zeros((HD, WIDE), F32)) for _ in range(heads))
        last = lax.fori_loop(low, high, weigh, first)
        outs = []
        for h in range(heads):
            total, acc = last[h]
            total = jnp.sum(total, axis=0, keepdims=True)
            out = acc / total
            out_ref[h * HD : (h + 1) * HD, at] = out
            lse_ref[h : h + 1, at] = tops[h] + jnp.log2(total)
            outs.append(out)
        o_rows[at, :] = jnp.concatenate(outs, axis=0).astype(BF16).T
        return carry

    lax.fori_loop(0, group // WIDE, attend, 0)

    def arrive(i, carry):
        here = lax.broadcasted_iota(jnp.int32, (rows, group), 0) + i * rows
        hot = jnp.where(here == order_ref[...], 1.0, 0.0).astype(BF16)
        att_ref[i] = nn_dot(hot, o_rows[...]).astype(BF16)
        return carry

    lax.fori_loop(0, seq_count, arrive, 0)
    for store in stores:
        store.wait()


def run_attention_forward(place, x_all, pieces, layout, heads):
    seq_count, rows, dim = x_all.shape
    group = seq_count * rows
    width = heads * HD
    (low, high), _, order, start, end, cos, sin = layout
    return pl.pallas_call(
        functools.partial(attention_forward, seq_count, heads, group),
        name="attention_forward",
        out_shape=(
            jax.ShapeDtypeStruct((2, dim), F32),
            jax.ShapeDtypeStruct((seq_count, rows, dim), BF16),
            jax.ShapeDtypeStruct((3 * width, group), BF16),
            jax.ShapeDtypeStruct((seq_count, rows, width), BF16),
            jax.ShapeDtypeStruct((width, group), F32),
            jax.ShapeDtypeStruct((heads, group), F32),
        ),
        in_specs=[smem_spec()] * 3 + [any_spec()] + [vmem_spec()] * (5 + len(pieces)),
        out_specs=[vmem_spec(), any_spec()] + [vmem_spec()] * 4,
        scratch_shapes=[
            pltpu.VMEM((dim, 3 * width), BF16),
            pltpu.VMEM((seq_count, rows, dim), BF16),
            pltpu.VMEM((seq_count, rows, dim), BF16),
            pltpu.VMEM((seq_count, 3 * width, rows), BF16),
            pltpu.VMEM((heads, group, HD), BF16),
            pltpu.VMEM((group, width), BF16),
            pltpu.VMEM((group // BLOCK, heads, BLOCK, WIDE), F32),
            pltpu.SemaphoreType.DMA((seq_count,)),
            pltpu.SemaphoreType.DMA((seq_count,)),
        ],
        compiler_params=params(),
        cost_estimate=cost(24e9, 20e6),
    )(low, high, place, x_all, order, start, end, cos, sin, *pieces)


def attention_backward(
    seq_count, heads, group, low_ref, high_ref, dout_ref, packed_ref, out_ref, lse_ref, order_ref,
    start_ref, end_ref, cos_ref, sin_ref, grad_ref, dout_t, dpack_t, drows, qrows, krows, vrows,
    delta_ref, dq_t, grows,
):
    width = heads * HD
    rows = group // seq_count
    blocks = group // BLOCK
    scale = HD**-0.5

    def turn(i, carry):
        dout_t[i] = dout_ref[i].T
        return carry

    lax.fori_loop(0, seq_count, turn, 0)

    def pack(i, carry):
        at = pl.ds(pl.multiple_of(i * BLOCK, BLOCK), BLOCK)
        order = order_ref[:, at]
        total = jnp.zeros((width, BLOCK), F32)
        for s in range(seq_count):
            here = lax.broadcasted_iota(jnp.int32, (rows, BLOCK), 0) + s * rows
            hot = jnp.where(here == order, 1.0, 0.0).astype(BF16)
            total = total + nn_dot(dout_t[s], hot)
        dpack_t[:, at] = total.astype(BF16)
        for h in range(heads):
            mine = total[h * HD : (h + 1) * HD]
            delta_ref[h : h + 1, at] = jnp.sum(
                mine * out_ref[h * HD : (h + 1) * HD, at], axis=0, keepdims=True
            )
            drows[h, at, :] = mine.T.astype(BF16)
            for part, ref in enumerate((qrows, krows, vrows)):
                base = part * width + h * HD
                ref[h, at, :] = packed_ref[base : base + HD, at].T
        dq_t[:, at] = jnp.zeros((width, BLOCK), F32)
        return carry

    lax.fori_loop(0, blocks, pack, 0)

    def keys(j, carry):
        there = pl.ds(pl.multiple_of(j * BLOCK, BLOCK), BLOCK)
        where = lax.broadcasted_iota(jnp.int32, (BLOCK, WIDE), 0) + j * BLOCK

        def queries(i, state):
            at = pl.ds(pl.multiple_of(i * WIDE, WIDE), WIDE)
            same = jnp.logical_and(where >= start_ref[:, at], where < end_ref[:, at])
            following = []
            for h in range(heads):
                dk, dv = state[h]
                base = h * HD
                key_rows = krows[h, there, :]
                query_t = packed_ref[base : base + HD, at]
                scores = nn_dot(key_rows, query_t) * (scale * LOG2E)
                scores = jnp.where(same, scores, -1e30)
                probs = jnp.exp2(scores - lse_ref[h : h + 1, at])
                dprobs = nn_dot(vrows[h, there, :], dpack_t[base : base + HD, at])
                raw = (probs * (dprobs - delta_ref[h : h + 1, at]) * scale).astype(BF16)
                dv = dv + nn_dot(probs.astype(BF16), drows[h, at, :])
                dk = dk + nn_dot(raw, qrows[h, at, :])
                key_t = packed_ref[width + base : width + base + HD, there]
                dq_t[base : base + HD, at] += nn_dot(key_t, raw)
                following.append((dk, dv))
            return tuple(following)

        zero = jnp.zeros((BLOCK, HD), F32)
        last = lax.fori_loop(low_ref[j], high_ref[j], queries, tuple((zero, zero) for _ in range(heads)))
        cos = cos_ref[:, there]
        sin = sin_ref[:, there]
        half = HD // 2
        turned = []
        for h in range(heads):
            dk_t = last[h][0].T
            first, second = dk_t[:half], dk_t[half:]
            turned.append(first * cos + second * sin)
            turned.append(second * cos - first * sin)
        grows[there, width : 2 * width] = jnp.concatenate(turned, axis=0).T.astype(BF16)
        grows[there, 2 * width :] = jnp.concatenate([last[h][1] for h in range(heads)], axis=1).astype(BF16)
        return carry

    lax.fori_loop(0, blocks, keys, 0)

    def finish(i, carry):
        at = pl.ds(pl.multiple_of(i * BLOCK, BLOCK), BLOCK)
        cos = cos_ref[:, at]
        sin = sin_ref[:, at]
        half = HD // 2
        turned = []
        for h in range(heads):
            first = dq_t[h * HD : h * HD + half, at]
            second = dq_t[h * HD + half : (h + 1) * HD, at]
            turned.append(first * cos + second * sin)
            turned.append(second * cos - first * sin)
        grows[at, :width] = jnp.concatenate(turned, axis=0).T.astype(BF16)
        return carry

    lax.fori_loop(0, blocks, finish, 0)

    def arrive(i, carry):
        here = lax.broadcasted_iota(jnp.int32, (rows, group), 0) + i * rows
        hot = jnp.where(here == order_ref[...], 1.0, 0.0).astype(BF16)
        grad_ref[i] = nn_dot(hot, grows[...]).astype(BF16)
        return carry

    lax.fori_loop(0, seq_count, arrive, 0)


def run_attention_backward(dout, packed, out_t, lse, layout, heads):
    seq_count, rows, width = dout.shape
    group = seq_count * rows
    _, (low, high), order, start, end, cos, sin = layout
    return pl.pallas_call(
        functools.partial(attention_backward, seq_count, heads, group),
        name="attention_backward",
        out_shape=jax.ShapeDtypeStruct((seq_count, rows, 3 * width), BF16),
        in_specs=[smem_spec()] * 2 + [vmem_spec()] * 9,
        out_specs=vmem_spec(),
        scratch_shapes=[
            pltpu.VMEM((seq_count, width, rows), BF16),
            pltpu.VMEM((width, group), BF16),
            pltpu.VMEM((heads, group, HD), BF16),
            pltpu.VMEM((heads, group, HD), BF16),
            pltpu.VMEM((heads, group, HD), BF16),
            pltpu.VMEM((heads, group, HD), BF16),
            pltpu.VMEM((heads, group), F32),
            pltpu.VMEM((width, group), F32),
            pltpu.VMEM((group, 3 * width), BF16),
        ],
        compiler_params=params(),
        cost_estimate=cost(30e9, 10e6),
    )(low, high, dout, packed, out_t, lse, order, start, end, cos, sin)


def qkv_weight_grad(seq_count, place_ref, normed_ref, grad_ref, *refs):
    outs, (total, turned) = refs[:-2], refs[-2:]
    total[...] = jnp.zeros_like(total)

    def step(i, carry):
        total[...] += nn_dot(grad_ref[i].T, normed_ref[i])
        return carry

    lax.fori_loop(0, seq_count, step, 0)
    if len(outs) == 1:
        outs[0][...] = total[...].T.astype(BF16)
        return
    turned[...] = total[...].T
    rows = outs[0].shape[1]
    for ref, keys in zip(outs, ((2, 3), (1,), (0,))):
        for at, key in enumerate(keys):
            base = pl.multiple_of(place_ref[key] * rows, 16)
            ref[at] = turned[pl.ds(base, rows), :].astype(BF16)


def run_qkv_weight_grad(place, normed, grad, regular):
    seq_count, rows, dim = normed.shape
    width = grad.shape[-1]
    if regular:
        outs = tuple(jax.ShapeDtypeStruct((n, dim // 4, width), BF16) for n in (2, 1, 1))
    else:
        outs = (jax.ShapeDtypeStruct((dim, width), BF16),)
    return pl.pallas_call(
        functools.partial(qkv_weight_grad, seq_count),
        name="qkv_weight_grad",
        out_shape=outs,
        in_specs=[smem_spec()] + [vmem_spec()] * 2,
        out_specs=[vmem_spec()] * len(outs),
        scratch_shapes=[pltpu.VMEM((width, dim), F32), pltpu.VMEM((dim, width), F32)],
        compiler_params=params(),
        cost_estimate=cost(3e9, 6e6),
    )(place, normed, grad)


def padded(hidden):
    return -(-hidden // 128) * 128


def load_down(place_ref, refs, count, hidden, left, full, sems):
    copies = down_copies(place_ref, refs[0], refs[1 : 1 + count], refs[1 + count :], left, full, sems, hidden)
    for copy in copies:
        copy.start()
    tail = padded(hidden) - hidden
    if tail:
        full[pl.ds(hidden, tail), :] = jnp.zeros((tail, full.shape[1]), BF16)
    for copy in copies:
        copy.wait()


def down_semaphores(downs):
    if len(downs) == 1:
        return pltpu.SemaphoreType.DMA((1,))
    blocks = len(down_blocks(downs[0].shape[0], downs[1].shape[0]))
    return pltpu.SemaphoreType.DMA((1 + (len(downs) - 1) * blocks,))


def hidden_grad(hidden, left, place_ref, cot_ref, *refs):
    downs, (out_ref, full, sems) = refs[:-3], refs[-3:]
    load_down(place_ref, downs, (len(downs) - 1) // 2, hidden, left, full, sems)
    cot = cot_ref[...]
    tiles = padded(hidden) // 128

    def step(i, carry):
        at = pl.multiple_of(i * 128, 128)
        out_ref[:, pl.ds(at, 128)] = nt_dot(cot, full[pl.ds(at, 128), :])
        return carry

    lax.fori_loop(0, tiles, step, 0)


def run_hidden_grad(place, cot, downs, left, hidden):
    rows, dim = cot.shape
    return pl.pallas_call(
        functools.partial(hidden_grad, hidden, left),
        name="hidden_grad",
        out_shape=jax.ShapeDtypeStruct((rows, padded(hidden)), F32),
        in_specs=[smem_spec(), vmem_spec()] + [any_spec()] * len(downs),
        out_specs=vmem_spec(),
        scratch_shapes=[pltpu.VMEM((padded(hidden), dim), BF16), down_semaphores(downs)],
        compiler_params=params(),
        cost_estimate=cost(4e9, 9e6),
    )(place, cot, *downs)


def layer_result(hidden, left, place_ref, mid_ref, keep_ref, *refs):
    downs, (out_ref, full, sems) = refs[:-3], refs[-3:]
    load_down(place_ref, downs, (len(downs) - 1) // 2, hidden, left, full, sems)
    wide = padded(hidden)

    def step(i, carry):
        at = pl.ds(pl.multiple_of(i * 256, 256), 256)
        out_ref[:, at] = (mid_ref[:, at] + nn_dot(keep_ref[:, :wide], full[:, at])).astype(BF16)
        return carry

    lax.fori_loop(0, out_ref.shape[1] // 256, step, 0)


def run_layer_result(place, middle, keep, downs, left, hidden):
    rows, dim = middle.shape
    return pl.pallas_call(
        functools.partial(layer_result, hidden, left),
        name="layer_result",
        out_shape=jax.ShapeDtypeStruct((rows, dim), BF16),
        in_specs=[smem_spec()] + [vmem_spec()] * 2 + [any_spec()] * len(downs),
        out_specs=vmem_spec(),
        scratch_shapes=[pltpu.VMEM((padded(hidden), dim), BF16), down_semaphores(downs)],
        compiler_params=params(),
        cost_estimate=cost(4e9, 9e6),
    )(place, middle, keep, *downs)


def feed_forward(
    count, hidden, heads_width, place_ref, x_ref, att_ref, cot_ref, gain_ref, gh_hbm, *refs
):
    out_own, in_own, mine, others = refs[0], refs[1], refs[2 : 2 + count], refs[2 + count : 2 + 2 * count]
    mid_ref, gmid_ref, send_hbm, keep_hbm, ga_ref = refs[2 + 2 * count : 7 + 2 * count]
    wo, wi, both, early, late, send_ref, keep_ref, gh_ref, sem_o, sem_i, sems = refs[7 + 2 * count :]
    fetch = pltpu.make_async_copy(gh_hbm, gh_ref, sems.at[0])
    send_out = pltpu.make_async_copy(send_ref, send_hbm, sems.at[1])
    keep_out = pltpu.make_async_copy(keep_ref, keep_hbm, sems.at[2])
    dim = x_ref.shape[1]
    wide_hidden = padded(hidden)
    nt_ref = send_ref.at[:, pl.ds(2 * hidden, dim)]
    gboth_ref = send_ref
    hid_ref = keep_ref
    gbr_ref = keep_ref.at[:, pl.ds(wide_hidden, dim)]
    att_all_ref = keep_ref.at[:, pl.ds(wide_hidden + dim, dim)]
    keep_ref[:, pl.ds(wide_hidden + 2 * dim, dim)] = cot_ref[...]
    copies_o = row_copies(place_ref, out_own, mine, others, 2 * hidden, wo, sem_o)
    copies_i = row_copies(place_ref, in_own, mine, others, 0, wi, sem_i)
    for copy in copies_o:
        copy.start()
    for copy in copies_i:
        copy.start()
    fetch.start()
    att = jnp.concatenate([att_ref[s] for s in range(att_ref.shape[0])], axis=1)
    att_all_ref[...] = att
    for copy in copies_o:
        copy.wait()

    def branch(i, carry):
        at = pl.ds(pl.multiple_of(i * 256, 256), 256)
        mid_ref[:, at] = x_ref[:, at].astype(F32) + nn_dot(att_all_ref[...], wo[:, at])
        return carry

    lax.fori_loop(0, dim // 256, branch, 0)
    middle = mid_ref[...]
    center = middle - jnp.mean(middle, axis=-1, keepdims=True)
    spread = jnp.mean(center * center, axis=-1, keepdims=True)
    scale = lax.rsqrt(spread + NORM_EPS)
    nt_ref[...] = (center * scale * gain_ref[...]).astype(BF16)
    for copy in copies_i:
        copy.wait()
    fetch.wait()
    wide = 2 * hidden // 128

    def expand(i, carry):
        at = pl.ds(pl.multiple_of(i * 256, 256), 256)
        both[:, at] = nn_dot(nt_ref[...], wi[:, at])
        return carry

    lax.fori_loop(0, wide // 2, expand, 0)
    if wide % 2:
        both[:, pl.ds(128 * (wide - 1), 128)] = nn_dot(nt_ref[...], wi[:, pl.ds(128 * (wide - 1), 128)])
    both[:, pl.ds(128 * wide, 128)] = jnp.zeros((both.shape[0], 128), F32)
    tiles = padded(hidden) // 128
    whole = hidden // 128
    lanes = lax.broadcasted_iota(jnp.int32, (both.shape[0], 128), 1)
    shift = hidden % 128

    def tile(i):
        return pl.ds(pl.multiple_of(i * 128, 128), 128)

    def gates(i):
        a = both[:, tile(i)]
        if shift:
            left = pltpu.roll(both[:, tile(whole + i)], 128 - shift, 1)
            right = pltpu.roll(both[:, tile(whole + i + 1)], 128 - shift, 1)
            b = jnp.where(lanes < 128 - shift, left, right)
        else:
            b = both[:, tile(whole + i)]
        gh = gh_ref[:, tile(i)]
        phi = 0.5 * (1.0 + lax.erf(a * (0.5**0.5)))
        gelu = a * phi
        slope = phi + a * ((0.5 / math.pi) ** 0.5 * jnp.exp(-0.5 * a * a))
        hid_ref[:, tile(i)] = (gelu * b).astype(BF16)
        return gh * b * slope, gh * gelu

    if shift:
        first_a, first_b = gates(0)
        gboth_ref[:, tile(0)] = first_a.astype(BF16)
        early[...] = pltpu.roll(first_b, shift, 1)
        late[...] = early[...]

        def inner(i, carry):
            ga, gb = gates(i)
            turned = pltpu.roll(gb, shift, 1)
            gboth_ref[:, tile(i)] = ga.astype(BF16)
            gboth_ref[:, tile(whole + i)] = jnp.where(lanes < shift, late[...], turned).astype(BF16)
            late[...] = turned
            return carry

        lax.fori_loop(1, tiles - 1, inner, 0)
        ga, gb = gates(tiles - 1)
        turned = pltpu.roll(gb, shift, 1)
        gboth_ref[:, tile(whole)] = jnp.where(lanes < shift, ga, early[...]).astype(BF16)
        gboth_ref[:, tile(2 * whole)] = jnp.where(lanes < shift, late[...], turned).astype(BF16)
    else:

        def inner(i, carry):
            ga, gb = gates(i)
            gboth_ref[:, tile(i)] = ga.astype(BF16)
            gboth_ref[:, tile(whole + i)] = gb.astype(BF16)
            return carry

        lax.fori_loop(0, tiles, inner, 0)

    send_out.start()

    def back(i, carry):
        at = pl.multiple_of(i * 128, 128)
        both[:, pl.ds(at, 128)] = nt_dot(gboth_ref[:, : 2 * hidden], wi[pl.ds(at, 128), :])
        return carry

    lax.fori_loop(0, dim // 128, back, 0)
    middle = mid_ref[...]
    center = middle - jnp.mean(middle, axis=-1, keepdims=True)
    spread = jnp.mean(center * center, axis=-1, keepdims=True)
    scale = lax.rsqrt(spread + NORM_EPS)
    normal = center * scale
    e = both[:, pl.ds(0, dim)] * gain_ref[...]
    pull = e - jnp.mean(e, axis=-1, keepdims=True) - normal * jnp.mean(e * normal, axis=-1, keepdims=True)
    gmid = cot_ref[...].astype(F32) + scale * pull
    gmid_ref[...] = gmid
    gbr_ref[...] = gmid.astype(BF16)
    keep_out.start()

    def spread_out(i, carry):
        at = pl.multiple_of(i * 128, 128)
        both[:, pl.ds(at, 128)] = nt_dot(gbr_ref[...], wo[pl.ds(at, 128), :])
        return carry

    lax.fori_loop(0, dim // 128, spread_out, 0)
    for s in range(att_ref.shape[0]):
        ga_ref[s] = both[:, s * heads_width : (s + 1) * heads_width].astype(BF16)
    send_out.wait()
    keep_out.wait()


def run_feed_forward(place, x, att, cot, gain, grad_hidden, w_out, w_in, mine, others, hidden):
    rows, dim = x.shape
    seq_count, _, heads_width = att.shape
    count = len(mine)
    return pl.pallas_call(
        functools.partial(feed_forward, count, hidden, heads_width),
        name="feed_forward",
        out_shape=(
            jax.ShapeDtypeStruct((rows, dim), F32),
            jax.ShapeDtypeStruct((rows, dim), F32),
            jax.ShapeDtypeStruct((rows, 2 * hidden + dim), BF16),
            jax.ShapeDtypeStruct((rows, padded(hidden) + 3 * dim), BF16),
            jax.ShapeDtypeStruct((seq_count, rows, heads_width), BF16),
        ),
        in_specs=[smem_spec()] + [vmem_spec()] * 4 + [any_spec()] * (3 + 2 * count),
        out_specs=[vmem_spec()] * 2 + [any_spec()] * 2 + [vmem_spec()],
        scratch_shapes=[
            pltpu.VMEM((dim, dim), BF16),
            pltpu.VMEM((dim, 2 * hidden), BF16),
            pltpu.VMEM((rows, 2 * hidden + 128), F32),
            pltpu.VMEM((rows, 128), F32),
            pltpu.VMEM((rows, 128), F32),
            pltpu.VMEM((rows, 2 * hidden + dim), BF16),
            pltpu.VMEM((rows, padded(hidden) + 3 * dim), BF16),
            pltpu.VMEM((rows, padded(hidden)), F32),
            pltpu.SemaphoreType.DMA((2 * count + 1,)),
            pltpu.SemaphoreType.DMA((2 * count + 1,)),
            pltpu.SemaphoreType.DMA((3,)),
        ],
        compiler_params=params(),
        cost_estimate=cost(16e9, 24e6),
    )(place, x, att, cot, gain, grad_hidden, w_out, w_in, *mine, *others)


ORDER = (0, 2, 1, 3)


def in_grad(hidden, wide, place_ref, send_ref, other_ref, a_ref, b_ref, c_ref, turned, picked):
    tokens = send_ref.shape[0]
    rows = turned.shape[0] // 4
    half, short = rows // 2, rows // 8

    @pl.when(pl.program_id(0) == 0)
    def _():
        turned[:, :tokens] = send_ref[:, 2 * hidden :].T
        turned[:, tokens:] = other_ref[:, 2 * hidden :].T
        core, z = place_ref[7], place_ref[8]
        for at, key in enumerate((2, 3, 1, 0)):
            for j, k in enumerate(ORDER):
                base = pl.multiple_of(place_ref[key] * rows + core * half + (z ^ k) * short, 16)
                to = at * half + j * short
                picked[to : to + short, :] = turned[pl.ds(base, short), :]

    at = pl.ds(pl.multiple_of(pl.program_id(0) * wide, 128), wide)
    right = jnp.concatenate([send_ref[:, at], other_ref[:, at]], axis=0)
    result = nn_dot(picked[...], right).astype(BF16)
    a_ref[0] = result[:half]
    a_ref[1] = result[half : 2 * half]
    b_ref[0] = result[2 * half : 3 * half]
    c_ref[0] = result[3 * half :]


def run_in_grad(place, send, other, hidden):
    tokens = send.shape[0]
    features = send.shape[1] - 2 * hidden
    columns = 2 * hidden
    half = features // 8
    wide = 896
    whole = pl.BlockSpec(send.shape, lambda i: (0, 0))
    return pl.pallas_call(
        functools.partial(in_grad, hidden, wide),
        name="in_grad",
        out_shape=tuple(jax.ShapeDtypeStruct((n, half, columns), BF16) for n in (2, 1, 1)),
        grid=(pl.cdiv(columns, wide),),
        in_specs=[smem_spec(), whole, whole],
        out_specs=[pl.BlockSpec((n, half, wide), lambda i: (0, 0, i)) for n in (2, 1, 1)],
        scratch_shapes=[
            pltpu.VMEM((features, 2 * tokens), BF16),
            pltpu.VMEM((features // 2, 2 * tokens), BF16),
        ],
        compiler_params=params(),
        cost_estimate=cost(2.0 * 2 * tokens * features * columns, 4 * tokens * columns + features * columns),
    )(place, send, other)


def rest_grad(hidden, place_ref, keep_ref, other_ref, a_ref, b_ref, c_ref, turned, picked):
    tokens = keep_ref.shape[0]
    wide = padded(hidden)
    dim = (keep_ref.shape[1] - wide) // 3
    half = dim // 2
    down_rows = hidden // 4
    short = dim // 32
    core, z = place_ref[7], place_ref[8]
    at = pl.program_id(0)

    @pl.when(at == 0)
    def _():
        turned[:wide, :tokens] = keep_ref[:, :wide].T
        turned[:wide, tokens:] = other_ref[:, :wide].T
        turned[wide:, :tokens] = keep_ref[:, wide + dim : wide + 2 * dim].T
        turned[wide:, tokens:] = other_ref[:, wide + dim : wide + 2 * dim].T
        for j, k in enumerate(ORDER):
            left = pl.ds(pl.multiple_of(wide + 2 * dim + core * half + (z ^ k) * 128, 128), 128)
            picked[:tokens, j * 128 : (j + 1) * 128] = keep_ref[:, left]
            picked[tokens:, j * 128 : (j + 1) * 128] = other_ref[:, left]
        picked[:tokens, half:] = keep_ref[:, wide : wide + dim]
        picked[tokens:, half:] = other_ref[:, wide : wide + dim]

    owner = place_ref[jnp.where(at < 2, at + 2, 3 - at)]
    base = pl.multiple_of(owner * down_rows, 16)
    down = nn_dot(turned[pl.ds(base, down_rows), :], picked[:, :half]).astype(BF16)
    left = []
    for k in ORDER:
        base = pl.multiple_of(wide + owner * 8 * short + core * 4 * short + (z ^ k) * short, 16)
        left.append(turned[pl.ds(base, short), :])
    out = nn_dot(jnp.concatenate(left, axis=0), picked[:, half:]).astype(BF16)
    first = dim // 128 * short

    def store(ref):
        for j in range(4):
            for t in range(dim // 128):
                ref[0, j, t * short : (t + 1) * short, :] = out[
                    j * short : (j + 1) * short, t * 128 : (t + 1) * 128
                ]
            ref[0, j, first:, :] = down[:, j * 128 : (j + 1) * 128]

    pl.when(at < 2)(lambda: store(a_ref))
    pl.when(at == 2)(lambda: store(b_ref))
    pl.when(at == 3)(lambda: store(c_ref))


def run_rest_grad(place, keep, other, hidden):
    tokens = keep.shape[0]
    wide = padded(hidden)
    dim = (keep.shape[1] - wide) // 3
    tall = dim // 128 * (dim // 32) + hidden // 4
    whole = pl.BlockSpec(keep.shape, lambda i: (0, 0))
    return pl.pallas_call(
        functools.partial(rest_grad, hidden),
        name="rest_grad",
        out_shape=tuple(jax.ShapeDtypeStruct((n, 4, tall, 128), BF16) for n in (2, 1, 1)),
        grid=(4,),
        in_specs=[smem_spec(), whole, whole],
        out_specs=[
            pl.BlockSpec((1, 4, tall, 128), lambda i: (jnp.minimum(i, 1), 0, 0, 0)),
            pl.BlockSpec((1, 4, tall, 128), lambda i: (0, 0, 0, 0)),
            pl.BlockSpec((1, 4, tall, 128), lambda i: (0, 0, 0, 0)),
        ],
        scratch_shapes=[
            pltpu.VMEM((wide + dim, 2 * tokens), BF16),
            pltpu.VMEM((2 * tokens, dim + dim // 2), BF16),
        ],
        compiler_params=params(),
        cost_estimate=cost(4e9, 10e6),
    )(place, keep, other)


def unpack_in(place_ref, *refs):
    pieces, w_ref, out_ref, sum_ref = refs[:4], refs[4], refs[5], refs[6]
    at = pl.program_id(0)
    for q, ref in enumerate(pieces):

        @pl.when(at // 2 == q)
        def _(ref=ref):
            value = ref[0].astype(F32)
            out_ref[...] = value
            sum_ref[...] = jnp.sum(value * w_ref[...].astype(F32), axis=1, keepdims=True)


def row_block(i, place_ref):
    order = jnp.where(i % 4 == 1, 2, jnp.where(i % 4 == 2, 1, i % 4))
    side = jnp.where(i < 4, place_ref[7], 1 - place_ref[7])
    return (side * 4 + (place_ref[8] ^ order), 0)


def run_unpack_in(place, pieces, weight):
    rows, columns = weight.shape
    short = rows // 8
    specs = [
        pl.BlockSpec((1, short, columns), lambda i, p, q=q: (jnp.clip(i - 2 * q, 0, 1), 0, 0))
        for q in range(4)
    ]
    block = pl.BlockSpec((short, columns), row_block)
    return pl.pallas_call(
        unpack_in,
        name="unpack_in",
        out_shape=(jax.ShapeDtypeStruct((rows, columns), F32), jax.ShapeDtypeStruct((rows, 1), F32)),
        grid_spec=pltpu.PrefetchScalarGridSpec(
            num_scalar_prefetch=1,
            grid=(8,),
            in_specs=specs + [block],
            out_specs=[block, pl.BlockSpec((short, 1), row_block)],
        ),
        compiler_params=params(),
        cost_estimate=cost(1e7, 11e6),
    )(place, *pieces, weight)


def sources(place_ref, pieces):
    core, z = place_ref[7], place_ref[8]
    for q, ref in enumerate(pieces):
        for at in range(2):
            yield ref.at[at], (core if q < 2 else 1 - core), z ^ ORDER[2 * (q % 2) + at]


def unpack_rest(place_ref, *refs):
    pieces, out_ref, down_ref = refs[:4], refs[4], refs[5]
    dim = out_ref.shape[1]
    short = dim // 32
    first = dim // 128 * short
    for ref, side, z in sources(place_ref, pieces):
        base = pl.multiple_of(side * 4 * short + z * short, 16)
        for t in range(dim // 128):
            out_ref[pl.ds(base, short), t * 128 : (t + 1) * 128] = ref[
                t * short : (t + 1) * short, :
            ].astype(F32)
        left = pl.multiple_of(side * (dim // 2) + z * 128, 128)
        down_ref[:, pl.ds(left, 128)] = ref[first:, :].astype(F32)


def run_unpack_rest(place, pieces, out_shape, down_shape):
    return pl.pallas_call(
        unpack_rest,
        name="unpack_rest",
        out_shape=(jax.ShapeDtypeStruct(out_shape, F32), jax.ShapeDtypeStruct(down_shape, F32)),
        in_specs=[smem_spec()] + [vmem_spec()] * 4,
        out_specs=[vmem_spec()] * 2,
        compiler_params=params(),
        cost_estimate=cost(1e7, 6e6),
    )(place, *pieces)


def unpack_qkv(place_ref, *refs):
    pieces, w_ref, out_ref, sum_ref = refs[:4], refs[4], refs[5], refs[6]
    width = pieces[0].shape[2] // 3
    dim = out_ref.shape[1] // 3
    total = jnp.zeros_like(sum_ref)
    for ref, side, z in sources(place_ref, pieces):
        for part in range(3):
            left = pl.multiple_of(part * dim + (z * 2 + side) * width, 128)
            value = ref[:, part * width : (part + 1) * width].astype(F32)
            out_ref[:, pl.ds(left, width)] = value
            weight = w_ref[:, pl.ds(left, width)].astype(F32)
            total = total + jnp.sum(value * weight, axis=1, keepdims=True)
    sum_ref[...] = total


def run_unpack_qkv(place, pieces, weight):
    return pl.pallas_call(
        unpack_qkv,
        name="unpack_qkv",
        out_shape=(
            jax.ShapeDtypeStruct(weight.shape, F32),
            jax.ShapeDtypeStruct((weight.shape[0], 1), F32),
        ),
        in_specs=[smem_spec()] + [vmem_spec()] * 5,
        out_specs=[vmem_spec()] * 2,
        compiler_params=params(),
        cost_estimate=cost(1e7, 7e6),
    )(place, *pieces, weight)


def input_grad(count, place_ref, x_ref, gmid_ref, gain_ref, g_ref, *refs):
    weights, (out_ref, full, grad, total, sems) = refs[:-5], refs[-5:]
    seq_count, _, width = g_ref.shape
    width //= 3
    dim = x_ref.shape[1]
    copies = row_copies(place_ref, weights[0], weights[1 : 1 + count], weights[1 + count :], 0, full, sems)
    for copy in copies:
        copy.start()
    grad[...] = jnp.concatenate(
        [g_ref[s][:, part * width : (part + 1) * width] for part in range(3) for s in range(seq_count)],
        axis=1,
    )
    for copy in copies:
        copy.wait()

    def step(i, carry):
        at = pl.multiple_of(i * 128, 128)
        total[:, pl.ds(at, 128)] = nt_dot(grad[...], full[pl.ds(at, 128), :])
        return carry

    lax.fori_loop(0, dim // 128, step, 0)
    x = x_ref[...].astype(F32)
    center = x - jnp.mean(x, axis=-1, keepdims=True)
    spread = jnp.mean(center * center, axis=-1, keepdims=True)
    scale = lax.rsqrt(spread + NORM_EPS)
    normal = center * scale
    e = total[...] * gain_ref[...]
    pull = e - jnp.mean(e, axis=-1, keepdims=True) - normal * jnp.mean(e * normal, axis=-1, keepdims=True)
    out_ref[...] = (gmid_ref[...] + scale * pull).astype(BF16)


def run_input_grad(place, x, gmid, gain, grads, weights, count):
    rows, dim = x.shape
    columns = weights[0].shape[1]
    return pl.pallas_call(
        functools.partial(input_grad, count),
        name="input_grad",
        out_shape=jax.ShapeDtypeStruct((rows, dim), BF16),
        in_specs=[smem_spec()] + [vmem_spec()] * 4 + [any_spec()] * len(weights),
        out_specs=vmem_spec(),
        scratch_shapes=[
            pltpu.VMEM((dim, columns), BF16),
            pltpu.VMEM((rows, columns), BF16),
            pltpu.VMEM((rows, dim), F32),
            pltpu.SemaphoreType.DMA((2 * count + 1,)),
        ],
        compiler_params=params(),
        cost_estimate=cost(4e9, 10e6),
    )(place, x, gmid, gain, grads, *weights)


def sequence_layout(lengths, order, group):
    ends = jnp.cumsum(lengths)
    starts = ends - lengths
    index = jnp.arange(group, dtype=jnp.int32)
    passed = index[:, None] >= ends[None, :]
    start = jnp.sum(jnp.where(passed, lengths[None, :], 0), axis=1).astype(jnp.int32)
    inside = jnp.logical_and(index[:, None] >= starts[None, :], jnp.logical_not(passed))
    end = jnp.sum(jnp.where(inside, ends[None, :], 0), axis=1).astype(jnp.int32)
    places = index - start
    half = HD // 2
    speeds = jnp.power(F32(ROPE_BASE), -2.0 * jnp.arange(half, dtype=F32) / HD)
    angles = speeds[:, None] * places.astype(F32)[None, :]
    keys = (start[::WIDE] // BLOCK, (end[WIDE - 1 :: WIDE] + BLOCK - 1) // BLOCK)
    queries = (start[::BLOCK] // WIDE, (end[BLOCK - 1 :: BLOCK] + WIDE - 1) // WIDE)
    return (keys, queries, order[None, :], start[None, :], end[None, :], jnp.cos(angles), jnp.sin(angles))


def local(tokens, seq_lengths, seq_order, norm_one, w_qkv, w_out, norm_two, w_in, w_down, cotangent):
    seq_count = lax.axis_size("seq")
    fsdp_count = lax.axis_size("fsdp")
    levels = fsdp_count.bit_length() - 1
    count = fsdp_count - 1
    seq_at = lax.axis_index("seq")
    fsdp_at = lax.axis_index("fsdp")
    core = seq_at % 2
    x = tokens[0]
    cot = cotangent[0]
    rows, dim = x.shape
    group = rows * seq_count
    heads = dim // HD // seq_count
    width = heads * HD
    hidden = w_in.shape[1] // 2
    def gather(piece, *others):
        return plane_gather(piece, seq_count, fsdp_count, *others)

    swap = functools.partial(core_swap, seq_count=seq_count)

    keys = [jnp.array([plane_mask(c, key, levels) for key in range(1, fsdp_count)], jnp.int32) for c in (0, 1)]
    mine = fsdp_at ^ jnp.where(core == 0, keys[0], keys[1])
    other = fsdp_at ^ jnp.where(core == 0, keys[1], keys[0])
    place = jnp.stack([fsdp_at, *mine, *other, core, seq_at // 2]).astype(jnp.int32)

    regular = fsdp_count == 4 and seq_count == 8 and w_down.shape[0] % 16 == 0 and dim == 1024

    x_all = lax.all_gather(x, "seq", axis=0, tiled=False)
    own_heads = lax.dynamic_slice_in_dim(w_qkv.reshape(w_qkv.shape[0], 3, dim), seq_at * width, width, 2)
    own_heads = own_heads.reshape(w_qkv.shape[0], 3 * width)
    gains = jnp.stack([norm_one, norm_two])
    if regular:
        extra = jnp.pad(gains, ((0, 14), (0, 3 * width - gains.shape[1])))
        own_heads = jnp.concatenate([own_heads, extra], axis=0)
        head_pieces = [own_heads] + [
            lax.ppermute(own_heads, "fsdp", [(f, f ^ mask) for f in range(4)]) for mask in (1, 2, 3)
        ]
    else:
        head_pieces = [
            lax.all_gather(own_heads, "fsdp", axis=0, tiled=True),
            lax.all_gather(gains, "fsdp", axis=1, tiled=True).astype(F32),
        ]
    piece = run_pack_pieces(place, w_in, w_out, w_down, regular)
    mine = gather(piece)
    left = 2 * hidden + dim

    layout = sequence_layout(seq_lengths[0], seq_order[0], group)
    gains, normed, packed, att, out_t, lse = run_attention_forward(place, x_all, head_pieces, layout, heads)
    gain_one, gain_two = gains[:1], gains[1:]
    qkv_piece = lax.dynamic_slice_in_dim(w_qkv, core * (w_qkv.shape[0] // 2), w_qkv.shape[0] // 2, 0)
    att_done = lax.all_to_all(att, "seq", split_axis=0, concat_axis=0, tiled=True)
    others = [swap(mine[0])] + [swap(after(p, att, *([att_done] if i else []))) for i, p in enumerate(mine[1:])]
    if regular:
        downs = [w_down] + mine + others
    else:
        downs = [lax.all_gather(w_down, "fsdp", axis=0, tiled=True)]
    att = att_done
    qkv_mine = gather(after(qkv_piece, att))
    grad_hidden = run_hidden_grad(place, cot, downs, left, hidden)
    middle, gmid, send, keep, gatt = run_feed_forward(
        place, x, after(att, qkv_mine[0]), cot, gain_two, grad_hidden, w_out, w_in, mine, others, hidden
    )
    send = after(send, *qkv_mine)
    qkvs = [w_qkv] + qkv_mine + [swap(p) for p in qkv_mine]
    dout = lax.all_to_all(gatt, "seq", split_axis=0, concat_axis=0, tiled=True)
    reduce = functools.partial(plane_reduce, seq_count=seq_count, fsdp_count=fsdp_count)
    send_other, keep_other = swap(send), swap(keep)
    wide = padded(hidden)
    if regular:
        short = w_in.shape[0] // 8
        in_a, in_b, in_c = run_in_grad(place, send, send_other, hidden)
        rest_a, rest_b, rest_c = run_rest_grad(place, keep, after(keep_other, in_b), hidden)
        dout = after(dout, in_b, rest_b)
        in_a = plane_swap(in_a, 1, seq_count, fsdp_count)
        rest_a = plane_swap(rest_a, 1, seq_count, fsdp_count)
    else:
        rest_a = keep_other

    grads = run_attention_backward(dout, packed, out_t, lse, layout, heads)
    layer_out = run_layer_result(place, middle, after(keep, grads), downs, left, hidden)
    grad_rows = lax.all_to_all(grads, "seq", split_axis=0, concat_axis=0, tiled=True)
    gw_heads = run_qkv_weight_grad(place, normed, after(grads, rest_a), regular)
    grad_tokens = run_input_grad(place, x, gmid, gain_one, grad_rows, qkvs, count)
    each = w_qkv.shape[0]
    if regular:
        in_parts = [p.reshape(4, short, 2 * hidden) for p in reduce(in_a, in_b, in_c)]
        in_parts[2] = after(in_parts[2], grad_rows, layer_out)
        rest_parts = reduce(rest_a, rest_b, rest_c)
        in_block = line_reduce(in_parts, seq_count)
        rest_block = line_reduce(rest_parts, seq_count)
        in_pieces = line_gather(after(in_block, grad_tokens), seq_count)
        rest_pieces = line_gather(rest_block, seq_count)
        qkv_a, qkv_b, qkv_c = gw_heads
        qkv_a = plane_swap(qkv_a, 1, seq_count, fsdp_count)
        qkv_pieces = line_gather(added(*reduce(qkv_a, qkv_b, qkv_c)), seq_count)
        gw_qkv, sum_qkv = run_unpack_qkv(place, qkv_pieces, w_qkv)
        gw_in, sum_in = run_unpack_in(place, in_pieces, w_in)
        gw_out, gw_down = run_unpack_rest(place, rest_pieces, w_out.shape, w_down.shape)
        sum_qkv = sum_qkv[:, 0]
        sum_in = sum_in[:, 0]
    else:

        def total(left_rows, right_rows):
            full = lax.dot_general(
                left_rows, right_rows, (((0,), (0,)), ((), ())), preferred_element_type=F32
            )
            return lax.psum(lax.psum_scatter(full, "fsdp", scatter_dimension=0, tiled=True), "seq")

        gw_in = total(send[:, 2 * hidden :], send[:, : 2 * hidden])
        gw_down = total(keep[:, :hidden], cot)
        gw_out = total(keep[:, wide + dim : wide + 2 * dim], keep[:, wide : wide + dim])
        sum_in = jnp.sum(gw_in * w_in.astype(F32), axis=1)
        gw_heads = lax.all_to_all(gw_heads[0].reshape(fsdp_count, each, -1), "fsdp", 0, 0, tiled=True)
        gw_heads = jnp.sum(gw_heads.astype(F32), axis=0).astype(BF16)
        gw_qkv = lax.all_gather(gw_heads, "seq", axis=0, tiled=False).reshape(seq_count, each, 3, width)
        gw_qkv = gw_qkv.transpose(1, 2, 0, 3).reshape(each, 3 * dim).astype(F32)
        sum_qkv = jnp.sum(gw_qkv * w_qkv.astype(F32), axis=1)

    grad_one = sum_qkv / norm_one.astype(F32)
    grad_two = sum_in / norm_two.astype(F32)
    return (layer_out[None], grad_tokens[None], grad_one, gw_qkv, gw_out, grad_two, gw_in, gw_down)


def solution(mesh):
    tokens = P("fsdp", "seq", None)
    rows = P("fsdp", None)
    return jax.shard_map(
        local,
        mesh=mesh,
        in_specs=(tokens, rows, rows, P("fsdp"), rows, rows, P("fsdp"), rows, rows, tokens),
        out_specs=(tokens, tokens, P("fsdp"), rows, rows, P("fsdp"), rows, rows),
        check_vma=False,
    )
```

time: 532 us -> 410 us (0.77)
  blocking collectives: 63.9 us -> 0 us
  waiting for transfers between devices: 150 us -> 126 us
  local copies, waits for them, and re-layouts: 27.1 us -> 6.8 us
  starting transfers between devices: 75.4 us -> 59.6 us
  Pallas kernels: 160 us -> 171 us
  other arithmetic: 33.5 us -> 24.4 us
    ppermute x14 -> x10, waiting for transfers between devices: 103 us -> 39.1 us  [line_swap(): lax.ppermute(value, 'seq', [(i, i ^ 2 << level) for i in range(seq_count)])]
    all_gather x2 -> x0, blocking collectives: 63.9 us -> none  [the longest x1 45.4 us: local(): lax.all_gather(own_heads.reshape(w_qkv.shape[0], 3 * width), 'fsdp', axis...]
    pallas_call x5 -> x8, Pallas kernels: 37.2 us -> 57.9 us  [the longest x1 11.8 us: run_hidden_grad(): pl.pallas_call(functools.partial(hidden_grad, hidden, left), name='hidden...]
    all_to_all x1, waiting for transfers between devices: 0.01 us -> 19.9 us  [local(): lax.all_to_all(grads, 'seq', split_axis=0, concat_axis=0, tiled=True)]
    all_gather x1, waiting for transfers between devices: 0.01 us -> 10.2 us  [local(): x_all = lax.all_gather(x, 'seq', axis=0, tiled=False)]
    ppermute x24 -> x12, waiting for transfers between devices: 41 us -> 49.3 us  [plane_swap(): return lax.ppermute(value, AXES, pairs)]
    ppermute x24 -> x12, starting transfers between devices: 18.6 us -> 10.4 us  [plane_swap(): return lax.ppermute(value, AXES, pairs)]
    select_n x13 -> x2, other arithmetic: 8.84 us -> 1.05 us  [the longest x1 0.52 us: sequence_layout(): keys = (start[::WIDE] // BLOCK, (end[WIDE - 1::WIDE] + BLOCK - 1) // BLOCK)]
  transfers between devices with their start and end apart: 64 -> 43, of which waited for: 22 -> 13; matrix products, arithmetic and copies ran while one was open for 10% -> 6% of each run, Pallas kernels for 24% -> 40%
where the time goes in v2:
time: 410 us; the launch traced here: 403 us
  Pallas kernels  171 us (42%)
  waiting for transfers between devices  126 us (31%)
  starting transfers between devices  59.6 us (15%)
  other arithmetic  24.4 us (6%)
  between operations  14.6 us (4%)
  local copies, waits for them, and re-layouts  6.8 us (2%)
    ppermute x12, waiting for transfers between devices, plane_swap(): return lax.ppermute(value, AXES, pairs)  49.3 us
    ppermute x10, waiting for transfers between devices, line_swap(): lax.ppermute(value, 'seq', [(i, i ^ 2 << level) for i in range(seq_count)])  39.1 us
    pallas_call x1, Pallas kernels, run_attention_backward(): pl.pallas_call(functools.partial(attention_backward, seq_count, heads, gr...  34 us
    pallas_call x1, Pallas kernels, run_attention_forward(): pl.pallas_call(functools.partial(attention_forward, seq_count, heads, gro...  32.2 us
    pallas_call x1, Pallas kernels, run_feed_forward(): pl.pallas_call(functools.partial(feed_forward, count, hidden, heads_width...  28.7 us
    ppermute x14, starting transfers between devices, core_swap(): return lax.ppermute(value, 'seq', [(i, i ^ 1) for i in range(seq_count)])  26.1 us
    all_to_all x1, waiting for transfers between devices, local(): lax.all_to_all(grads, 'seq', split_axis=0, concat_axis=0, tiled=True)  19.9 us
    convert_element_type x9, other arithmetic, added(): return sum((v.astype(F32) for v in values)).astype(BF16)  13.9 us
  transfers between devices with their start and end apart: 43, of which 13 were waited for; matrix products, arithmetic and copies ran while one was open for 6% of the time, Pallas kernels for 40%

profile of v2, /device:TPU:1, one launch (start us, length us, event | category | flops | bytes accessed | tf_op | source)
XLA Modules:
  0.0 402.6 jit_solution(9288556561166573650)
XLA Ops:
  21.8 25.1 %collective-permute-done.4.refs_1_.refs_2_ = bf16[128,9344]{1,0:T(8,128)(2,1)} collective-permute-done((bf16[128,9344]{1,0:T(8,128)(2,1)}, bf16[128,9344]{1,0:T(8,128)(2,1)}, u32[]{:S(2)}, u32[]{:S(2)}) %collective-permute-start.4) | collective-permute-done | bytes 2392096 | tf_op jit(solution)/shard_map/ppermute | solution.py:46
  49.1 10.2 %all-gather.2.cloned.1.call-done.x_hbm = bf16[8,256,1024]{2,1,0:T(8,128)(2,1)} async-done(((bf16[1,256,1024]{2,1,0:T(8,128)(2,1)}), bf16[8,256,1024]{2,1,0:T(8,128)(2,1)}) %all-gather.2.cloned.1.call-update) | async-done | bytes 4194320 | tf_op jit(solution)/shard_map/all_gather | solution.py:1119
  59.3 32.2 %attention_forward.1 = (f32[2,1024]{1,0:T(2,128)}, bf16[8,256,1024]{2,1,0:T(8,128)(2,1)}, bf16[384,2048]{1,0:T(8,128)(2,1)}, bf16[8,256,128]{2,1,0:T(8,128)(2,1)...) custom-call(s32[4]{0:T(128)} %get-tuple-element.97.low_ref, s32[4]{0:T(128)} %get-tuple-element.96.high_ref, s32[9]{0:T(128)} %stack.51.place_ref, ...), custom_call_target="tpu_custom_call" | custom-call | flops 24000000000 | bytes 20000000 | tf_op jit(solution)/shard_map/attention_forward/pallas_call | solution.py:347
  95.8 7.6 %collective-permute-done.6.refs_3_.refs_4_ = bf16[128,9344]{1,0:T(8,128)(2,1)} collective-permute-done((bf16[128,9344]{1,0:T(8,128)(2,1)}, bf16[128,9344]{1,0:T(8,128)(2,1)}, u32[]{:S(2)}, u32[]{:S(2)}) %collective-permute-start.6) | collective-permute-done | bytes 2392096 | tf_op jit(solution)/shard_map/ppermute | solution.py:46
  103.4 6.3 %all-to-all-done.att_ref = bf16[8,256,128]{2,1,0:T(8,128)(2,1)S(1)} async-done(((bf16[8,256,128]{2,1,0:T(8,128)(2,1)}), bf16[8,256,128]{2,1,0:T(8,128)(2,1)S(1)}, u32[]{:S(2)}, u32[]{:S(2)}) %all-to-all-start) | async-done | bytes 524320 | tf_op jit(solution)/shard_map/all_to_all | solution.py:1142
  111.4 10.6 %collective-permute-done.3.refs_1_ = bf16[128,3072]{1,0:T(8,128)(2,1)} collective-permute-done((bf16[128,3072]{1,0:T(8,128)(2,1)S(1)}, bf16[128,3072]{1,0:T(8,128)(2,1)}, u32[]{:S(2)}, u32[]{:S(2)}) %collective-permute-start.3) | collective-permute-done | bytes 786464 | tf_op jit(solution)/shard_map/ppermute | solution.py:46
  123.5 11.8 %hidden_grad.1.gh_hbm = f32[256,2688]{1,0:T(8,128)} custom-call(s32[9]{0:T(128)} %stack.51.place_ref, bf16[256,1024]{1,0:T(8,128)(2,1)} %bitcast.78, bf16[656,1024]{1,0:T(8,128)(2,1)} %refs_0_.6, bf16[128,9344]{1,0:T(8,128)(2,1)} %collective-permute-done.4.refs_1_.refs_2_, bf16[128,9344]{1,0:T(8,128)(2,1)} %collective-permute-done.5.refs_2_.refs_3_, ...), custom_call_target="tpu_custom_call" | custom-call | flops 4000000000 | bytes 9000000 | tf_op jit(solution)/shard_map/hidden_grad/pallas_call | solution.py:585
  135.3 28.7 %feed_forward.1 = (f32[256,1024]{1,0:T(8,128)}, f32[256,1024]{1,0:T(8,128)}, bf16[256,6272]{1,0:T(8,128)(2,1)}, bf16[256,5760]{1,0:T(8,128)(2,1)}, bf16[8,256,128]{2,1,0:T(8,128)(2,1)}) custom-call(s32[9]{0:T(128)} %stack.51.place_ref, bf16[256,1024]{1,0:T(8,128)(2,1)} %bitcast.81, bf16[8,256,128]{2,1,0:T(8,128)(2,1)} %copy-done.12, ...), custom_call_target="tpu_custom_call" | custom-call | flops 16000000000 | bytes 24000000 | tf_op jit(solution)/shard_map/feed_forward/pallas_call | solution.py:766
  171.5 9.0 %in_grad.1 = (bf16[2,128,5248]{2,1,0:T(8,128)(2,1)}, bf16[1,128,5248]{2,1,0:T(8,128)(2,1)}, bf16[1,128,5248]{2,1,0:T(8,128)(2,1)}) custom-call(s32[9]{0:T(128)} %stack.51.place_ref, bf16[256,6272]{1,0:T(8,128)(2,1)} %get-tuple-element.59.send_ref, bf16[256,6272]{1,0:T(8,128)(2,1)} %collective-permute-done.12.other_ref), custom_call_target="tpu_custom_call" | custom-call | flops 5502926848 | bytes 10747904 | tf_op jit(solution)/shard_map/in_grad/pallas_call | solution.py:831
  180.5 8.8 %rest_grad.1 = (bf16[2,4,912,128]{3,2,1,0:T(8,128)(2,1)}, bf16[1,4,912,128]{3,2,1,0:T(8,128)(2,1)}, bf16[1,4,912,128]{3,2,1,0:T(8,128)(2,1)}) custom-call(s32[9]{0:T(128)} %stack.51.place_ref, bf16[256,5760]{1,0:T(8,128)(2,1)} %get-tuple-element.67.keep_ref, bf16[256,5760]{1,0:T(8,128)(2,1)} %collective-permute-done.13.other_ref), custom_call_target="tpu_custom_call" | custom-call | flops 4000000000 | bytes 10000000 | tf_op jit(solution)/shard_map/rest_grad/pallas_call | solution.py:899
  190.8 34.0 %attention_backward.1.grad_ref = bf16[8,256,384]{2,1,0:T(8,128)(2,1)} custom-call(s32[8]{0:T(128)} %get-tuple-element.95.low_ref, s32[8]{0:T(128)} %get-tuple-element.94.high_ref, bf16[8,256,128]{2,1,0:T(8,128)(2,1)} %copy-done.13, bf16[384,2048]{1,0:T(8,128)(2,1)} %get-tuple-element.64.packed_ref, f32[128,2048]{1,0:T(8,128)} %get-tuple-element.65.out_ref, ...), custom_call_target="tpu_custom_call" | custom-call | flops 30000001024 | bytes 10000000 | tf_op jit(solution)/shard_map/attention_backward/pallas_call | solution.py:486
  224.7 5.7 %all-to-all-start.2 = ((bf16[8,256,384]{2,1,0:T(8,128)(2,1)}), bf16[8,256,384]{2,1,0:T(8,128)(2,1)}, u32[]{:S(2)}, u32[]{:S(2)}) async-start(bf16[8,256,384]{2,1,0:T(8,128)(2,1)} %attention_backward.1.grad_ref), calls=%async_computation.2 | async-start | bytes 3145728 | tf_op jit(solution)/shard_map/all_to_all | solution.py:1172
  230.4 8.1 %layer_result.1 = bf16[256,1024]{1,0:T(8,128)(2,1)} custom-call(s32[9]{0:T(128)} %stack.51.place_ref, f32[256,1024]{1,0:T(8,128)} %get-tuple-element.54.mid_ref, bf16[256,5760]{1,0:T(8,128)(2,1)} %get-tuple-element.67.keep_ref, bf16[656,1024]{1,0:T(8,128)(2,1)} %refs_0_.6, bf16[128,9344]{1,0:T(8,128)(2,1)} %collective-permute-done.4.refs_1_.refs_2_, ...), custom_call_target="tpu_custom_call" | custom-call | flops 4000000000 | bytes 9000000 | tf_op jit(solution)/shard_map/layer_result/pallas_call | solution.py:612
  247.6 19.9 %all-to-all-done.2.g_ref = bf16[8,256,384]{2,1,0:T(8,128)(2,1)} async-done(((bf16[8,256,384]{2,1,0:T(8,128)(2,1)}), bf16[8,256,384]{2,1,0:T(8,128)(2,1)}, u32[]{:S(2)}, u32[]{:S(2)}) %all-to-all-start.2) | async-done | bytes 1572896 | tf_op jit(solution)/shard_map/all_to_all | solution.py:1172
  269.6 7.4 %qkv_weight_grad.1 = (bf16[2,256,384]{2,1,0:T(8,128)(2,1)}, bf16[1,256,384]{2,1,0:T(8,128)(2,1)}, bf16[1,256,384]{2,1,0:T(8,128)(2,1)}) custom-call(s32[9]{0:T(128)} %stack.51.place_ref, bf16[8,256,1024]{2,1,0:T(8,128)(2,1)} %get-tuple-element.69.normed_ref, bf16[8,256,384]{2,1,0:T(8,128)(2,1)} %attention_backward.1.grad_ref), custom_call_target="tpu_custom_call" | custom-call | flops 3000000000 | bytes 6000000 | tf_op jit(solution)/shard_map/qkv_weight_grad/pallas_call | solution.py:535
  291.2 10.8 %input_grad.1 = bf16[256,1024]{1,0:T(8,128)(2,1)} custom-call(s32[9]{0:T(128)} %stack.51.place_ref, bf16[256,1024]{1,0:T(8,128)(2,1)} %bitcast.82, f32[256,1024]{1,0:T(8,128)} %get-tuple-element.68.gmid_ref, f32[1,1024]{1,0:T(1,128)} %get-tuple-element.90.gain_ref, bf16[8,256,384]{2,1,0:T(8,128)(2,1)} %all-to-all-done.2.g_ref, bf16[256,3072]{1,0:T(8,128)(2,1)} %refs_4_.2, ...), custom_call_target="tpu_custom_call" | custom-call | flops 4000000000 | bytes 10000000 | tf_op jit(solution)/shard_map/input_grad/pallas_call | solution.py:1058
  310.2 10.3 %collective-permute-done.25 = bf16[2,912,128]{2,1,0:T(8,128)(2,1)S(1)} collective-permute-done((bf16[2,912,128]{2,1,0:T(8,128)(2,1)S(1)}, bf16[2,912,128]{2,1,0:T(8,128)(2,1)S(1)}, u32[]{:S(2)}, u32[]{:S(2)}) %collective-permute-start.25) | collective-permute-done | bytes 466976 | tf_op jit(solution)/shard_map/ppermute | solution.py:72
  322.6 18.4 %collective-permute-done.26 = bf16[912,128]{1,0:T(8,128)(2,1)S(1)} collective-permute-done((bf16[912,128]{1,0:T(8,128)(2,1)S(1)}, bf16[912,128]{1,0:T(8,128)(2,1)S(1)}, u32[]{:S(2)}, u32[]{:S(2)}) %collective-permute-start.26) | collective-permute-done | bytes 233504 | tf_op jit(solution)/shard_map/ppermute | solution.py:72
  344.0 8.5 %collective-permute-done.27 = bf16[912,128]{1,0:T(8,128)(2,1)S(1)} collective-permute-done((bf16[912,128]{1,0:T(8,128)(2,1)S(1)}, bf16[912,128]{1,0:T(8,128)(2,1)S(1)}, u32[]{:S(2)}, u32[]{:S(2)}) %collective-permute-start.27) | collective-permute-done | bytes 233504 | tf_op jit(solution)/shard_map/ppermute | solution.py:72
  356.1 4.9 %collective-permute-start.38 = (bf16[2,32,5248]{2,1,0:T(8,128)(2,1)S(1)}, bf16[2,32,5248]{2,1,0:T(8,128)(2,1)S(1)}, u32[]{:S(2)}, u32[]{:S(2)}) collective-permute-start(bf16[2,32,5248]{2,1,0:T(8,128)(2,1)S(1)} %collective-permute-done.36.refs_1_), channel_id=1, source_target_pairs={{0,4},{4,0},{8,12},{12,8},{16,20},{20,16},{24,28},{28,24},{1,5},{5... | collective-permute-start | bytes 2015240 | tf_op jit(solution)/shard_map/ppermute | solution.py:24
  361.0 8.3 %collective-permute-start.23 = (bf16[2,256,384]{2,1,0:T(8,128)(2,1)S(1)}, bf16[2,256,384]{2,1,0:T(8,128)(2,1)}, u32[]{:S(2)}, u32[]{:S(2)}) collective-permute-start(bf16[2,256,384]{2,1,0:T(8,128)(2,1)S(1)} %collective-permute-done.21.refs_1_), channel_id=1, source_target_pairs={{0,4},{4,0},{8,12},{12,8},{16,20},{20,16},{24,28},{28,24},{1,5},{5... | collective-permute-start | bytes 1179656 | tf_op jit(solution)/shard_map/ppermute | solution.py:24
  369.4 5.0 %collective-permute-start.30 = (bf16[2,912,128]{2,1,0:T(8,128)(2,1)}, bf16[2,912,128]{2,1,0:T(8,128)(2,1)}, u32[]{:S(2)}, u32[]{:S(2)}) collective-permute-start(bf16[2,912,128]{2,1,0:T(8,128)(2,1)} %collective-permute-done.28.refs_1_), channel_id=1, source_target_pairs={{0,4},{4,0},{8,12},{12,8},{16,20},{20,16},{24,28},{28,24},{1,5},{5... | collective-permute-start | bytes 1400840 | tf_op jit(solution)/shard_map/ppermute | solution.py:24
  374.4 4.4 %unpack_qkv.1 = (f32[256,3072]{1,0:T(8,128)}, f32[256,1]{1,0:T(8,128)}) custom-call(s32[9]{0:T(128)} %stack.51.place_ref, bf16[2,256,384]{2,1,0:T(8,128)(2,1)} %copy-done.4, bf16[2,256,384]{2,1,0:T(8,128)(2,1)} %copy-done.16, bf16[2,256,384]{2,1,0:T(8,128)(2,1)} %copy-done.17, bf16[2,256,384]{2,1,0:T(8,128)(2,1)} %collective-permute-done.23.refs_3_, ...), custom_call_target="tpu_custom_call" | custom-call | flops 10000000 | bytes 7000000 | tf_op jit(solution)/shard_map/unpack_qkv/pallas_call | solution.py:1010
  385.8 8.4 %unpack_in.1 = (f32[256,5248]{1,0:T(8,128)}, f32[256,1]{1,0:T(8,128)}) custom-call(s32[9]{0:T(128)} %stack.51.place_ref, bf16[2,32,5248]{2,1,0:T(8,128)(2,1)} %copy-done.2, bf16[2,32,5248]{2,1,0:T(8,128)(2,1)} %copy-done.9, bf16[2,32,5248]{2,1,0:T(8,128)(2,1)} %copy-done.10, bf16[2,32,5248]{2,1,0:T(8,128)(2,1)} %copy-done.11, bf16[256,5248]{1,0:T(8,128)(2,1)} %refs_4_.3), custom_call_target="tpu_custom_call" | custom-call | flops 10000000 | bytes 11000000 | tf_op jit(solution)/shard_map/unpack_in/pallas_call | solution.py:945
  (183 shorter events, 83.8 us)
Async XLA Ops:
  7.2 52.1 %all-gather.2.cloned.1.call-start = ((), (), s32[]{:S(2)}) async-start(), calls=%async_computation.3 | async-start | bytes 4718592 | tf_op jit(solution)/shard_map/all_gather | solution.py:1119
  13.1 33.8 %collective-permute-start.4 = (bf16[128,9344]{1,0:T(8,128)(2,1)}, bf16[128,9344]{1,0:T(8,128)(2,1)}, u32[]{:S(2)}, u32[]{:S(2)}) collective-permute-start(bf16[128,9344]{1,0:T(8,128)(2,1)} %pack_pieces.1), channel_id=1, source_target_pairs={{0,1},{1,0},{2,3},{3,2},{4,6},{5,7},{6,4},{7,5},{8,9},{9,8},{10,11... | collective-permute-start | bytes 7176200 | tf_op jit(solution)/shard_map/ppermute | solution.py:46
  16.2 32.1 %collective-permute-start = (bf16[272,384]{1,0:T(8,128)(2,1)S(1)}, bf16[272,384]{1,0:T(8,128)(2,1)S(1)}, u32[]{:S(2)}, u32[]{:S(2)}) collective-permute-start(bf16[272,384]{1,0:T(8,128)(2,1)S(1)} %pad_maximum_fusion.3.refs_0_), channel_id=1, source_target_pairs={{0,1},{1,0},{2,3},{3,2},{4,5},{5,4},{6,7},{7,6},{8,9},{9,8},{10,11... | collective-permute-start | bytes 626696 | tf_op jit(solution)/shard_map/ppermute | solution.py:1127
  17.5 31.6 %collective-permute-start.1 = (bf16[272,384]{1,0:T(8,128)(2,1)S(1)}, bf16[272,384]{1,0:T(8,128)(2,1)S(1)}, u32[]{:S(2)}, u32[]{:S(2)}) collective-permute-start(bf16[272,384]{1,0:T(8,128)(2,1)S(1)} %pad_maximum_fusion.3.refs_0_), channel_id=1, source_target_pairs={{0,2},{1,3},{2,0},{3,1},{4,6},{5,7},{6,4},{7,5},{8,10},{9,11},{10,... | collective-permute-start | bytes 626696 | tf_op jit(solution)/shard_map/ppermute | solution.py:1127
  17.7 31.4 %collective-permute-start.2 = (bf16[272,384]{1,0:T(8,128)(2,1)S(1)}, bf16[272,384]{1,0:T(8,128)(2,1)S(1)}, u32[]{:S(2)}, u32[]{:S(2)}) collective-permute-start(bf16[272,384]{1,0:T(8,128)(2,1)S(1)} %pad_maximum_fusion.3.refs_0_), channel_id=1, source_target_pairs={{0,3},{1,2},{2,1},{3,0},{4,7},{5,6},{6,5},{7,4},{8,11},{9,10},{10,... | collective-permute-start | bytes 626696 | tf_op jit(solution)/shard_map/ppermute | solution.py:1127
  46.9 48.7 %collective-permute-start.5 = (bf16[128,9344]{1,0:T(8,128)(2,1)}, bf16[128,9344]{1,0:T(8,128)(2,1)}, u32[]{:S(2)}, u32[]{:S(2)}) collective-permute-start(bf16[128,9344]{1,0:T(8,128)(2,1)} %pack_pieces.1), channel_id=1, source_target_pairs={{0,2},{1,3},{2,0},{3,1},{4,5},{5,4},{6,7},{7,6},{8,10},{9,11},{10,... | collective-permute-start | bytes 7176200 | tf_op jit(solution)/shard_map/ppermute | solution.py:46
  48.3 55.1 %collective-permute-start.6 = (bf16[128,9344]{1,0:T(8,128)(2,1)}, bf16[128,9344]{1,0:T(8,128)(2,1)}, u32[]{:S(2)}, u32[]{:S(2)}) collective-permute-start(bf16[128,9344]{1,0:T(8,128)(2,1)} %collective-permute-done.4.refs_1_.refs_2_), channel_id=1, source_target_pairs={{0,2},{1,3},{2,0},{3,1},{4,5},{5,4},{6,7},{7,6},{8,10},{9,11},{10,... | collective-permute-start | bytes 7176200 | tf_op jit(solution)/shard_map/ppermute | solution.py:46
  91.6 18.2 %all-to-all-start = ((bf16[8,256,128]{2,1,0:T(8,128)(2,1)}), bf16[8,256,128]{2,1,0:T(8,128)(2,1)S(1)}, u32[]{:S(2)}, u32[]{:S(2)}) async-start(bf16[8,256,128]{2,1,0:T(8,128)(2,1)} %get-tuple-element.47), calls=%async_computation | async-start | bytes 1048576 | tf_op jit(solution)/shard_map/all_to_all | solution.py:1142
  95.2 28.2 %collective-permute-start.7 = (bf16[128,9344]{1,0:T(8,128)(2,1)}, bf16[128,9344]{1,0:T(8,128)(2,1)}, u32[]{:S(2)}, u32[]{:S(2)}) collective-permute-start(bf16[128,9344]{1,0:T(8,128)(2,1)} %collective-permute-done.4.refs_1_.refs_2_), channel_id=1, source_target_pairs={{0,4},{4,0},{8,12},{12,8},{16,20},{20,16},{24,28},{28,24},{1,5},{5... | collective-permute-start | bytes 7176200 | tf_op jit(solution)/shard_map/ppermute | solution.py:24
  95.6 27.9 %collective-permute-start.8 = (bf16[128,9344]{1,0:T(8,128)(2,1)}, bf16[128,9344]{1,0:T(8,128)(2,1)}, u32[]{:S(2)}, u32[]{:S(2)}) collective-permute-start(bf16[128,9344]{1,0:T(8,128)(2,1)} %collective-permute-done.5.refs_2_.refs_3_), channel_id=1, source_target_pairs={{0,4},{4,0},{8,12},{12,8},{16,20},{20,16},{24,28},{28,24},{1,5},{5... | collective-permute-start | bytes 7176200 | tf_op jit(solution)/shard_map/ppermute | solution.py:24
  122.0 42.0 %collective-permute-start.10 = (bf16[128,3072]{1,0:T(8,128)(2,1)S(1)}, bf16[128,3072]{1,0:T(8,128)(2,1)}, u32[]{:S(2)}, u32[]{:S(2)}) collective-permute-start(bf16[128,3072]{1,0:T(8,128)(2,1)S(1)} %constant_dynamic-slice_fusion), channel_id=1, source_target_pairs={{0,2},{1,3},{2,0},{3,1},{4,5},{5,4},{6,7},{7,6},{8,10},{9,11},{10,... | collective-permute-start | bytes 2359304 | tf_op jit(solution)/shard_map/ppermute | solution.py:46
  123.2 40.7 %collective-permute-start.11 = (bf16[128,3072]{1,0:T(8,128)(2,1)}, bf16[128,3072]{1,0:T(8,128)(2,1)}, u32[]{:S(2)}, u32[]{:S(2)}) collective-permute-start(bf16[128,3072]{1,0:T(8,128)(2,1)} %collective-permute-done.3.refs_1_), channel_id=1, source_target_pairs={{0,2},{1,3},{2,0},{3,1},{4,5},{5,4},{6,7},{7,6},{8,10},{9,11},{10,... | collective-permute-start | bytes 2359304 | tf_op jit(solution)/shard_map/ppermute | solution.py:46
  167.1 22.1 %all-to-all-start.1 = ((bf16[8,256,128]{2,1,0:T(8,128)(2,1)}), bf16[8,256,128]{2,1,0:T(8,128)(2,1)S(1)}, u32[]{:S(2)}, u32[]{:S(2)}) async-start(bf16[8,256,128]{2,1,0:T(8,128)(2,1)} %get-tuple-element.56), calls=%async_computation.1 | async-start | bytes 1048576 | tf_op jit(solution)/shard_map/all_to_all | solution.py:1156
  189.2 49.3 %collective-permute-start.17 = (bf16[2,4,912,128]{3,2,1,0:T(8,128)(2,1)}, bf16[2,4,912,128]{3,2,1,0:T(8,128)(2,1)}, u32[]{:S(2)}, u32[]{:S(2)}) collective-permute-start(bf16[2,4,912,128]{3,2,1,0:T(8,128)(2,1)} %get-tuple-element.70), channel_id=1, source_target_pairs={{0,2},{1,3},{2,0},{3,1},{4,5},{5,4},{6,7},{7,6},{8,10},{9,11},{10,... | collective-permute-start | bytes 5603336 | tf_op jit(solution)/shard_map/ppermute | solution.py:46
  190.6 50.5 %collective-permute-start.31 = (bf16[2,128,5248]{2,1,0:T(8,128)(2,1)}, bf16[2,128,5248]{2,1,0:T(8,128)(2,1)S(1)}, u32[]{:S(2)}, u32[]{:S(2)}) collective-permute-start(bf16[2,128,5248]{2,1,0:T(8,128)(2,1)} %get-tuple-element.80), channel_id=1, source_target_pairs={{0,2},{1,3},{2,0},{3,1},{4,5},{5,4},{6,7},{7,6},{8,10},{9,11},{10,... | collective-permute-start | bytes 8060936 | tf_op jit(solution)/shard_map/ppermute | solution.py:46
  224.7 42.8 %all-to-all-start.2 = ((bf16[8,256,384]{2,1,0:T(8,128)(2,1)}), bf16[8,256,384]{2,1,0:T(8,128)(2,1)}, u32[]{:S(2)}, u32[]{:S(2)}) async-start(bf16[8,256,384]{2,1,0:T(8,128)(2,1)} %attention_backward.1.grad_ref), calls=%async_computation.2 | async-start | bytes 3145728 | tf_op jit(solution)/shard_map/all_to_all | solution.py:1172
  244.8 22.7 %collective-permute-start.32 = (bf16[128,5248]{1,0:T(8,128)(2,1)}, bf16[128,5248]{1,0:T(8,128)(2,1)}, u32[]{:S(2)}, u32[]{:S(2)}) collective-permute-start(bf16[128,5248]{1,0:T(8,128)(2,1)} %fusion), channel_id=1, source_target_pairs={{0,1},{1,0},{2,3},{3,2},{4,6},{5,7},{6,4},{7,5},{8,9},{9,8},{10,11... | collective-permute-start | bytes 4030472 | tf_op jit(solution)/shard_map/ppermute | solution.py:46
  286.3 20.7 %collective-permute-start.19 = (bf16[256,384]{1,0:T(8,128)(2,1)S(1)}, bf16[256,384]{1,0:T(8,128)(2,1)}, u32[]{:S(2)}, u32[]{:S(2)}) collective-permute-start(bf16[256,384]{1,0:T(8,128)(2,1)S(1)} %fusion.9), channel_id=1, source_target_pairs={{0,1},{1,0},{2,3},{3,2},{4,6},{5,7},{6,4},{7,5},{8,9},{9,8},{10,11... | collective-permute-start | bytes 589832 | tf_op jit(solution)/shard_map/ppermute | solution.py:46
  308.0 34.2 %collective-permute-start.20 = (bf16[256,384]{1,0:T(8,128)(2,1)S(1)}, bf16[256,384]{1,0:T(8,128)(2,1)S(1)}, u32[]{:S(2)}, u32[]{:S(2)}) collective-permute-start(bf16[256,384]{1,0:T(8,128)(2,1)S(1)} %fusion.7), channel_id=1, source_target_pairs={{0,16},{4,20},{8,24},{12,28},{16,0},{20,4},{24,8},{28,12},{1,17},{... | collective-permute-start | bytes 589832 | tf_op jit(solution)/shard_map/ppermute | solution.py:72
  321.6 19.4 %collective-permute-start.26 = (bf16[912,128]{1,0:T(8,128)(2,1)S(1)}, bf16[912,128]{1,0:T(8,128)(2,1)S(1)}, u32[]{:S(2)}, u32[]{:S(2)}) collective-permute-start(bf16[912,128]{1,0:T(8,128)(2,1)S(1)} %fusion.4), channel_id=1, source_target_pairs={{0,16},{4,20},{8,24},{12,28},{16,0},{20,4},{24,8},{28,12},{1,17},{... | collective-permute-start | bytes 700424 | tf_op jit(solution)/shard_map/ppermute | solution.py:72
  321.8 34.3 %collective-permute-start.36 = (bf16[2,32,5248]{2,1,0:T(8,128)(2,1)S(1)}, bf16[2,32,5248]{2,1,0:T(8,128)(2,1)S(1)}, u32[]{:S(2)}, u32[]{:S(2)}) collective-permute-start(bf16[2,32,5248]{2,1,0:T(8,128)(2,1)S(1)} %pad_maximum_fusion.refs_0_), channel_id=1, source_target_pairs={{0,8},{4,12},{8,0},{12,4},{16,24},{20,28},{24,16},{28,20},{1,9},{5... | collective-permute-start | bytes 2015240 | tf_op jit(solution)/shard_map/ppermute | solution.py:72
  342.2 18.7 %collective-permute-start.21 = (bf16[2,256,384]{2,1,0:T(8,128)(2,1)S(1)}, bf16[2,256,384]{2,1,0:T(8,128)(2,1)S(1)}, u32[]{:S(2)}, u32[]{:S(2)}) collective-permute-start(bf16[2,256,384]{2,1,0:T(8,128)(2,1)S(1)} %pad_maximum_fusion.2.refs_0_), channel_id=1, source_target_pairs={{0,8},{4,12},{8,0},{12,4},{16,24},{20,28},{24,16},{28,20},{1,9},{5... | collective-permute-start | bytes 1179656 | tf_op jit(solution)/shard_map/ppermute | solution.py:72
  356.0 28.1 %collective-permute-start.37 = (bf16[2,32,5248]{2,1,0:T(8,128)(2,1)S(1)}, bf16[2,32,5248]{2,1,0:T(8,128)(2,1)S(1)}, u32[]{:S(2)}, u32[]{:S(2)}) collective-permute-start(bf16[2,32,5248]{2,1,0:T(8,128)(2,1)S(1)} %pad_maximum_fusion.refs_0_), channel_id=1, source_target_pairs={{0,4},{4,0},{8,12},{12,8},{16,20},{20,16},{24,28},{28,24},{1,5},{5... | collective-permute-start | bytes 2015240 | tf_op jit(solution)/shard_map/ppermute | solution.py:24
  356.1 28.0 %collective-permute-start.38 = (bf16[2,32,5248]{2,1,0:T(8,128)(2,1)S(1)}, bf16[2,32,5248]{2,1,0:T(8,128)(2,1)S(1)}, u32[]{:S(2)}, u32[]{:S(2)}) collective-permute-start(bf16[2,32,5248]{2,1,0:T(8,128)(2,1)S(1)} %collective-permute-done.36.refs_1_), channel_id=1, source_target_pairs={{0,4},{4,0},{8,12},{12,8},{16,20},{20,16},{24,28},{28,24},{1,5},{5... | collective-permute-start | bytes 2015240 | tf_op jit(solution)/shard_map/ppermute | solution.py:24
  (52 other events, 705.6 us)
Sparse Core Ops, SparseCore 0:
  9.6 49.6 all-gather.1

commit v3 on v2

--- a/solution.py
+++ b/solution.py
@@ -50,13 +50,11 @@
     return lax.optimization_barrier((value, *others))[0]
 
 
-def plane_gather(piece, seq_count, fsdp_count, *others):
-    pieces = [piece]
-    for phase in range(fsdp_count.bit_length() - 1):
-        if phase == 1:
-            pieces[0] = after(piece, pieces[1], *others)
+def plane_gather_rest(piece, first, seq_count, fsdp_count, *others):
+    pieces = [after(piece, first, *others), after(first, *others)]
+    for phase in range(1, fsdp_count.bit_length() - 1):
         pieces = pieces + [plane_swap(p, phase, seq_count, fsdp_count) for p in pieces]
-    return pieces[1:]
+    return [first] + pieces[2:]
 
 
 def added(*values):
@@ -69,7 +67,7 @@
 
 
 def line_swap(value, level, seq_count):
-    return lax.ppermute(value, "seq", [(i, i ^ (2 << level)) for i in range(seq_count)])
+    return lax.ppermute(value, "seq", [(i, i ^ (2 << (level ^ (i & 1)))) for i in range(seq_count)])
 
 
 def line_reduce(parts, seq_count):
@@ -78,10 +76,10 @@
     return added(*(p[0] for p in parts), got[0], last)
 
 
-def line_gather(block, seq_count):
+def line_gather(block, seq_count, *others):
     pair = jnp.stack([block, line_swap(block, 1, seq_count)])
     rest = line_swap(pair, 0, seq_count)
-    return [pair, rest, core_swap(pair, seq_count), core_swap(rest, seq_count)]
+    return [pair, rest, core_swap(pair, seq_count), core_swap(after(rest, *others), seq_count)]
 
 
 def any_spec():
@@ -135,8 +133,19 @@
     return copies
 
 
-def down_blocks(rows, tall):
-    return [(start, min(tall, rows - start)) for start in range(0, rows, tall)]
+def down_blocks(rows, columns, tall):
+    whole = rows // tall
+    blocks = [(k * tall, 0, tall, columns, 0, k * columns) for k in range(whole)]
+    left = rows - whole * tall
+    if left:
+        blocks += [
+            (whole * tall, 128 * q, left, 128, q * left, whole * columns) for q in range(columns // 128)
+        ]
+    return blocks
+
+
+def down_width(rows, columns, tall):
+    return rows // tall * columns + (128 if rows % tall else 0)
 
 
 def down_copies(place_ref, own, mine, others, left, full, sems, hidden):
@@ -146,45 +155,44 @@
     rows = own.shape[0]
     half = own.shape[1] // 2
     core = place_ref[2 * count + 1]
-    blocks = down_blocks(rows, mine[0].shape[0])
+    blocks = down_blocks(rows, half, mine[0].shape[0])
     copies = [own_copy(place_ref, own, full, sems, rows)]
     for which, (refs, side) in enumerate(((mine, core), (others, 1 - core))):
         for i, ref in enumerate(refs):
             at = 1 + which * count + i
             side_at = pl.multiple_of(side * half, 128)
-            for k, (start, tall) in enumerate(blocks):
-                base = pl.multiple_of(place_ref[at] * rows + start, 16)
+            for k, (row, column, tall, wide, packed_row, packed_column) in enumerate(blocks):
+                base = pl.multiple_of(place_ref[at] * rows + row, 16)
                 copies.append(
                     pltpu.make_async_copy(
-                        ref.at[pl.ds(0, tall), pl.ds(left + k * half, half)],
-                        full.at[pl.ds(base, tall), pl.ds(side_at, half)],
+                        ref.at[pl.ds(packed_row, tall), pl.ds(left + packed_column, wide)],
+                        full.at[pl.ds(base, tall), pl.ds(pl.multiple_of(side_at + column, 128), wide)],
                         sems.at[1 + (at - 1) * len(blocks) + k],
                     )
                 )
     return copies
 
 
-def pack_pieces(place_ref, in_ref, out_ref, down_ref, packed_ref, sems):
+def pack_pieces(place_ref, in_ref, out_ref, down_ref, first_ref, second_ref, sems):
     half = in_ref.shape[0] // 2
     core = place_ref[place_ref.shape[0] - 2]
     base = pl.multiple_of(core * half, 16)
-    wide, also = in_ref.shape[1], out_ref.shape[1]
+    also = out_ref.shape[1]
     copies = [
         pltpu.make_async_copy(
-            in_ref.at[pl.ds(base, half), :], packed_ref.at[:, pl.ds(0, wide)], sems.at[0]
+            out_ref.at[pl.ds(base, half), :], first_ref.at[:, pl.ds(0, also)], sems.at[0]
         ),
-        pltpu.make_async_copy(
-            out_ref.at[pl.ds(base, half), :], packed_ref.at[:, pl.ds(wide, also)], sems.at[1]
-        ),
+        pltpu.make_async_copy(in_ref.at[pl.ds(base, half), :], second_ref, sems.at[1]),
     ]
-    if packed_ref.shape[1] > wide + also:
+    if first_ref.shape[1] > also:
         columns = down_ref.shape[1] // 2
         side = pl.multiple_of(core * columns, 128)
-        for k, (start, tall) in enumerate(down_blocks(down_ref.shape[0], half)):
+        blocks = down_blocks(down_ref.shape[0], columns, half)
+        for k, (row, column, tall, part, packed_row, packed_column) in enumerate(blocks):
             copies.append(
                 pltpu.make_async_copy(
-                    down_ref.at[pl.ds(start, tall), pl.ds(side, columns)],
-                    packed_ref.at[pl.ds(0, tall), pl.ds(wide + also + k * columns, columns)],
+                    down_ref.at[pl.ds(row, tall), pl.ds(pl.multiple_of(side + column, 128), part)],
+                    first_ref.at[pl.ds(packed_row, tall), pl.ds(also + packed_column, part)],
                     sems.at[2 + k],
                 )
             )
@@ -196,14 +204,18 @@
 
 def run_pack_pieces(place, w_in, w_out, w_down, regular):
     half = w_in.shape[0] // 2
-    blocks = len(down_blocks(w_down.shape[0], half)) if regular else 0
-    wide = w_in.shape[1] + w_out.shape[1] + blocks * (w_down.shape[1] // 2)
+    down = (w_down.shape[0], w_down.shape[1] // 2, half)
+    blocks = len(down_blocks(*down)) if regular else 0
+    wide = w_out.shape[1] + (down_width(*down) if regular else 0)
     return pl.pallas_call(
         pack_pieces,
         name="pack_pieces",
-        out_shape=jax.ShapeDtypeStruct((half, wide), BF16),
+        out_shape=(
+            jax.ShapeDtypeStruct((half, wide), BF16),
+            jax.ShapeDtypeStruct((half, w_in.shape[1]), BF16),
+        ),
         in_specs=[smem_spec()] + [any_spec()] * 3,
-        out_specs=vmem_spec(),
+        out_specs=[vmem_spec()] * 2,
         scratch_shapes=[pltpu.SemaphoreType.DMA((2 + blocks,))],
         compiler_params=params(),
         cost_estimate=cost(1e6, 5e6),
@@ -562,7 +574,7 @@
 def down_semaphores(downs):
     if len(downs) == 1:
         return pltpu.SemaphoreType.DMA((1,))
-    blocks = len(down_blocks(downs[0].shape[0], downs[1].shape[0]))
+    blocks = len(down_blocks(downs[0].shape[0], downs[0].shape[1] // 2, downs[1].shape[0]))
     return pltpu.SemaphoreType.DMA((1 + (len(downs) - 1) * blocks,))
 
 
@@ -571,13 +583,14 @@
     load_down(place_ref, downs, (len(downs) - 1) // 2, hidden, left, full, sems)
     cot = cot_ref[...]
     tiles = padded(hidden) // 128
+    wide = 128 * max(n for n in (1, 2, 3) if tiles % n == 0)
 
     def step(i, carry):
-        at = pl.multiple_of(i * 128, 128)
-        out_ref[:, pl.ds(at, 128)] = nt_dot(cot, full[pl.ds(at, 128), :])
-        return carry
-
-    lax.fori_loop(0, tiles, step, 0)
+        at = pl.multiple_of(i * wide, 128)
+        out_ref[:, pl.ds(at, wide)] = nt_dot(cot, full[pl.ds(at, wide), :])
+        return carry
+
+    lax.fori_loop(0, padded(hidden) // wide, step, 0)
 
 
 def run_hidden_grad(place, cot, downs, left, hidden):
@@ -624,9 +637,11 @@
 def feed_forward(
     count, hidden, heads_width, place_ref, x_ref, att_ref, cot_ref, gain_ref, gh_hbm, *refs
 ):
-    out_own, in_own, mine, others = refs[0], refs[1], refs[2 : 2 + count], refs[2 + count : 2 + 2 * count]
-    mid_ref, gmid_ref, send_hbm, keep_hbm, ga_ref = refs[2 + 2 * count : 7 + 2 * count]
-    wo, wi, both, early, late, send_ref, keep_ref, gh_ref, sem_o, sem_i, sems = refs[7 + 2 * count :]
+    out_own, in_own, refs = refs[0], refs[1], refs[2:]
+    first, others, refs = refs[:count], refs[count : 2 * count], refs[2 * count :]
+    second, second_others, refs = refs[:count], refs[count : 2 * count], refs[2 * count :]
+    mid_ref, gmid_ref, send_hbm, keep_hbm, ga_ref = refs[:5]
+    wo, wi, both, early, late, send_ref, keep_ref, gh_ref, sem_o, sem_i, sems = refs[5:]
     fetch = pltpu.make_async_copy(gh_hbm, gh_ref, sems.at[0])
     send_out = pltpu.make_async_copy(send_ref, send_hbm, sems.at[1])
     keep_out = pltpu.make_async_copy(keep_ref, keep_hbm, sems.at[2])
@@ -638,8 +653,8 @@
     gbr_ref = keep_ref.at[:, pl.ds(wide_hidden, dim)]
     att_all_ref = keep_ref.at[:, pl.ds(wide_hidden + dim, dim)]
     keep_ref[:, pl.ds(wide_hidden + 2 * dim, dim)] = cot_ref[...]
-    copies_o = row_copies(place_ref, out_own, mine, others, 2 * hidden, wo, sem_o)
-    copies_i = row_copies(place_ref, in_own, mine, others, 0, wi, sem_i)
+    copies_o = row_copies(place_ref, out_own, first, others, 0, wo, sem_o)
+    copies_i = row_copies(place_ref, in_own, second, second_others, 0, wi, sem_i)
     for copy in copies_o:
         copy.start()
     for copy in copies_i:
@@ -730,11 +745,11 @@
     send_out.start()
 
     def back(i, carry):
-        at = pl.multiple_of(i * 128, 128)
-        both[:, pl.ds(at, 128)] = nt_dot(gboth_ref[:, : 2 * hidden], wi[pl.ds(at, 128), :])
-        return carry
-
-    lax.fori_loop(0, dim // 128, back, 0)
+        at = pl.multiple_of(i * 256, 256)
+        both[:, pl.ds(at, 256)] = nt_dot(gboth_ref[:, : 2 * hidden], wi[pl.ds(at, 256), :])
+        return carry
+
+    lax.fori_loop(0, dim // 256, back, 0)
     middle = mid_ref[...]
     center = middle - jnp.mean(middle, axis=-1, keepdims=True)
     spread = jnp.mean(center * center, axis=-1, keepdims=True)
@@ -748,21 +763,21 @@
     keep_out.start()
 
     def spread_out(i, carry):
-        at = pl.multiple_of(i * 128, 128)
-        both[:, pl.ds(at, 128)] = nt_dot(gbr_ref[...], wo[pl.ds(at, 128), :])
-        return carry
-
-    lax.fori_loop(0, dim // 128, spread_out, 0)
+        at = pl.multiple_of(i * 256, 256)
+        both[:, pl.ds(at, 256)] = nt_dot(gbr_ref[...], wo[pl.ds(at, 256), :])
+        return carry
+
+    lax.fori_loop(0, dim // 256, spread_out, 0)
     for s in range(att_ref.shape[0]):
         ga_ref[s] = both[:, s * heads_width : (s + 1) * heads_width].astype(BF16)
     send_out.wait()
     keep_out.wait()
 
 
-def run_feed_forward(place, x, att, cot, gain, grad_hidden, w_out, w_in, mine, others, hidden):
+def run_feed_forward(place, x, att, cot, gain, grad_hidden, w_out, w_in, first, second, hidden):
     rows, dim = x.shape
     seq_count, _, heads_width = att.shape
-    count = len(mine)
+    count = len(first) // 2
     return pl.pallas_call(
         functools.partial(feed_forward, count, hidden, heads_width),
         name="feed_forward",
@@ -773,7 +788,7 @@
             jax.ShapeDtypeStruct((rows, padded(hidden) + 3 * dim), BF16),
             jax.ShapeDtypeStruct((seq_count, rows, heads_width), BF16),
         ),
-        in_specs=[smem_spec()] + [vmem_spec()] * 4 + [any_spec()] * (3 + 2 * count),
+        in_specs=[smem_spec()] + [vmem_spec()] * 4 + [any_spec()] * (3 + 4 * count),
         out_specs=[vmem_spec()] * 2 + [any_spec()] * 2 + [vmem_spec()],
         scratch_shapes=[
             pltpu.VMEM((dim, dim), BF16),
@@ -790,10 +805,11 @@
         ],
         compiler_params=params(),
         cost_estimate=cost(16e9, 24e6),
-    )(place, x, att, cot, gain, grad_hidden, w_out, w_in, *mine, *others)
-
-
-ORDER = (0, 2, 1, 3)
+    )(place, x, att, cot, gain, grad_hidden, w_out, w_in, *first, *second)
+
+
+def block_order(core):
+    return (0, 2 - core, 1 + core, 3)
 
 
 def in_grad(hidden, wide, place_ref, send_ref, other_ref, a_ref, b_ref, c_ref, turned, picked):
@@ -807,7 +823,7 @@
         turned[:, tokens:] = other_ref[:, 2 * hidden :].T
         core, z = place_ref[7], place_ref[8]
         for at, key in enumerate((2, 3, 1, 0)):
-            for j, k in enumerate(ORDER):
+            for j, k in enumerate(block_order(core)):
                 base = pl.multiple_of(place_ref[key] * rows + core * half + (z ^ k) * short, 16)
                 to = at * half + j * short
                 picked[to : to + short, :] = turned[pl.ds(base, short), :]
@@ -860,7 +876,7 @@
         turned[:wide, tokens:] = other_ref[:, :wide].T
         turned[wide:, :tokens] = keep_ref[:, wide + dim : wide + 2 * dim].T
         turned[wide:, tokens:] = other_ref[:, wide + dim : wide + 2 * dim].T
-        for j, k in enumerate(ORDER):
+        for j, k in enumerate(block_order(core)):
             left = pl.ds(pl.multiple_of(wide + 2 * dim + core * half + (z ^ k) * 128, 128), 128)
             picked[:tokens, j * 128 : (j + 1) * 128] = keep_ref[:, left]
             picked[tokens:, j * 128 : (j + 1) * 128] = other_ref[:, left]
@@ -871,7 +887,7 @@
     base = pl.multiple_of(owner * down_rows, 16)
     down = nn_dot(turned[pl.ds(base, down_rows), :], picked[:, :half]).astype(BF16)
     left = []
-    for k in ORDER:
+    for k in block_order(core):
         base = pl.multiple_of(wide + owner * 8 * short + core * 4 * short + (z ^ k) * short, 16)
         left.append(turned[pl.ds(base, short), :])
     out = nn_dot(jnp.concatenate(left, axis=0), picked[:, half:]).astype(BF16)
@@ -929,8 +945,8 @@
 
 
 def row_block(i, place_ref):
-    order = jnp.where(i % 4 == 1, 2, jnp.where(i % 4 == 2, 1, i % 4))
     side = jnp.where(i < 4, place_ref[7], 1 - place_ref[7])
+    order = jnp.where(i % 4 == 1, 2 - side, jnp.where(i % 4 == 2, 1 + side, i % 4))
     return (side * 4 + (place_ref[8] ^ order), 0)
 
 
@@ -961,7 +977,8 @@
     core, z = place_ref[7], place_ref[8]
     for q, ref in enumerate(pieces):
         for at in range(2):
-            yield ref.at[at], (core if q < 2 else 1 - core), z ^ ORDER[2 * (q % 2) + at]
+            side = core if q < 2 else 1 - core
+            yield ref.at[at], side, z ^ block_order(side)[2 * (q % 2) + at]
 
 
 def unpack_rest(place_ref, *refs):
@@ -1037,11 +1054,11 @@
         copy.wait()
 
     def step(i, carry):
-        at = pl.multiple_of(i * 128, 128)
-        total[:, pl.ds(at, 128)] = nt_dot(grad[...], full[pl.ds(at, 128), :])
-        return carry
-
-    lax.fori_loop(0, dim // 128, step, 0)
+        at = pl.multiple_of(i * 256, 256)
+        total[:, pl.ds(at, 256)] = nt_dot(grad[...], full[pl.ds(at, 256), :])
+        return carry
+
+    lax.fori_loop(0, dim // 256, step, 0)
     x = x_ref[...].astype(F32)
     center = x - jnp.mean(x, axis=-1, keepdims=True)
     spread = jnp.mean(center * center, axis=-1, keepdims=True)
@@ -1104,16 +1121,13 @@
     heads = dim // HD // seq_count
     width = heads * HD
     hidden = w_in.shape[1] // 2
-    def gather(piece, *others):
-        return plane_gather(piece, seq_count, fsdp_count, *others)
-
+    counts = (seq_count, fsdp_count)
     swap = functools.partial(core_swap, seq_count=seq_count)
 
     keys = [jnp.array([plane_mask(c, key, levels) for key in range(1, fsdp_count)], jnp.int32) for c in (0, 1)]
     mine = fsdp_at ^ jnp.where(core == 0, keys[0], keys[1])
     other = fsdp_at ^ jnp.where(core == 0, keys[1], keys[0])
     place = jnp.stack([fsdp_at, *mine, *other, core, seq_at // 2]).astype(jnp.int32)
-
     regular = fsdp_count == 4 and seq_count == 8 and w_down.shape[0] % 16 == 0 and dim == 1024
 
     x_all = lax.all_gather(x, "seq", axis=0, tiled=False)
@@ -1131,28 +1145,28 @@
             lax.all_gather(own_heads, "fsdp", axis=0, tiled=True),
             lax.all_gather(gains, "fsdp", axis=1, tiled=True).astype(F32),
         ]
-    piece = run_pack_pieces(place, w_in, w_out, w_down, regular)
-    mine = gather(piece)
-    left = 2 * hidden + dim
+    first_piece, second_piece = run_pack_pieces(place, w_in, w_out, w_down, regular)
+    first_a, second_a = plane_swap(first_piece, 0, *counts), plane_swap(second_piece, 0, *counts)
+    first = plane_gather_rest(first_piece, first_a, *counts)
+    second = plane_gather_rest(second_piece, second_a, *counts, first_a)
+    left = dim
 
     layout = sequence_layout(seq_lengths[0], seq_order[0], group)
     gains, normed, packed, att, out_t, lse = run_attention_forward(place, x_all, head_pieces, layout, heads)
     gain_one, gain_two = gains[:1], gains[1:]
     qkv_piece = lax.dynamic_slice_in_dim(w_qkv, core * (w_qkv.shape[0] // 2), w_qkv.shape[0] // 2, 0)
     att_done = lax.all_to_all(att, "seq", split_axis=0, concat_axis=0, tiled=True)
-    others = [swap(mine[0])] + [swap(after(p, att, *([att_done] if i else []))) for i, p in enumerate(mine[1:])]
+    first = first + [swap(first[0])] + [swap(after(piece, att)) for piece in first[1:]]
     if regular:
-        downs = [w_down] + mine + others
+        downs = [w_down] + first
     else:
         downs = [lax.all_gather(w_down, "fsdp", axis=0, tiled=True)]
+    grad_hidden = run_hidden_grad(place, cot, downs, left, hidden)
+    second = second + [swap(second[0])] + [swap(after(piece, att_done, grad_hidden)) for piece in second[1:]]
     att = att_done
-    qkv_mine = gather(after(qkv_piece, att))
-    grad_hidden = run_hidden_grad(place, cot, downs, left, hidden)
     middle, gmid, send, keep, gatt = run_feed_forward(
-        place, x, after(att, qkv_mine[0]), cot, gain_two, grad_hidden, w_out, w_in, mine, others, hidden
+        place, x, att, cot, gain_two, grad_hidden, w_out, w_in, first, second, hidden
     )
-    send = after(send, *qkv_mine)
-    qkvs = [w_qkv] + qkv_mine + [swap(p) for p in qkv_mine]
     dout = lax.all_to_all(gatt, "seq", split_axis=0, concat_axis=0, tiled=True)
     reduce = functools.partial(plane_reduce, seq_count=seq_count, fsdp_count=fsdp_count)
     send_other, keep_other = swap(send), swap(keep)
@@ -1160,32 +1174,51 @@
     if regular:
         short = w_in.shape[0] // 8
         in_a, in_b, in_c = run_in_grad(place, send, send_other, hidden)
-        rest_a, rest_b, rest_c = run_rest_grad(place, keep, after(keep_other, in_b), hidden)
-        dout = after(dout, in_b, rest_b)
-        in_a = plane_swap(in_a, 1, seq_count, fsdp_count)
-        rest_a = plane_swap(rest_a, 1, seq_count, fsdp_count)
+        dout = after(dout, in_b)
+        in_a = plane_swap(in_a, 1, *counts)
+        in_sum = added(in_b[0], in_a[1])
     else:
-        rest_a = keep_other
+        in_b = in_sum = gatt
+    qkv_piece = after(qkv_piece, in_b)
+    qkv_mine = {1 << phase: plane_swap(qkv_piece, phase, *counts) for phase in range(levels)}
+    keep_other = after(keep_other, *qkv_mine.values())
 
     grads = run_attention_backward(dout, packed, out_t, lse, layout, heads)
-    layer_out = run_layer_result(place, middle, after(keep, grads), downs, left, hidden)
     grad_rows = lax.all_to_all(grads, "seq", split_axis=0, concat_axis=0, tiled=True)
-    gw_heads = run_qkv_weight_grad(place, normed, after(grads, rest_a), regular)
+    gw_heads = run_qkv_weight_grad(place, normed, after(grads, in_sum), regular)
+    each = w_qkv.shape[0]
+    qkv_rest = in_sum
+    if regular:
+        in_second = plane_swap(in_sum, 0, *counts)
+        in_parts = [p.reshape(4, short, 2 * hidden) for p in (in_c[0], in_a[0], in_second)]
+        rest_a, rest_b, rest_c = run_rest_grad(place, keep, after(keep_other, in_sum), hidden)
+        in_z1 = line_swap(after(added(*(p[2:] for p in in_parts)), rest_b), 0, seq_count)
+        layer_out = run_layer_result(place, middle, after(keep, rest_b), downs, left, hidden)
+        rest_parts = reduce(plane_swap(after(rest_a, in_second), 1, *counts), rest_b, rest_c)
+        qkv_rest = rest_parts[2]
+    else:
+        layer_out = run_layer_result(place, middle, keep, downs, left, hidden)
+    for phase in range(1, levels):
+        for key in range(1, 1 << phase):
+            qkv_mine[key + (1 << phase)] = plane_swap(after(qkv_mine[key], qkv_rest), phase, *counts)
+    qkv_mine = [qkv_mine[key] for key in range(1, fsdp_count)]
+    qkvs = [w_qkv] + qkv_mine + [swap(p) for p in qkv_mine]
     grad_tokens = run_input_grad(place, x, gmid, gain_one, grad_rows, qkvs, count)
-    each = w_qkv.shape[0]
     if regular:
-        in_parts = [p.reshape(4, short, 2 * hidden) for p in reduce(in_a, in_b, in_c)]
-        in_parts[2] = after(in_parts[2], grad_rows, layer_out)
-        rest_parts = reduce(rest_a, rest_b, rest_c)
-        in_block = line_reduce(in_parts, seq_count)
-        rest_block = line_reduce(rest_parts, seq_count)
-        in_pieces = line_gather(after(in_block, grad_tokens), seq_count)
-        rest_pieces = line_gather(rest_block, seq_count)
         qkv_a, qkv_b, qkv_c = gw_heads
-        qkv_a = plane_swap(qkv_a, 1, seq_count, fsdp_count)
-        qkv_pieces = line_gather(added(*reduce(qkv_a, qkv_b, qkv_c)), seq_count)
+        qkv_a = plane_swap(after(qkv_a, rest_parts[1]), 1, *counts)
+        qkv_block = added(*reduce(qkv_a, qkv_b, qkv_c))
+        in_sum = after(added(*(p[1] for p in in_parts), in_z1[1]), grad_rows, layer_out)
+        in_z2 = line_swap(in_sum, 1, seq_count)
+        in_block = added(*(p[0] for p in in_parts), in_z1[0], in_z2)
+        rest_z1 = line_swap(after(added(*(p[2:] for p in rest_parts)), in_z1), 0, seq_count)
+        rest_z2 = line_swap(after(added(*(p[1] for p in rest_parts), rest_z1[1]), in_z2), 1, seq_count)
+        rest_block = added(*(p[0] for p in rest_parts), rest_z1[0], rest_z2)
+        in_pieces = line_gather(in_block, seq_count)
+        gw_in, sum_in = run_unpack_in(place, in_pieces, w_in)
+        rest_pieces = line_gather(rest_block, seq_count, sum_in)
+        qkv_pieces = line_gather(after(qkv_block, rest_z2, grad_tokens), seq_count, sum_in)
         gw_qkv, sum_qkv = run_unpack_qkv(place, qkv_pieces, w_qkv)
-        gw_in, sum_in = run_unpack_in(place, in_pieces, w_in)
         gw_out, gw_down = run_unpack_rest(place, rest_pieces, w_out.shape, w_down.shape)
         sum_qkv = sum_qkv[:, 0]
         sum_in = sum_in[:, 0]

time: 410 us -> 381 us (0.929)
  waiting for transfers between devices: 126 us -> 99.4 us
  Pallas kernels: 171 us -> 162 us
  local copies, waits for them, and re-layouts: 6.8 us -> 14.7 us
  starting transfers between devices: 59.6 us -> 64.6 us
    all_to_all x1, waiting for transfers between devices: 19.9 us -> 0.01 us  [local(): lax.all_to_all(grads, 'seq', split_axis=0, concat_axis=0, tiled=True)]
    all_gather x1, waiting for transfers between devices: 10.2 us -> 0.01 us  [local(): x_all = lax.all_gather(x, 'seq', axis=0, tiled=False)]
    ppermute x10, starting transfers between devices: 7.14 us -> 16.7 us  [line_swap(): lax.ppermute(value, 'seq', [(i, i ^ 2 << (level ^ i & 1)) for i in range(...]
    ppermute x14 -> x17, starting transfers between devices: 26.1 us -> 17.5 us  [core_swap(): return lax.ppermute(value, 'seq', [(i, i ^ 1) for i in range(seq_count)])]
    ppermute x10, waiting for transfers between devices: 39.1 us -> 31.5 us  [line_swap(): lax.ppermute(value, 'seq', [(i, i ^ 2 << (level ^ i & 1)) for i in range(...]
    ppermute x12 -> x15, waiting for transfers between devices: 49.3 us -> 55.4 us  [plane_swap(): return lax.ppermute(value, AXES, pairs)]
    unnamed x67 -> x69, local copies, waits for them, and re-layouts: 3.59 us -> 8.94 us
    ppermute x12 -> x15, starting transfers between devices: 10.4 us -> 12.6 us  [plane_swap(): return lax.ppermute(value, AXES, pairs)]
  transfers between devices with their start and end apart: 43 -> 49, of which waited for: 13 -> 16; matrix products, arithmetic and copies ran while one was open for 6% -> 7% of each run, Pallas kernels for 40% -> 35%
where the time goes in v3:
time: 381 us; the launch traced here: 377 us
  Pallas kernels  162 us (43%)
  waiting for transfers between devices  99.4 us (26%)
  starting transfers between devices  64.6 us (17%)
  other arithmetic  21.7 us (6%)
  local copies, waits for them, and re-layouts  14.7 us (4%)
  between operations  14.5 us (4%)
    ppermute x15, waiting for transfers between devices, plane_swap(): return lax.ppermute(value, AXES, pairs)  55.4 us
    pallas_call x1, Pallas kernels, run_attention_backward(): pl.pallas_call(functools.partial(attention_backward, seq_count, heads, gr...  34 us
    pallas_call x1, Pallas kernels, run_attention_forward(): pl.pallas_call(functools.partial(attention_forward, seq_count, heads, gro...  32.2 us
    ppermute x10, waiting for transfers between devices, line_swap(): lax.ppermute(value, 'seq', [(i, i ^ 2 << (level ^ i & 1)) for i in range(...  31.5 us
    pallas_call x1, Pallas kernels, run_feed_forward(): pl.pallas_call(functools.partial(feed_forward, count, hidden, heads_width...  24.8 us
    ppermute x17, starting transfers between devices, core_swap(): return lax.ppermute(value, 'seq', [(i, i ^ 1) for i in range(seq_count)])  17.5 us
    ppermute x10, starting transfers between devices, line_swap(): lax.ppermute(value, 'seq', [(i, i ^ 2 << (level ^ i & 1)) for i in range(...  16.7 us
    convert_element_type x10, other arithmetic, added(): return sum((v.astype(F32) for v in values)).astype(BF16)  13.8 us
  transfers between devices with their start and end apart: 49, of which 16 were waited for; matrix products, arithmetic and copies ran while one was open for 7% of the time, Pallas kernels for 35%

profile of v3, /device:TPU:1, one launch (start us, length us, event | category | flops | bytes accessed | tf_op | source)
XLA Modules:
  0.0 377.2 jit_solution(1359324404301960086)
XLA Ops:
  23.6 11.7 %collective-permute-done.3.refs_1_.refs_2_ = bf16[128,3712]{1,0:T(8,128)(2,1)} collective-permute-done((bf16[128,3712]{1,0:T(8,128)(2,1)}, bf16[128,3712]{1,0:T(8,128)(2,1)}, u32[]{:S(2)}, u32[]{:S(2)}) %collective-permute-start.3) | collective-permute-done | bytes 950304 | tf_op jit(solution)/shard_map/ppermute | solution.py:46
  36.2 23.2 %collective-permute-done.9.refs_8_ = bf16[128,5248]{1,0:T(8,128)(2,1)S(1)} collective-permute-done((bf16[128,5248]{1,0:T(8,128)(2,1)}, bf16[128,5248]{1,0:T(8,128)(2,1)S(1)}, u32[]{:S(2)}, u32[]{:S(2)}) %collective-permute-start.9) | collective-permute-done | bytes 1343520 | tf_op jit(solution)/shard_map/ppermute | solution.py:46
  62.9 32.2 %attention_forward.1 = (f32[2,1024]{1,0:T(2,128)}, bf16[8,256,1024]{2,1,0:T(8,128)(2,1)}, bf16[384,2048]{1,0:T(8,128)(2,1)}, bf16[8,256,128]{2,1,0:T(8,128)(2,1)...) custom-call(s32[4]{0:T(128)} %get-tuple-element.119.low_ref, s32[4]{0:T(128)} %get-tuple-element.118.high_ref, ...), custom_call_target="tpu_custom_call" | custom-call | flops 24000000000 | bytes 20000000 | tf_op jit(solution)/shard_map/attention_forward/pallas_call | solution.py:359
  95.7 5.2 %all-to-all-start = ((bf16[8,256,128]{2,1,0:T(8,128)(2,1)}), bf16[8,256,128]{2,1,0:T(8,128)(2,1)S(1)}, u32[]{:S(2)}, u32[]{:S(2)}) async-start(bf16[8,256,128]{2,1,0:T(8,128)(2,1)} %get-tuple-element.58), calls=%async_computation | async-start | bytes 1048576 | tf_op jit(solution)/shard_map/all_to_all | solution.py:1158
  101.0 9.0 %hidden_grad.1.gh_hbm = f32[256,2688]{1,0:T(8,128)} custom-call(s32[9]{0:T(128)} %stack.51.place_ref, bf16[256,1024]{1,0:T(8,128)(2,1)} %bitcast.104, bf16[656,1024]{1,0:T(8,128)(2,1)} %refs_0_.6, bf16[128,3712]{1,0:T(8,128)(2,1)} %collective-permute-done.3.refs_1_.refs_2_, bf16[128,3712]{1,0:T(8,128)(2,1)} %collective-permute-done.4.refs_2_.refs_3_, ...), custom_call_target="tpu_custom_call" | custom-call | flops 4000000000 | bytes 9000000 | tf_op jit(solution)/shard_map/hidden_grad/pallas_call | solution.py:598
  110.0 5.4 %all-to-all-done.att_ref = bf16[8,256,128]{2,1,0:T(8,128)(2,1)S(1)} async-done(((bf16[8,256,128]{2,1,0:T(8,128)(2,1)}), bf16[8,256,128]{2,1,0:T(8,128)(2,1)S(1)}, u32[]{:S(2)}, u32[]{:S(2)}) %all-to-all-start) | async-done | bytes 524320 | tf_op jit(solution)/shard_map/all_to_all | solution.py:1158
  122.0 24.8 %feed_forward.1 = (f32[256,1024]{1,0:T(8,128)}, f32[256,1024]{1,0:T(8,128)}, bf16[256,6272]{1,0:T(8,128)(2,1)}, bf16[256,5760]{1,0:T(8,128)(2,1)}, bf16[8,256,128]{2,1,0:T(8,128)(2,1)}) custom-call(s32[9]{0:T(128)} %stack.51.place_ref, bf16[256,1024]{1,0:T(8,128)(2,1)} %bitcast.92, bf16[8,256,128]{2,1,0:T(8,128)(2,1)} %copy-done.9, ...), custom_call_target="tpu_custom_call" | custom-call | flops 16000000000 | bytes 24000000 | tf_op jit(solution)/shard_map/feed_forward/pallas_call | solution.py:781
  148.8 4.2 %all-to-all-start.1 = ((bf16[8,256,128]{2,1,0:T(8,128)(2,1)}), bf16[8,256,128]{2,1,0:T(8,128)(2,1)}, u32[]{:S(2)}, u32[]{:S(2)}) async-start(bf16[8,256,128]{2,1,0:T(8,128)(2,1)} %get-tuple-element.80), calls=%async_computation.1 | async-start | bytes 1048576 | tf_op jit(solution)/shard_map/all_to_all | solution.py:1170
  153.7 9.0 %in_grad.1 = (bf16[2,128,5248]{2,1,0:T(8,128)(2,1)}, bf16[1,128,5248]{2,1,0:T(8,128)(2,1)}, bf16[1,128,5248]{2,1,0:T(8,128)(2,1)}) custom-call(s32[9]{0:T(128)} %stack.51.place_ref, bf16[256,6272]{1,0:T(8,128)(2,1)} %get-tuple-element.71.send_ref, bf16[256,6272]{1,0:T(8,128)(2,1)} %collective-permute-done.16.other_ref), custom_call_target="tpu_custom_call" | custom-call | flops 5502926848 | bytes 10747904 | tf_op jit(solution)/shard_map/in_grad/pallas_call | solution.py:847
  167.6 34.0 %attention_backward.1.grad_ref = bf16[8,256,384]{2,1,0:T(8,128)(2,1)} custom-call(s32[8]{0:T(128)} %get-tuple-element.117.low_ref, s32[8]{0:T(128)} %get-tuple-element.116.high_ref, bf16[8,256,128]{2,1,0:T(8,128)(2,1)} %all-to-all-done.1.dout_ref, bf16[384,2048]{1,0:T(8,128)(2,1)} %get-tuple-element.82.packed_ref, f32[128,2048]{1,0:T(8,128)} %get-tuple-element.83.out_ref, ...), custom_call_target="tpu_custom_call" | custom-call | flops 30000001024 | bytes 10000000 | tf_op jit(solution)/shard_map/attention_backward/pallas_call | solution.py:498
  201.6 5.0 %all-to-all-start.2 = ((bf16[8,256,384]{2,1,0:T(8,128)(2,1)}), bf16[8,256,384]{2,1,0:T(8,128)(2,1)}, u32[]{:S(2)}, u32[]{:S(2)}) async-start(bf16[8,256,384]{2,1,0:T(8,128)(2,1)} %attention_backward.1.grad_ref), calls=%async_computation.2 | async-start | bytes 3145728 | tf_op jit(solution)/shard_map/all_to_all | solution.py:1187
  206.6 5.4 %collective-permute-done.19 = bf16[2,128,5248]{2,1,0:T(8,128)(2,1)S(1)} collective-permute-done((bf16[2,128,5248]{2,1,0:T(8,128)(2,1)}, bf16[2,128,5248]{2,1,0:T(8,128)(2,1)S(1)}, u32[]{:S(2)}, u32[]{:S(2)}) %collective-permute-start.19) | collective-permute-done | bytes 2687008 | tf_op jit(solution)/shard_map/ppermute | solution.py:46
  215.2 8.8 %rest_grad.1 = (bf16[2,4,912,128]{3,2,1,0:T(8,128)(2,1)}, bf16[1,4,912,128]{3,2,1,0:T(8,128)(2,1)}, bf16[1,4,912,128]{3,2,1,0:T(8,128)(2,1)}) custom-call(s32[9]{0:T(128)} %stack.51.place_ref, bf16[256,5760]{1,0:T(8,128)(2,1)} %get-tuple-element.78.keep_ref, bf16[256,5760]{1,0:T(8,128)(2,1)} %collective-permute-done.15.other_ref), custom_call_target="tpu_custom_call" | custom-call | flops 4000000000 | bytes 10000000 | tf_op jit(solution)/shard_map/rest_grad/pallas_call | solution.py:915
  225.2 6.9 %collective-permute-done.20 = bf16[128,5248]{1,0:T(8,128)(2,1)} collective-permute-done((bf16[128,5248]{1,0:T(8,128)(2,1)}, bf16[128,5248]{1,0:T(8,128)(2,1)}, u32[]{:S(2)}, u32[]{:S(2)}) %collective-permute-start.20) | collective-permute-done | bytes 1343520 | tf_op jit(solution)/shard_map/ppermute | solution.py:46
  236.8 8.3 %layer_result.1 = bf16[256,1024]{1,0:T(8,128)(2,1)} custom-call(s32[9]{0:T(128)} %stack.51.place_ref, f32[256,1024]{1,0:T(8,128)} %get-tuple-element.69.mid_ref, bf16[256,5760]{1,0:T(8,128)(2,1)} %get-tuple-element.78.keep_ref, bf16[656,1024]{1,0:T(8,128)(2,1)} %refs_0_.6, bf16[128,3712]{1,0:T(8,128)(2,1)} %collective-permute-done.3.refs_1_.refs_2_, ...), custom_call_target="tpu_custom_call" | custom-call | flops 4000000000 | bytes 9000000 | tf_op jit(solution)/shard_map/layer_result/pallas_call | solution.py:625
  245.1 13.1 %collective-permute-done.29 = bf16[2,32,5248]{2,1,0:T(8,128)(2,1)S(1)} collective-permute-done((bf16[2,32,5248]{2,1,0:T(8,128)(2,1)}, bf16[2,32,5248]{2,1,0:T(8,128)(2,1)S(1)}, u32[]{:S(2)}, u32[]{:S(2)}) %collective-permute-start.29) | collective-permute-done | bytes 671776 | tf_op jit(solution)/shard_map/ppermute | solution.py:70
  263.5 5.0 %collective-permute-done.31 = bf16[32,5248]{1,0:T(8,128)(2,1)S(1)} collective-permute-done((bf16[32,5248]{1,0:T(8,128)(2,1)}, bf16[32,5248]{1,0:T(8,128)(2,1)S(1)}, u32[]{:S(2)}, u32[]{:S(2)}) %collective-permute-start.31) | collective-permute-done | bytes 335904 | tf_op jit(solution)/shard_map/ppermute | solution.py:70
  270.0 7.3 %qkv_weight_grad.1 = (bf16[2,256,384]{2,1,0:T(8,128)(2,1)}, bf16[1,256,384]{2,1,0:T(8,128)(2,1)}, bf16[1,256,384]{2,1,0:T(8,128)(2,1)}) custom-call(s32[9]{0:T(128)} %stack.51.place_ref, bf16[8,256,1024]{2,1,0:T(8,128)(2,1)} %get-tuple-element.88.normed_ref, bf16[8,256,384]{2,1,0:T(8,128)(2,1)} %attention_backward.1.grad_ref), custom_call_target="tpu_custom_call" | custom-call | flops 3000000000 | bytes 6000000 | tf_op jit(solution)/shard_map/qkv_weight_grad/pallas_call | solution.py:547
  287.7 5.2 %collective-permute-done.23.refs_3_ = bf16[128,3072]{1,0:T(8,128)(2,1)S(1)} collective-permute-done((bf16[128,3072]{1,0:T(8,128)(2,1)}, bf16[128,3072]{1,0:T(8,128)(2,1)S(1)}, u32[]{:S(2)}, u32[]{:S(2)}) %collective-permute-start.23) | collective-permute-done | bytes 786464 | tf_op jit(solution)/shard_map/ppermute | solution.py:46
  300.9 11.7 %collective-permute-done.37.refs_1_ = bf16[2,32,5248]{2,1,0:T(8,128)(2,1)S(1)} collective-permute-done((bf16[2,32,5248]{2,1,0:T(8,128)(2,1)S(1)}, bf16[2,32,5248]{2,1,0:T(8,128)(2,1)S(1)}, u32[]{:S(2)}, u32[]{:S(2)}) %collective-permute-start.37) | collective-permute-done | bytes 671776 | tf_op jit(solution)/shard_map/ppermute | solution.py:70
  317.2 8.7 %input_grad.1 = bf16[256,1024]{1,0:T(8,128)(2,1)} custom-call(s32[9]{0:T(128)} %stack.51.place_ref, bf16[256,1024]{1,0:T(8,128)(2,1)} %bitcast.93, f32[256,1024]{1,0:T(8,128)} %get-tuple-element.79.gmid_ref, f32[1,1024]{1,0:T(1,128)} %get-tuple-element.112.gain_ref, bf16[8,256,384]{2,1,0:T(8,128)(2,1)} %all-to-all-done.2.g_ref, bf16[256,3072]{1,0:T(8,128)(2,1)} %refs_4_.3, ...), custom_call_target="tpu_custom_call" | custom-call | flops 4000000000 | bytes 10000000 | tf_op jit(solution)/shard_map/input_grad/pallas_call | solution.py:1075
  335.5 8.4 %unpack_in.1 = (f32[256,5248]{1,0:T(8,128)}, f32[256,1]{1,0:T(8,128)}) custom-call(s32[9]{0:T(128)} %stack.51.place_ref, bf16[2,32,5248]{2,1,0:T(8,128)(2,1)} %copy-done.1, bf16[2,32,5248]{2,1,0:T(8,128)(2,1)} %copy-done.6, bf16[2,32,5248]{2,1,0:T(8,128)(2,1)} %copy-done.7, bf16[2,32,5248]{2,1,0:T(8,128)(2,1)} %copy-done.8, bf16[256,5248]{1,0:T(8,128)(2,1)} %refs_4_.2), custom_call_target="tpu_custom_call" | custom-call | flops 10000000 | bytes 11000000 | tf_op jit(solution)/shard_map/unpack_in/pallas_call | solution.py:961
  343.9 10.2 %collective-permute-start.43 = (bf16[2,912,128]{2,1,0:T(8,128)(2,1)S(1)}, bf16[2,912,128]{2,1,0:T(8,128)(2,1)S(1)}, u32[]{:S(2)}, u32[]{:S(2)}) collective-permute-start(bf16[2,912,128]{2,1,0:T(8,128)(2,1)S(1)} %pad_maximum_fusion.1.refs_0_), channel_id=1, source_target_pairs={{0,4},{4,0},{8,12},{12,8},{16,20},{20,16},{24,28},{28,24},{1,5},{5... | collective-permute-start | bytes 1400840 | tf_op jit(solution)/shard_map/ppermute | solution.py:24
  364.4 4.4 %unpack_qkv.1 = (f32[256,3072]{1,0:T(8,128)}, f32[256,1]{1,0:T(8,128)}) custom-call(s32[9]{0:T(128)} %stack.51.place_ref, bf16[2,256,384]{2,1,0:T(8,128)(2,1)} %copy-done.3, bf16[2,256,384]{2,1,0:T(8,128)(2,1)} %collective-permute-done.34.refs_1_, bf16[2,256,384]{2,1,0:T(8,128)(2,1)} %copy-done.12, bf16[2,256,384]{2,1,0:T(8,128)(2,1)} %copy-done.13, ...), custom_call_target="tpu_custom_call" | custom-call | flops 10000000 | bytes 7000000 | tf_op jit(solution)/shard_map/unpack_qkv/pallas_call | solution.py:1027
  (198 shorter events, 95.8 us)
Async XLA Ops:
  7.2 55.3 %all-gather.2.cloned.1.call-start = ((), (), s32[]{:S(2)}) async-start(), calls=%async_computation.3 | async-start | bytes 4718592 | tf_op jit(solution)/shard_map/all_gather | solution.py:1133
  11.2 49.2 %collective-permute-start = (bf16[272,384]{1,0:T(8,128)(2,1)S(1)}, bf16[272,384]{1,0:T(8,128)(2,1)S(1)}, u32[]{:S(2)}, u32[]{:S(2)}) collective-permute-start(bf16[272,384]{1,0:T(8,128)(2,1)S(1)} %pad_maximum_fusion.3.refs_0_), channel_id=1, source_target_pairs={{0,1},{1,0},{2,3},{3,2},{4,5},{5,4},{6,7},{7,6},{8,9},{9,8},{10,11... | collective-permute-start | bytes 626696 | tf_op jit(solution)/shard_map/ppermute | solution.py:1141
  13.3 47.7 %collective-permute-start.1 = (bf16[272,384]{1,0:T(8,128)(2,1)S(1)}, bf16[272,384]{1,0:T(8,128)(2,1)S(1)}, u32[]{:S(2)}, u32[]{:S(2)}) collective-permute-start(bf16[272,384]{1,0:T(8,128)(2,1)S(1)} %pad_maximum_fusion.3.refs_0_), channel_id=1, source_target_pairs={{0,2},{1,3},{2,0},{3,1},{4,6},{5,7},{6,4},{7,5},{8,10},{9,11},{10,... | collective-permute-start | bytes 626696 | tf_op jit(solution)/shard_map/ppermute | solution.py:1141
  14.6 47.7 %collective-permute-start.2 = (bf16[272,384]{1,0:T(8,128)(2,1)S(1)}, bf16[272,384]{1,0:T(8,128)(2,1)S(1)}, u32[]{:S(2)}, u32[]{:S(2)}) collective-permute-start(bf16[272,384]{1,0:T(8,128)(2,1)S(1)} %pad_maximum_fusion.3.refs_0_), channel_id=1, source_target_pairs={{0,3},{1,2},{2,1},{3,0},{4,7},{5,6},{6,5},{7,4},{8,11},{9,10},{10,... | collective-permute-start | bytes 626696 | tf_op jit(solution)/shard_map/ppermute | solution.py:1141
  20.6 38.9 %collective-permute-start.9 = (bf16[128,5248]{1,0:T(8,128)(2,1)}, bf16[128,5248]{1,0:T(8,128)(2,1)S(1)}, u32[]{:S(2)}, u32[]{:S(2)}) collective-permute-start(bf16[128,5248]{1,0:T(8,128)(2,1)} %get-tuple-element.65), channel_id=1, source_target_pairs={{0,1},{1,0},{2,3},{3,2},{4,6},{5,7},{6,4},{7,5},{8,9},{9,8},{10,11... | collective-permute-start | bytes 4030472 | tf_op jit(solution)/shard_map/ppermute | solution.py:46
  35.3 59.9 %collective-permute-start.4 = (bf16[128,3712]{1,0:T(8,128)(2,1)}, bf16[128,3712]{1,0:T(8,128)(2,1)}, u32[]{:S(2)}, u32[]{:S(2)}) collective-permute-start(bf16[128,3712]{1,0:T(8,128)(2,1)} %get-tuple-element.61), channel_id=1, source_target_pairs={{0,2},{1,3},{2,0},{3,1},{4,5},{5,4},{6,7},{7,6},{8,10},{9,11},{10,... | collective-permute-start | bytes 2850824 | tf_op jit(solution)/shard_map/ppermute | solution.py:46
  59.5 36.0 %collective-permute-start.5 = (bf16[128,3712]{1,0:T(8,128)(2,1)}, bf16[128,3712]{1,0:T(8,128)(2,1)}, u32[]{:S(2)}, u32[]{:S(2)}) collective-permute-start(bf16[128,3712]{1,0:T(8,128)(2,1)} %collective-permute-done.3.refs_1_.refs_2_), channel_id=1, source_target_pairs={{0,2},{1,3},{2,0},{3,1},{4,5},{5,4},{6,7},{7,6},{8,10},{9,11},{10,... | collective-permute-start | bytes 2850824 | tf_op jit(solution)/shard_map/ppermute | solution.py:46
  60.4 40.5 %collective-permute-start.6 = (bf16[128,3712]{1,0:T(8,128)(2,1)}, bf16[128,3712]{1,0:T(8,128)(2,1)}, u32[]{:S(2)}, u32[]{:S(2)}) collective-permute-start(bf16[128,3712]{1,0:T(8,128)(2,1)} %collective-permute-done.3.refs_1_.refs_2_), channel_id=1, source_target_pairs={{0,4},{4,0},{8,12},{12,8},{16,20},{20,16},{24,28},{28,24},{1,5},{5... | collective-permute-start | bytes 2850824 | tf_op jit(solution)/shard_map/ppermute | solution.py:24
  61.0 49.0 %collective-permute-start.10 = (bf16[128,5248]{1,0:T(8,128)(2,1)}, bf16[128,5248]{1,0:T(8,128)(2,1)}, u32[]{:S(2)}, u32[]{:S(2)}) collective-permute-start(bf16[128,5248]{1,0:T(8,128)(2,1)} %get-tuple-element.65), channel_id=1, source_target_pairs={{0,2},{1,3},{2,0},{3,1},{4,5},{5,4},{6,7},{7,6},{8,10},{9,11},{10,... | collective-permute-start | bytes 4030472 | tf_op jit(solution)/shard_map/ppermute | solution.py:46
  62.2 54.1 %collective-permute-start.11 = (bf16[128,5248]{1,0:T(8,128)(2,1)S(1)}, bf16[128,5248]{1,0:T(8,128)(2,1)S(1)}, u32[]{:S(2)}, u32[]{:S(2)}) collective-permute-start(bf16[128,5248]{1,0:T(8,128)(2,1)S(1)} %collective-permute-done.9.refs_8_), channel_id=1, source_target_pairs={{0,2},{1,3},{2,0},{3,1},{4,5},{5,4},{6,7},{7,6},{8,10},{9,11},{10,... | collective-permute-start | bytes 4030472 | tf_op jit(solution)/shard_map/ppermute | solution.py:46
  153.5 53.1 %collective-permute-start.15 = (bf16[256,5760]{1,0:T(8,128)(2,1)}, bf16[256,5760]{1,0:T(8,128)(2,1)}, u32[]{:S(2)}, u32[]{:S(2)}) collective-permute-start(bf16[256,5760]{1,0:T(8,128)(2,1)} %get-tuple-element.78.keep_ref), channel_id=1, source_target_pairs={{0,4},{4,0},{8,12},{12,8},{16,20},{20,16},{24,28},{28,24},{1,5},{5... | collective-permute-start | bytes 8847368 | tf_op jit(solution)/shard_map/ppermute | solution.py:24
  162.8 43.8 %collective-permute-start.17 = (bf16[128,3072]{1,0:T(8,128)(2,1)S(1)}, bf16[128,3072]{1,0:T(8,128)(2,1)}, u32[]{:S(2)}, u32[]{:S(2)}) collective-permute-start(bf16[128,3072]{1,0:T(8,128)(2,1)S(1)} %constant_dynamic-slice_fusion), channel_id=1, source_target_pairs={{0,1},{1,0},{2,3},{3,2},{4,6},{5,7},{6,4},{7,5},{8,9},{9,8},{10,11... | collective-permute-start | bytes 2359304 | tf_op jit(solution)/shard_map/ppermute | solution.py:46
  162.8 43.8 %collective-permute-start.18 = (bf16[128,3072]{1,0:T(8,128)(2,1)S(1)}, bf16[128,3072]{1,0:T(8,128)(2,1)}, u32[]{:S(2)}, u32[]{:S(2)}) collective-permute-start(bf16[128,3072]{1,0:T(8,128)(2,1)S(1)} %constant_dynamic-slice_fusion), channel_id=1, source_target_pairs={{0,2},{1,3},{2,0},{3,1},{4,5},{5,4},{6,7},{7,6},{8,10},{9,11},{10,... | collective-permute-start | bytes 2359304 | tf_op jit(solution)/shard_map/ppermute | solution.py:46
  165.0 47.0 %collective-permute-start.19 = (bf16[2,128,5248]{2,1,0:T(8,128)(2,1)}, bf16[2,128,5248]{2,1,0:T(8,128)(2,1)S(1)}, u32[]{:S(2)}, u32[]{:S(2)}) collective-permute-start(bf16[2,128,5248]{2,1,0:T(8,128)(2,1)} %get-tuple-element.75), channel_id=1, source_target_pairs={{0,2},{1,3},{2,0},{3,1},{4,5},{5,4},{6,7},{7,6},{8,10},{9,11},{10,... | collective-permute-start | bytes 8060936 | tf_op jit(solution)/shard_map/ppermute | solution.py:46
  201.6 58.8 %all-to-all-start.2 = ((bf16[8,256,384]{2,1,0:T(8,128)(2,1)}), bf16[8,256,384]{2,1,0:T(8,128)(2,1)}, u32[]{:S(2)}, u32[]{:S(2)}) async-start(bf16[8,256,384]{2,1,0:T(8,128)(2,1)} %attention_backward.1.grad_ref), calls=%async_computation.2 | async-start | bytes 3145728 | tf_op jit(solution)/shard_map/all_to_all | solution.py:1187
  234.2 23.9 %collective-permute-start.29 = (bf16[2,32,5248]{2,1,0:T(8,128)(2,1)}, bf16[2,32,5248]{2,1,0:T(8,128)(2,1)S(1)}, u32[]{:S(2)}, u32[]{:S(2)}) collective-permute-start(bf16[2,32,5248]{2,1,0:T(8,128)(2,1)} %fusion.1), channel_id=1, source_target_pairs={{0,8},{4,20},{8,0},{12,28},{16,24},{20,4},{24,16},{28,12},{1,9},{5... | collective-permute-start | bytes 2015240 | tf_op jit(solution)/shard_map/ppermute | solution.py:70
  236.6 24.3 %collective-permute-start.21 = (bf16[2,4,912,128]{3,2,1,0:T(8,128)(2,1)}, bf16[2,4,912,128]{3,2,1,0:T(8,128)(2,1)}, u32[]{:S(2)}, u32[]{:S(2)}) collective-permute-start(bf16[2,4,912,128]{3,2,1,0:T(8,128)(2,1)} %get-tuple-element.86), channel_id=1, source_target_pairs={{0,2},{1,3},{2,0},{3,1},{4,5},{5,4},{6,7},{7,6},{8,10},{9,11},{10,... | collective-permute-start | bytes 5603336 | tf_op jit(solution)/shard_map/ppermute | solution.py:46
  260.4 55.5 %collective-permute-start.24 = (bf16[128,3072]{1,0:T(8,128)(2,1)}, bf16[128,3072]{1,0:T(8,128)(2,1)}, u32[]{:S(2)}, u32[]{:S(2)}) collective-permute-start(bf16[128,3072]{1,0:T(8,128)(2,1)} %collective-permute-done.17.refs_1_), channel_id=1, source_target_pairs={{0,4},{4,0},{8,12},{12,8},{16,20},{20,16},{24,28},{28,24},{1,5},{5... | collective-permute-start | bytes 2359304 | tf_op jit(solution)/shard_map/ppermute | solution.py:24
  260.4 55.9 %collective-permute-start.25 = (bf16[128,3072]{1,0:T(8,128)(2,1)}, bf16[128,3072]{1,0:T(8,128)(2,1)}, u32[]{:S(2)}, u32[]{:S(2)}) collective-permute-start(bf16[128,3072]{1,0:T(8,128)(2,1)} %collective-permute-done.18.refs_2_), channel_id=1, source_target_pairs={{0,4},{4,0},{8,12},{12,8},{16,20},{20,16},{24,28},{28,24},{1,5},{5... | collective-permute-start | bytes 2359304 | tf_op jit(solution)/shard_map/ppermute | solution.py:24
  284.5 28.0 %collective-permute-start.37 = (bf16[2,32,5248]{2,1,0:T(8,128)(2,1)S(1)}, bf16[2,32,5248]{2,1,0:T(8,128)(2,1)S(1)}, u32[]{:S(2)}, u32[]{:S(2)}) collective-permute-start(bf16[2,32,5248]{2,1,0:T(8,128)(2,1)S(1)} %pad_maximum_fusion.refs_0_), channel_id=1, source_target_pairs={{0,8},{4,20},{8,0},{12,28},{16,24},{20,4},{24,16},{28,12},{1,9},{5... | collective-permute-start | bytes 2015240 | tf_op jit(solution)/shard_map/ppermute | solution.py:70
  292.9 23.4 %collective-permute-start.26 = (bf16[128,3072]{1,0:T(8,128)(2,1)S(1)}, bf16[128,3072]{1,0:T(8,128)(2,1)S(1)}, u32[]{:S(2)}, u32[]{:S(2)}) collective-permute-start(bf16[128,3072]{1,0:T(8,128)(2,1)S(1)} %collective-permute-done.23.refs_3_), channel_id=1, source_target_pairs={{0,4},{4,0},{8,12},{12,8},{16,20},{20,16},{24,28},{28,24},{1,5},{5... | collective-permute-start | bytes 2359304 | tf_op jit(solution)/shard_map/ppermute | solution.py:24
  312.5 21.3 %collective-permute-start.38 = (bf16[2,32,5248]{2,1,0:T(8,128)(2,1)S(1)}, bf16[2,32,5248]{2,1,0:T(8,128)(2,1)S(1)}, u32[]{:S(2)}, u32[]{:S(2)}) collective-permute-start(bf16[2,32,5248]{2,1,0:T(8,128)(2,1)S(1)} %pad_maximum_fusion.refs_0_), channel_id=1, source_target_pairs={{0,4},{4,0},{8,12},{12,8},{16,20},{20,16},{24,28},{28,24},{1,5},{5... | collective-permute-start | bytes 2015240 | tf_op jit(solution)/shard_map/ppermute | solution.py:24
  327.1 27.1 %collective-permute-start.42 = (bf16[2,912,128]{2,1,0:T(8,128)(2,1)S(1)}, bf16[2,912,128]{2,1,0:T(8,128)(2,1)}, u32[]{:S(2)}, u32[]{:S(2)}) collective-permute-start(bf16[2,912,128]{2,1,0:T(8,128)(2,1)S(1)} %pad_maximum_fusion.1.refs_0_), channel_id=1, source_target_pairs={{0,8},{4,20},{8,0},{12,28},{16,24},{20,4},{24,16},{28,12},{1,9},{5... | collective-permute-start | bytes 1400840 | tf_op jit(solution)/shard_map/ppermute | solution.py:70
  330.6 24.1 %collective-permute-start.34 = (bf16[2,256,384]{2,1,0:T(8,128)(2,1)S(1)}, bf16[2,256,384]{2,1,0:T(8,128)(2,1)}, u32[]{:S(2)}, u32[]{:S(2)}) collective-permute-start(bf16[2,256,384]{2,1,0:T(8,128)(2,1)S(1)} %pad_maximum_fusion.2.refs_0_), channel_id=1, source_target_pairs={{0,8},{4,20},{8,0},{12,28},{16,24},{20,4},{24,16},{28,12},{1,9},{5... | collective-permute-start | bytes 1179656 | tf_op jit(solution)/shard_map/ppermute | solution.py:70
  (59 other events, 683.4 us)
Sparse Core Ops, SparseCore 0:
  9.6 49.6 all-gather.1

commit v4 on v3

--- a/solution.py
+++ b/solution.py
@@ -223,18 +223,26 @@
 
 
 def attention_forward(
-    seq_count, heads, group, low_ref, high_ref, place_ref, x_hbm, order_ref, start_ref, end_ref,
+    seq_count, heads, group, low_ref, high_ref, place_ref, order_ref, start_ref, end_ref,
     cos_ref, sin_ref, *refs,
 ):
+    x_hbm, refs = (refs[:1], refs[1:]) if len(refs[0].shape) == 3 else (refs[:seq_count], refs[seq_count:])
     pieces, refs = refs[:-15], refs[-15:]
-    gains_ref, normed_hbm, packed_ref, att_ref, out_ref, lse_ref = refs[:6]
-    w_ref, x_ref, normed_ref, qkv_t, k_rows, o_rows, scores_ref, x_sems, normed_sems = refs[6:15]
+    gains_ref, w_ref, normed_hbm, packed_ref, att_ref, out_ref, lse_ref = refs[:7]
+    x_ref, normed_ref, qkv_t, k_rows, o_rows, scores_ref, x_sems, normed_sems = refs[7:]
     width = heads * HD
     rows = group // seq_count
     blocks = group // BLOCK
-    fetches = [pltpu.make_async_copy(x_hbm.at[i], x_ref.at[i], x_sems.at[i]) for i in range(seq_count)]
+    if len(x_hbm) == 1:
+        chunks = list(range(seq_count))
+        x_hbm = [x_hbm[0].at[i] for i in chunks]
+    else:
+        core, z = place_ref[7], place_ref[8]
+        chunks = [(z ^ k) * 2 + side for side in (core, 1 - core) for k in block_order(side)]
+    fetches = [pltpu.make_async_copy(x_hbm[i], x_ref.at[i], x_sems.at[i]) for i in range(seq_count)]
     stores = [
-        pltpu.make_async_copy(normed_ref.at[i], normed_hbm.at[i], normed_sems.at[i]) for i in range(seq_count)
+        pltpu.make_async_copy(normed_ref.at[i], normed_hbm.at[chunks[i]], normed_sems.at[i])
+        for i in range(seq_count)
     ]
     for fetch in fetches:
         fetch.start()
@@ -243,8 +251,8 @@
         gains_ref[...] = pieces[1][...]
     else:
         tall = w_ref.shape[0] // len(pieces)
-        for mask, piece in enumerate(pieces):
-            base = pl.multiple_of((place_ref[0] ^ mask) * tall, 128)
+        for key, piece in enumerate(pieces):
+            base = pl.multiple_of(place_ref[key] * tall, 128)
             w_ref[pl.ds(base, tall), :] = piece[:tall]
             gains_ref[:, pl.ds(base, tall)] = piece[tall : tall + 2, :tall].astype(F32)
     gain_ref = gains_ref.at[pl.ds(0, 1), :]
@@ -256,7 +264,7 @@
         normed = (center * lax.rsqrt(spread + NORM_EPS) * gain_ref[...]).astype(BF16)
         normed_ref[i] = normed
         qkv = nn_dot(normed, w_ref[...]).astype(BF16)
-        qkv_t[i] = qkv.T
+        qkv_t[chunks[i]] = qkv.T
 
     for i in range(seq_count):
         fetches[i].wait()
@@ -351,9 +359,10 @@
         store.wait()
 
 
-def run_attention_forward(place, x_all, pieces, layout, heads):
-    seq_count, rows, dim = x_all.shape
-    group = seq_count * rows
+def run_attention_forward(place, chunks, pieces, layout, heads):
+    rows, dim = chunks[0].shape[-2:]
+    group = layout[2].shape[1]
+    seq_count = group // rows
     width = heads * HD
     (low, high), _, order, start, end, cos, sin = layout
     return pl.pallas_call(
@@ -361,16 +370,16 @@
         name="attention_forward",
         out_shape=(
             jax.ShapeDtypeStruct((2, dim), F32),
+            jax.ShapeDtypeStruct((dim, 3 * width), BF16),
             jax.ShapeDtypeStruct((seq_count, rows, dim), BF16),
             jax.ShapeDtypeStruct((3 * width, group), BF16),
             jax.ShapeDtypeStruct((seq_count, rows, width), BF16),
             jax.ShapeDtypeStruct((width, group), F32),
             jax.ShapeDtypeStruct((heads, group), F32),
         ),
-        in_specs=[smem_spec()] * 3 + [any_spec()] + [vmem_spec()] * (5 + len(pieces)),
-        out_specs=[vmem_spec(), any_spec()] + [vmem_spec()] * 4,
+        in_specs=[smem_spec()] * 3 + [vmem_spec()] * 5 + [any_spec()] * len(chunks) + [vmem_spec()] * len(pieces),
+        out_specs=[vmem_spec()] * 2 + [any_spec()] + [vmem_spec()] * 4,
         scratch_shapes=[
-            pltpu.VMEM((dim, 3 * width), BF16),
             pltpu.VMEM((seq_count, rows, dim), BF16),
             pltpu.VMEM((seq_count, rows, dim), BF16),
             pltpu.VMEM((seq_count, 3 * width, rows), BF16),
@@ -382,14 +391,15 @@
         ],
         compiler_params=params(),
         cost_estimate=cost(24e9, 20e6),
-    )(low, high, place, x_all, order, start, end, cos, sin, *pieces)
+    )(low, high, place, order, start, end, cos, sin, *chunks, *pieces)
 
 
 def attention_backward(
-    seq_count, heads, group, low_ref, high_ref, dout_ref, packed_ref, out_ref, lse_ref, order_ref,
-    start_ref, end_ref, cos_ref, sin_ref, grad_ref, dout_t, dpack_t, drows, qrows, krows, vrows,
-    delta_ref, dq_t, grows,
+    seq_count, heads, group, low_ref, high_ref, place_ref, dout_ref, packed_ref, out_ref, lse_ref, order_ref,
+    start_ref, end_ref, cos_ref, sin_ref, w_ref, grad_ref, *refs,
 ):
+    shares, refs = refs[:-9], refs[-9:]
+    dout_t, dpack_t, drows, qrows, krows, vrows, delta_ref, dq_t, grows = refs
     width = heads * HD
     rows = group // seq_count
     blocks = group // BLOCK
@@ -482,25 +492,44 @@
 
     lax.fori_loop(0, blocks, finish, 0)
 
-    def arrive(i, carry):
+    def arrive(i):
         here = lax.broadcasted_iota(jnp.int32, (rows, group), 0) + i * rows
         hot = jnp.where(here == order_ref[...], 1.0, 0.0).astype(BF16)
-        grad_ref[i] = nn_dot(hot, grows[...]).astype(BF16)
-        return carry
-
-    lax.fori_loop(0, seq_count, arrive, 0)
-
-
-def run_attention_backward(dout, packed, out_t, lse, layout, heads):
+        grad = nn_dot(hot, grows[...]).astype(BF16)
+        grad_ref[i] = grad
+        return nt_dot(grad, w_ref[...]).astype(BF16)
+
+    if len(shares) == 1:
+
+        def each(i, carry):
+            shares[0][i] = arrive(i)
+            return carry
+
+        lax.fori_loop(0, seq_count, each, 0)
+    else:
+        for side, share in zip((1 - place_ref[7], place_ref[7]), shares):
+
+            def each(j, carry, side=side, share=share):
+                k = jnp.where(j == 1, 2 - side, jnp.where(j == 2, 1 + side, j))
+                share[j] = arrive((place_ref[8] ^ k) * 2 + side)
+                return carry
+
+            lax.fori_loop(0, seq_count // 2, each, 0)
+
+
+def run_attention_backward(place, dout, packed, out_t, lse, w_heads, layout, heads, regular):
     seq_count, rows, width = dout.shape
     group = seq_count * rows
+    dim = w_heads.shape[0]
     _, (low, high), order, start, end, cos, sin = layout
+    shares = [seq_count // 2] * 2 if regular else [seq_count]
     return pl.pallas_call(
         functools.partial(attention_backward, seq_count, heads, group),
         name="attention_backward",
-        out_shape=jax.ShapeDtypeStruct((seq_count, rows, 3 * width), BF16),
-        in_specs=[smem_spec()] * 2 + [vmem_spec()] * 9,
-        out_specs=vmem_spec(),
+        out_shape=[jax.ShapeDtypeStruct((seq_count, rows, 3 * width), BF16)]
+        + [jax.ShapeDtypeStruct((share, rows, dim), BF16) for share in shares],
+        in_specs=[smem_spec()] * 3 + [vmem_spec()] * 10,
+        out_specs=[vmem_spec()] * (1 + len(shares)),
         scratch_shapes=[
             pltpu.VMEM((seq_count, width, rows), BF16),
             pltpu.VMEM((width, group), BF16),
@@ -513,8 +542,8 @@
             pltpu.VMEM((group, 3 * width), BF16),
         ],
         compiler_params=params(),
-        cost_estimate=cost(30e9, 10e6),
-    )(low, high, dout, packed, out_t, lse, order, start, end, cos, sin)
+        cost_estimate=cost(33e9, 15e6),
+    )(low, high, place, dout, packed, out_t, lse, order, start, end, cos, sin, w_heads)
 
 
 def qkv_weight_grad(seq_count, place_ref, normed_ref, grad_ref, *refs):
@@ -1038,55 +1067,32 @@
     )(place, *pieces, weight)
 
 
-def input_grad(count, place_ref, x_ref, gmid_ref, gain_ref, g_ref, *refs):
-    weights, (out_ref, full, grad, total, sems) = refs[:-5], refs[-5:]
-    seq_count, _, width = g_ref.shape
-    width //= 3
-    dim = x_ref.shape[1]
-    copies = row_copies(place_ref, weights[0], weights[1 : 1 + count], weights[1 + count :], 0, full, sems)
-    for copy in copies:
-        copy.start()
-    grad[...] = jnp.concatenate(
-        [g_ref[s][:, part * width : (part + 1) * width] for part in range(3) for s in range(seq_count)],
-        axis=1,
-    )
-    for copy in copies:
-        copy.wait()
-
-    def step(i, carry):
-        at = pl.multiple_of(i * 256, 256)
-        total[:, pl.ds(at, 256)] = nt_dot(grad[...], full[pl.ds(at, 256), :])
-        return carry
-
-    lax.fori_loop(0, dim // 256, step, 0)
+def input_grad(x_ref, gmid_ref, gain_ref, *refs):
+    parts, out_ref = refs[:-1], refs[-1]
     x = x_ref[...].astype(F32)
     center = x - jnp.mean(x, axis=-1, keepdims=True)
     spread = jnp.mean(center * center, axis=-1, keepdims=True)
     scale = lax.rsqrt(spread + NORM_EPS)
     normal = center * scale
-    e = total[...] * gain_ref[...]
+    e = sum(part[...].astype(F32) for part in parts) * gain_ref[...]
     pull = e - jnp.mean(e, axis=-1, keepdims=True) - normal * jnp.mean(e * normal, axis=-1, keepdims=True)
     out_ref[...] = (gmid_ref[...] + scale * pull).astype(BF16)
 
 
-def run_input_grad(place, x, gmid, gain, grads, weights, count):
+def run_input_grad(x, gmid, gain, parts):
     rows, dim = x.shape
-    columns = weights[0].shape[1]
+    tall = rows // 4
+    block = pl.BlockSpec((tall, dim), lambda i: (i, 0))
     return pl.pallas_call(
-        functools.partial(input_grad, count),
+        input_grad,
         name="input_grad",
         out_shape=jax.ShapeDtypeStruct((rows, dim), BF16),
-        in_specs=[smem_spec()] + [vmem_spec()] * 4 + [any_spec()] * len(weights),
-        out_specs=vmem_spec(),
-        scratch_shapes=[
-            pltpu.VMEM((dim, columns), BF16),
-            pltpu.VMEM((rows, columns), BF16),
-            pltpu.VMEM((rows, dim), F32),
-            pltpu.SemaphoreType.DMA((2 * count + 1,)),
-        ],
+        grid=(4,),
+        in_specs=[block, block, pl.BlockSpec((1, dim), lambda i: (0, 0))] + [block] * len(parts),
+        out_specs=block,
         compiler_params=params(),
-        cost_estimate=cost(4e9, 10e6),
-    )(place, x, gmid, gain, grads, *weights)
+        cost_estimate=cost(1e8, 5e6),
+    )(x, gmid, gain, *parts)
 
 
 def sequence_layout(lengths, order, group):
@@ -1130,31 +1136,37 @@
     place = jnp.stack([fsdp_at, *mine, *other, core, seq_at // 2]).astype(jnp.int32)
     regular = fsdp_count == 4 and seq_count == 8 and w_down.shape[0] % 16 == 0 and dim == 1024
 
-    x_all = lax.all_gather(x, "seq", axis=0, tiled=False)
-    own_heads = lax.dynamic_slice_in_dim(w_qkv.reshape(w_qkv.shape[0], 3, dim), seq_at * width, width, 2)
-    own_heads = own_heads.reshape(w_qkv.shape[0], 3 * width)
+    if regular:
+        chunks = [x, line_swap(x, 1, seq_count), line_swap(x, 0, seq_count)]
+        chunks.append(line_swap(after(chunks[1], chunks[2]), 0, seq_count))
+        chunks += [swap(chunk) for chunk in chunks]
+    else:
+        chunks = [lax.all_gather(x, "seq", axis=0, tiled=False)]
+    own_heads = jnp.concatenate(
+        [lax.dynamic_slice_in_dim(w_qkv, part * dim + seq_at * width, width, 1) for part in range(3)], axis=1
+    )
     gains = jnp.stack([norm_one, norm_two])
     if regular:
         extra = jnp.pad(gains, ((0, 14), (0, 3 * width - gains.shape[1])))
         own_heads = jnp.concatenate([own_heads, extra], axis=0)
-        head_pieces = [own_heads] + [
-            lax.ppermute(own_heads, "fsdp", [(f, f ^ mask) for f in range(4)]) for mask in (1, 2, 3)
-        ]
+        head_pieces = [own_heads] + [plane_swap(own_heads, phase, *counts) for phase in range(2)]
+        head_pieces.append(plane_swap(head_pieces[1], 1, *counts))
     else:
         head_pieces = [
             lax.all_gather(own_heads, "fsdp", axis=0, tiled=True),
             lax.all_gather(gains, "fsdp", axis=1, tiled=True).astype(F32),
         ]
     first_piece, second_piece = run_pack_pieces(place, w_in, w_out, w_down, regular)
+    if regular:
+        first_piece, second_piece = after(first_piece, *head_pieces[1:3]), after(second_piece, *head_pieces[1:])
     first_a, second_a = plane_swap(first_piece, 0, *counts), plane_swap(second_piece, 0, *counts)
-    first = plane_gather_rest(first_piece, first_a, *counts)
+    first = plane_gather_rest(first_piece, first_a, *counts, second_a)
     second = plane_gather_rest(second_piece, second_a, *counts, first_a)
     left = dim
 
     layout = sequence_layout(seq_lengths[0], seq_order[0], group)
-    gains, normed, packed, att, out_t, lse = run_attention_forward(place, x_all, head_pieces, layout, heads)
+    gains, w_heads, normed, packed, att, out_t, lse = run_attention_forward(place, chunks, head_pieces, layout, heads)
     gain_one, gain_two = gains[:1], gains[1:]
-    qkv_piece = lax.dynamic_slice_in_dim(w_qkv, core * (w_qkv.shape[0] // 2), w_qkv.shape[0] // 2, 0)
     att_done = lax.all_to_all(att, "seq", split_axis=0, concat_axis=0, tiled=True)
     first = first + [swap(first[0])] + [swap(after(piece, att)) for piece in first[1:]]
     if regular:
@@ -1174,55 +1186,49 @@
     if regular:
         short = w_in.shape[0] // 8
         in_a, in_b, in_c = run_in_grad(place, send, send_other, hidden)
-        dout = after(dout, in_b)
         in_a = plane_swap(in_a, 1, *counts)
-        in_sum = added(in_b[0], in_a[1])
-    else:
-        in_b = in_sum = gatt
-    qkv_piece = after(qkv_piece, in_b)
-    qkv_mine = {1 << phase: plane_swap(qkv_piece, phase, *counts) for phase in range(levels)}
-    keep_other = after(keep_other, *qkv_mine.values())
-
-    grads = run_attention_backward(dout, packed, out_t, lse, layout, heads)
-    grad_rows = lax.all_to_all(grads, "seq", split_axis=0, concat_axis=0, tiled=True)
-    gw_heads = run_qkv_weight_grad(place, normed, after(grads, in_sum), regular)
+        packed = after(packed, in_b)
+
+    grads, *shares = run_attention_backward(place, dout, packed, out_t, lse, w_heads, layout, heads, regular)
     each = w_qkv.shape[0]
-    qkv_rest = in_sum
     if regular:
+        in_sum = after(added(in_b[0], in_a[1]), grads)
         in_second = plane_swap(in_sum, 0, *counts)
+        got, share = swap(shares[0]), shares[1]
+        token_sum = added(share[2:], got[2:])
+        token_z1 = line_swap(token_sum, 0, seq_count)
+        rest_a, rest_b, rest_c = run_rest_grad(place, keep, after(keep_other, in_sum, token_sum), hidden)
+        rest_a = plane_swap(rest_a, 1, *counts)
+        gw_heads = run_qkv_weight_grad(place, normed, after(grads, rest_b), regular)
         in_parts = [p.reshape(4, short, 2 * hidden) for p in (in_c[0], in_a[0], in_second)]
-        rest_a, rest_b, rest_c = run_rest_grad(place, keep, after(keep_other, in_sum), hidden)
-        in_z1 = line_swap(after(added(*(p[2:] for p in in_parts)), rest_b), 0, seq_count)
-        layer_out = run_layer_result(place, middle, after(keep, rest_b), downs, left, hidden)
-        rest_parts = reduce(plane_swap(after(rest_a, in_second), 1, *counts), rest_b, rest_c)
-        qkv_rest = rest_parts[2]
-    else:
-        layer_out = run_layer_result(place, middle, keep, downs, left, hidden)
-    for phase in range(1, levels):
-        for key in range(1, 1 << phase):
-            qkv_mine[key + (1 << phase)] = plane_swap(after(qkv_mine[key], qkv_rest), phase, *counts)
-    qkv_mine = [qkv_mine[key] for key in range(1, fsdp_count)]
-    qkvs = [w_qkv] + qkv_mine + [swap(p) for p in qkv_mine]
-    grad_tokens = run_input_grad(place, x, gmid, gain_one, grad_rows, qkvs, count)
-    if regular:
+        in_z1 = line_swap(after(added(*(p[2:] for p in in_parts)), gw_heads[1]), 0, seq_count)
+        rest_sum = added(rest_b[0], rest_a[1])
+        rest_second = plane_swap(rest_sum, 0, *counts)
+        rest_parts = (rest_c[0], rest_a[0], rest_second)
+        layer_out = run_layer_result(place, middle, after(keep, rest_sum), downs, left, hidden)
+        token_z2 = line_swap(added(share[1], got[1], token_z1[1]), 1, seq_count)
+        grad_tokens = run_input_grad(x, gmid, gain_one, [share[0], got[0], token_z1[0], token_z2])
         qkv_a, qkv_b, qkv_c = gw_heads
-        qkv_a = plane_swap(after(qkv_a, rest_parts[1]), 1, *counts)
+        qkv_a = plane_swap(after(qkv_a, rest_second), 1, *counts)
         qkv_block = added(*reduce(qkv_a, qkv_b, qkv_c))
-        in_sum = after(added(*(p[1] for p in in_parts), in_z1[1]), grad_rows, layer_out)
-        in_z2 = line_swap(in_sum, 1, seq_count)
-        in_block = added(*(p[0] for p in in_parts), in_z1[0], in_z2)
-        rest_z1 = line_swap(after(added(*(p[2:] for p in rest_parts)), in_z1), 0, seq_count)
+        in_z2 = line_swap(added(*(p[1] for p in in_parts), in_z1[1]), 1, seq_count)
+        in_block = after(added(*(p[0] for p in in_parts), in_z1[0], in_z2), layer_out)
+        rest_z1 = line_swap(after(added(*(p[2:] for p in rest_parts)), token_z2), 0, seq_count)
         rest_z2 = line_swap(after(added(*(p[1] for p in rest_parts), rest_z1[1]), in_z2), 1, seq_count)
         rest_block = added(*(p[0] for p in rest_parts), rest_z1[0], rest_z2)
         in_pieces = line_gather(in_block, seq_count)
         gw_in, sum_in = run_unpack_in(place, in_pieces, w_in)
         rest_pieces = line_gather(rest_block, seq_count, sum_in)
-        qkv_pieces = line_gather(after(qkv_block, rest_z2, grad_tokens), seq_count, sum_in)
+        qkv_pieces = line_gather(after(qkv_block, grad_tokens), seq_count, sum_in)
         gw_qkv, sum_qkv = run_unpack_qkv(place, qkv_pieces, w_qkv)
         gw_out, gw_down = run_unpack_rest(place, rest_pieces, w_out.shape, w_down.shape)
         sum_qkv = sum_qkv[:, 0]
         sum_in = sum_in[:, 0]
     else:
+        layer_out = run_layer_result(place, middle, keep, downs, left, hidden)
+        gw_heads = run_qkv_weight_grad(place, normed, grads, regular)
+        share = lax.psum_scatter(shares[0].astype(F32), "seq", scatter_dimension=0, tiled=False)
+        grad_tokens = run_input_grad(x, gmid, gain_one, [share])
 
         def total(left_rows, right_rows):
             full = lax.dot_general(

time: 381 us -> 371 us (0.974)
  waiting for transfers between devices: 99.4 us -> 80 us
  starting transfers between devices: 64.6 us -> 80.4 us
  between operations: 14.5 us -> 1.14 us
  local copies, waits for them, and re-layouts: 14.7 us -> 19 us
    ppermute x15, waiting for transfers between devices: 55.4 us -> 12.6 us  [plane_swap(): return lax.ppermute(value, AXES, pairs)]
    ppermute x17 -> x19, starting transfers between devices: 17.5 us -> 46.9 us  [core_swap(): return lax.ppermute(value, 'seq', [(i, i ^ 1) for i in range(seq_count)])]
    ppermute x10 -> x15, waiting for transfers between devices: 31.5 us -> 50.2 us  [line_swap(): lax.ppermute(value, 'seq', [(i, i ^ 2 << (level ^ i & 1)) for i in range(...]
    all_to_all x1 -> x0, starting transfers between devices: 5.05 us -> none  [local(): lax.all_to_all(grads, 'seq', split_axis=0, concat_axis=0, tiled=True)]
    ppermute x17 -> x19, waiting for transfers between devices: 3.87 us -> 8.66 us  [core_swap(): return lax.ppermute(value, 'seq', [(i, i ^ 1) for i in range(seq_count)])]
    squeeze x0 -> x3, local copies, waits for them, and re-layouts: none -> 4.74 us  [the longest x1 2.04 us: local(): share[0]]
    pallas_call x1, Pallas kernels: 34 us -> 38.3 us  [run_attention_backward(): pl.pallas_call(functools.partial(attention_backward, seq_count, heads, gr...]
    pallas_call x1, Pallas kernels: 8.66 us -> 4.48 us  [run_input_grad(): pl.pallas_call(input_grad, name='input_grad', out_shape=jax.ShapeDtypeStr...]
  transfers between devices with their start and end apart: 49 -> 51, of which waited for: 16 -> 17; matrix products, arithmetic and copies ran while one was open for 7% -> 9% of each run, Pallas kernels for 35% -> 37%
where the time goes in v4:
time: 371 us; the launch traced here: 369 us
  Pallas kernels  163 us (44%)
  starting transfers between devices  80.4 us (22%)
  waiting for transfers between devices  80 us (22%)
  other arithmetic  25.2 us (7%)
  local copies, waits for them, and re-layouts  19 us (5%)
    ppermute x15, waiting for transfers between devices, line_swap(): lax.ppermute(value, 'seq', [(i, i ^ 2 << (level ^ i & 1)) for i in range(...  50.2 us
    ppermute x19, starting transfers between devices, core_swap(): return lax.ppermute(value, 'seq', [(i, i ^ 1) for i in range(seq_count)])  46.9 us
    pallas_call x1, Pallas kernels, run_attention_backward(): pl.pallas_call(functools.partial(attention_backward, seq_count, heads, gr...  38.3 us
    pallas_call x1, Pallas kernels, run_attention_forward(): pl.pallas_call(functools.partial(attention_forward, seq_count, heads, gro...  33.1 us
    pallas_call x1, Pallas kernels, run_feed_forward(): pl.pallas_call(functools.partial(feed_forward, count, hidden, heads_width...  24.7 us
    convert_element_type x12, other arithmetic, added(): return sum((v.astype(F32) for v in values)).astype(BF16)  16.1 us
    ppermute x15, starting transfers between devices, line_swap(): lax.ppermute(value, 'seq', [(i, i ^ 2 << (level ^ i & 1)) for i in range(...  15 us
    ppermute x15, waiting for transfers between devices, plane_swap(): return lax.ppermute(value, AXES, pairs)  12.6 us
  transfers between devices with their start and end apart: 51, of which 17 were waited for; matrix products, arithmetic and copies ran while one was open for 9% of the time, Pallas kernels for 37%

profile of v4, /device:TPU:1, one launch (start us, length us, event | category | flops | bytes accessed | tf_op | source)
XLA Modules:
  0.0 369.0 jit_solution(9025366409393056247)
XLA Ops:
  11.5 3.8 %pack_pieces.1 = (bf16[128,3712]{1,0:T(8,128)(2,1)}, bf16[128,5248]{1,0:T(8,128)(2,1)}) custom-call(s32[9]{0:T(128)} %stack.51.place_ref, bf16[256,5248]{1,0:T(8,128)(2,1)} %refs_4_.2, bf16[256,1024]{1,0:T(8,128)(2,1)} %refs_0_.4, bf16[656,1024]{1,0:T(8,128)(2,1)} %refs_0_.5), custom_call_target="tpu_custom_call" | custom-call | flops 1000000 | bytes 5000000 | tf_op jit(solution)/shard_map/pack_pieces/pallas_call | solution.py:210
  22.2 10.6 %collective-permute-done.1.refs_2_ = bf16[256,1024]{1,0:T(8,128)(2,1)S(1)} collective-permute-done((bf16[256,1024]{1,0:T(8,128)(2,1)}, bf16[256,1024]{1,0:T(8,128)(2,1)S(1)}, u32[]{:S(2)}, u32[]{:S(2)}) %collective-permute-start.1) | collective-permute-done | bytes 524320 | tf_op jit(solution)/shard_map/ppermute | solution.py:70
  34.9 11.6 %collective-permute-done.2.refs_3_ = bf16[256,1024]{1,0:T(8,128)(2,1)} collective-permute-done((bf16[256,1024]{1,0:T(8,128)(2,1)}, bf16[256,1024]{1,0:T(8,128)(2,1)}, u32[]{:S(2)}, u32[]{:S(2)}) %collective-permute-start.2) | collective-permute-done | bytes 524320 | tf_op jit(solution)/shard_map/ppermute | solution.py:70
  54.5 33.1 %attention_forward.1 = (f32[2,1024]{1,0:T(2,128)}, bf16[1024,384]{1,0:T(8,128)(2,1)}, bf16[8,256,1024]{2,1,0:T(8,128)(2,1)}, bf16[384,2048]{1,0:T(8,128)(2,1)}, ...) custom-call(s32[4]{0:T(128)} %get-tuple-element.134.low_ref, s32[4]{0:T(128)} %get-tuple-element.133.high_ref, ...), custom_call_target="tpu_custom_call" | custom-call | flops 24000000000 | bytes 20000000 | tf_op jit(solution)/shard_map/attention_forward/pallas_call | solution.py:368
  89.0 3.8 %all-to-all-start = ((bf16[8,256,128]{2,1,0:T(8,128)(2,1)}), bf16[8,256,128]{2,1,0:T(8,128)(2,1)S(1)}, u32[]{:S(2)}, u32[]{:S(2)}) async-start(bf16[8,256,128]{2,1,0:T(8,128)(2,1)} %get-tuple-element.65), calls=%async_computation | async-start | bytes 1048576 | tf_op jit(solution)/shard_map/all_to_all | solution.py:1170
  93.2 8.9 %hidden_grad.1.gh_hbm = f32[256,2688]{1,0:T(8,128)} custom-call(s32[9]{0:T(128)} %stack.51.place_ref, bf16[256,1024]{1,0:T(8,128)(2,1)} %bitcast.113, bf16[656,1024]{1,0:T(8,128)(2,1)} %refs_0_.5, bf16[128,3712]{1,0:T(8,128)(2,1)} %copy-done.29, bf16[128,3712]{1,0:T(8,128)(2,1)} %collective-permute-done.12.refs_2_.refs_3_, ...), custom_call_target="tpu_custom_call" | custom-call | flops 4000000000 | bytes 9000000 | tf_op jit(solution)/shard_map/hidden_grad/pallas_call | solution.py:627
  102.1 5.2 %all-to-all-done.att_ref = bf16[8,256,128]{2,1,0:T(8,128)(2,1)S(1)} async-done(((bf16[8,256,128]{2,1,0:T(8,128)(2,1)}), bf16[8,256,128]{2,1,0:T(8,128)(2,1)S(1)}, u32[]{:S(2)}, u32[]{:S(2)}) %all-to-all-start) | async-done | bytes 524320 | tf_op jit(solution)/shard_map/all_to_all | solution.py:1170
  113.2 24.7 %feed_forward.1 = (f32[256,1024]{1,0:T(8,128)}, f32[256,1024]{1,0:T(8,128)}, bf16[256,6272]{1,0:T(8,128)(2,1)}, bf16[256,5760]{1,0:T(8,128)(2,1)}, bf16[8,256,128]{2,1,0:T(8,128)(2,1)}) custom-call(s32[9]{0:T(128)} %stack.51.place_ref, bf16[256,1024]{1,0:T(8,128)(2,1)} %bitcast.99, bf16[8,256,128]{2,1,0:T(8,128)(2,1)} %copy-done.12, ...), custom_call_target="tpu_custom_call" | custom-call | flops 16000000000 | bytes 24000000 | tf_op jit(solution)/shard_map/feed_forward/pallas_call | solution.py:810
  144.0 9.0 %in_grad.1 = (bf16[2,128,5248]{2,1,0:T(8,128)(2,1)}, bf16[1,128,5248]{2,1,0:T(8,128)(2,1)}, bf16[1,128,5248]{2,1,0:T(8,128)(2,1)}) custom-call(s32[9]{0:T(128)} %stack.51.place_ref, bf16[256,6272]{1,0:T(8,128)(2,1)} %get-tuple-element.81.send_ref, bf16[256,6272]{1,0:T(8,128)(2,1)} %collective-permute-done.23.other_ref), custom_call_target="tpu_custom_call" | custom-call | flops 5502926848 | bytes 10747904 | tf_op jit(solution)/shard_map/in_grad/pallas_call | solution.py:876
  157.1 38.3 %attention_backward.1 = (bf16[8,256,384]{2,1,0:T(8,128)(2,1)}, bf16[4,256,1024]{2,1,0:T(8,128)(2,1)}, bf16[4,256,1024]{2,1,0:T(8,128)(2,1)}) custom-call(s32[8]{0:T(128)} %get-tuple-element.132.low_ref, s32[8]{0:T(128)} %get-tuple-element.131.high_ref, s32[9]{0:T(128)} %stack.51.place_ref, bf16[8,256,128]{2,1,0:T(8,128)(2,1)} %copy-done.13, ...), custom_call_target="tpu_custom_call" | custom-call | flops 32999999488 | bytes 15000000 | tf_op jit(solution)/shard_map/attention_backward/pallas_call | solution.py:526
  198.4 4.2 %collective-permute-done.25 = bf16[4,256,1024]{2,1,0:T(8,128)(2,1)S(1)} collective-permute-done((bf16[4,256,1024]{2,1,0:T(8,128)(2,1)}, bf16[4,256,1024]{2,1,0:T(8,128)(2,1)S(1)}, u32[]{:S(2)}, u32[]{:S(2)}) %collective-permute-start.25) | collective-permute-done | bytes 2097184 | tf_op jit(solution)/shard_map/ppermute | solution.py:24
  208.1 8.8 %rest_grad.1 = (bf16[2,4,912,128]{3,2,1,0:T(8,128)(2,1)}, bf16[1,4,912,128]{3,2,1,0:T(8,128)(2,1)}, bf16[1,4,912,128]{3,2,1,0:T(8,128)(2,1)}) custom-call(s32[9]{0:T(128)} %stack.51.place_ref, bf16[256,5760]{1,0:T(8,128)(2,1)} %get-tuple-element.97.keep_ref, bf16[256,5760]{1,0:T(8,128)(2,1)} %collective-permute-done.22.other_ref), custom_call_target="tpu_custom_call" | custom-call | flops 4000000000 | bytes 10000000 | tf_op jit(solution)/shard_map/rest_grad/pallas_call | solution.py:944
  218.3 7.3 %qkv_weight_grad.1 = (bf16[2,256,384]{2,1,0:T(8,128)(2,1)}, bf16[1,256,384]{2,1,0:T(8,128)(2,1)}, bf16[1,256,384]{2,1,0:T(8,128)(2,1)}) custom-call(s32[9]{0:T(128)} %stack.51.place_ref, bf16[8,256,1024]{2,1,0:T(8,128)(2,1)} %get-tuple-element.99.normed_ref, bf16[8,256,384]{2,1,0:T(8,128)(2,1)} %get-tuple-element.100.grad_ref), custom_call_target="tpu_custom_call" | custom-call | flops 3000000000 | bytes 6000000 | tf_op jit(solution)/shard_map/qkv_weight_grad/pallas_call | solution.py:576
  236.8 9.0 %collective-permute-done.26 = bf16[2,4,912,128]{3,2,1,0:T(8,128)(2,1)} collective-permute-done((bf16[2,4,912,128]{3,2,1,0:T(8,128)(2,1)}, bf16[2,4,912,128]{3,2,1,0:T(8,128)(2,1)}, u32[]{:S(2)}, u32[]{:S(2)}) %collective-permute-start.26) | collective-permute-done | bytes 1867808 | tf_op jit(solution)/shard_map/ppermute | solution.py:46
  248.7 5.9 %collective-permute-done.36 = bf16[2,32,5248]{2,1,0:T(8,128)(2,1)S(1)} collective-permute-done((bf16[2,32,5248]{2,1,0:T(8,128)(2,1)S(1)}, bf16[2,32,5248]{2,1,0:T(8,128)(2,1)S(1)}, u32[]{:S(2)}, u32[]{:S(2)}) %collective-permute-start.36) | collective-permute-done | bytes 671776 | tf_op jit(solution)/shard_map/ppermute | solution.py:70
  255.9 8.3 %layer_result.1 = bf16[256,1024]{1,0:T(8,128)(2,1)} custom-call(s32[9]{0:T(128)} %stack.51.place_ref, f32[256,1024]{1,0:T(8,128)} %get-tuple-element.79.mid_ref, bf16[256,5760]{1,0:T(8,128)(2,1)} %get-tuple-element.97.keep_ref, bf16[656,1024]{1,0:T(8,128)(2,1)} %refs_0_.5, bf16[128,3712]{1,0:T(8,128)(2,1)} %copy-done.29, ...), custom_call_target="tpu_custom_call" | custom-call | flops 4000000000 | bytes 9000000 | tf_op jit(solution)/shard_map/layer_result/pallas_call | solution.py:654
  269.3 4.5 %input_grad.1 = bf16[256,1024]{1,0:T(8,128)(2,1)} custom-call(bf16[256,1024]{1,0:T(8,128)(2,1)} %bitcast.100, f32[256,1024]{1,0:T(8,128)} %get-tuple-element.98.gmid_ref, f32[1,1024]{1,0:T(1,128)} %get-tuple-element.127.gain_ref, bf16[256,1024]{1,0:T(8,128)(2,1)} %slice_bitcast_fusion.2.refs_0_, bf16[256,1024]{1,0:T(8,128)(2,1)} %slice_bitcast_fusion.1.refs_1_, ...), custom_call_target="tpu_custom_call" | custom-call | flops 100000000 | bytes 5000000 | tf_op jit(solution)/shard_map/input_grad/pallas_call | solution.py:1086
  278.1 25.7 %collective-permute-start.40 = (bf16[2,32,5248]{2,1,0:T(8,128)(2,1)S(1)}, bf16[2,32,5248]{2,1,0:T(8,128)(2,1)S(1)}, u32[]{:S(2)}, u32[]{:S(2)}) collective-permute-start(bf16[2,32,5248]{2,1,0:T(8,128)(2,1)S(1)} %pad_maximum_fusion.refs_0_), channel_id=1, source_target_pairs={{0,4},{4,0},{8,12},{12,8},{16,20},{20,16},{24,28},{28,24},{1,5},{5... | collective-permute-start | bytes 2015240 | tf_op jit(solution)/shard_map/ppermute | solution.py:24
  310.5 10.0 %collective-permute-done.44 = bf16[912,128]{1,0:T(8,128)(2,1)S(1)} collective-permute-done((bf16[912,128]{1,0:T(8,128)(2,1)S(1)}, bf16[912,128]{1,0:T(8,128)(2,1)S(1)}, u32[]{:S(2)}, u32[]{:S(2)}) %collective-permute-start.44) | collective-permute-done | bytes 233504 | tf_op jit(solution)/shard_map/ppermute | solution.py:70
  321.8 10.8 %collective-permute-start.41 = (bf16[2,32,5248]{2,1,0:T(8,128)(2,1)S(1)}, bf16[2,32,5248]{2,1,0:T(8,128)(2,1)S(1)}, u32[]{:S(2)}, u32[]{:S(2)}) collective-permute-start(bf16[2,32,5248]{2,1,0:T(8,128)(2,1)S(1)} %collective-permute-done.39.refs_1_), channel_id=1, source_target_pairs={{0,4},{4,0},{8,12},{12,8},{16,20},{20,16},{24,28},{28,24},{1,5},{5... | collective-permute-start | bytes 2015240 | tf_op jit(solution)/shard_map/ppermute | solution.py:24
  336.9 8.4 %unpack_in.1 = (f32[256,5248]{1,0:T(8,128)}, f32[256,1]{1,0:T(8,128)}) custom-call(s32[9]{0:T(128)} %stack.51.place_ref, bf16[2,32,5248]{2,1,0:T(8,128)(2,1)} %copy-done, bf16[2,32,5248]{2,1,0:T(8,128)(2,1)} %copy-done.8, bf16[2,32,5248]{2,1,0:T(8,128)(2,1)} %copy-done.9, bf16[2,32,5248]{2,1,0:T(8,128)(2,1)} %copy-done.10, bf16[256,5248]{1,0:T(8,128)(2,1)} %refs_4_.2), custom_call_target="tpu_custom_call" | custom-call | flops 10000000 | bytes 11000000 | tf_op jit(solution)/shard_map/unpack_in/pallas_call | solution.py:990
  346.1 8.0 %collective-permute-done.46.refs_1_ = bf16[2,912,128]{2,1,0:T(8,128)(2,1)S(1)} collective-permute-done((bf16[2,912,128]{2,1,0:T(8,128)(2,1)S(1)}, bf16[2,912,128]{2,1,0:T(8,128)(2,1)S(1)}, u32[]{:S(2)}, u32[]{:S(2)}) %collective-permute-start.46) | collective-permute-done | bytes 466976 | tf_op jit(solution)/shard_map/ppermute | solution.py:70
  357.7 4.4 %unpack_qkv.1 = (f32[256,3072]{1,0:T(8,128)}, f32[256,1]{1,0:T(8,128)}) custom-call(s32[9]{0:T(128)} %stack.51.place_ref, bf16[2,256,384]{2,1,0:T(8,128)(2,1)} %copy-done.4, bf16[2,256,384]{2,1,0:T(8,128)(2,1)} %copy-done.17, bf16[2,256,384]{2,1,0:T(8,128)(2,1)} %copy-done.18, bf16[2,256,384]{2,1,0:T(8,128)(2,1)} %collective-permute-done.42.refs_3_, ...), custom_call_target="tpu_custom_call" | custom-call | flops 10000000 | bytes 7000000 | tf_op jit(solution)/shard_map/unpack_qkv/pallas_call | solution.py:1056
  365.3 3.7 %unpack_rest.1 = (f32[256,1024]{1,0:T(8,128)}, f32[656,1024]{1,0:T(8,128)}) custom-call(s32[9]{0:T(128)} %stack.51.place_ref, bf16[2,912,128]{2,1,0:T(8,128)(2,1)} %copy-done.3, bf16[2,912,128]{2,1,0:T(8,128)(2,1)} %copy-done.14, bf16[2,912,128]{2,1,0:T(8,128)(2,1)} %copy-done.15, bf16[2,912,128]{2,1,0:T(8,128)(2,1)} %copy-done.16), custom_call_target="tpu_custom_call" | custom-call | flops 10000000 | bytes 6000000 | tf_op jit(solution)/shard_map/unpack_rest/pallas_call | solution.py:1029
  (211 shorter events, 100.0 us)
Async XLA Ops:
  6.4 26.4 %collective-permute-start.1 = (bf16[256,1024]{1,0:T(8,128)(2,1)}, bf16[256,1024]{1,0:T(8,128)(2,1)S(1)}, u32[]{:S(2)}, u32[]{:S(2)}) collective-permute-start(bf16[256,1024]{1,0:T(8,128)(2,1)} %bitcast.97), channel_id=1, source_target_pairs={{0,8},{4,20},{8,0},{12,28},{16,24},{20,4},{24,16},{28,12},{1,9},{5... | collective-permute-start | bytes 1572872 | tf_op jit(solution)/shard_map/ppermute | solution.py:70
  15.4 33.0 %collective-permute-start.10 = (bf16[128,3712]{1,0:T(8,128)(2,1)}, bf16[128,3712]{1,0:T(8,128)(2,1)S(1)}, u32[]{:S(2)}, u32[]{:S(2)}) collective-permute-start(bf16[128,3712]{1,0:T(8,128)(2,1)} %get-tuple-element.71), channel_id=1, source_target_pairs={{0,1},{1,0},{2,3},{3,2},{4,6},{5,7},{6,4},{7,5},{8,9},{9,8},{10,11... | collective-permute-start | bytes 2850824 | tf_op jit(solution)/shard_map/ppermute | solution.py:46
  16.5 34.2 %collective-permute-start.3 = (bf16[256,1024]{1,0:T(8,128)(2,1)S(1)}, bf16[256,1024]{1,0:T(8,128)(2,1)}, u32[]{:S(2)}, u32[]{:S(2)}) collective-permute-start(bf16[256,1024]{1,0:T(8,128)(2,1)S(1)} %bitcast.101), channel_id=1, source_target_pairs={{0,4},{4,0},{8,12},{12,8},{16,20},{20,16},{24,28},{28,24},{1,5},{5... | collective-permute-start | bytes 1572872 | tf_op jit(solution)/shard_map/ppermute | solution.py:24
  19.5 30.7 %collective-permute-start.11 = (bf16[128,5248]{1,0:T(8,128)(2,1)}, bf16[128,5248]{1,0:T(8,128)(2,1)S(1)}, u32[]{:S(2)}, u32[]{:S(2)}) collective-permute-start(bf16[128,5248]{1,0:T(8,128)(2,1)} %get-tuple-element.75), channel_id=1, source_target_pairs={{0,1},{1,0},{2,3},{3,2},{4,6},{5,7},{6,4},{7,5},{8,9},{9,8},{10,11... | collective-permute-start | bytes 4030472 | tf_op jit(solution)/shard_map/ppermute | solution.py:46
  50.3 42.5 %collective-permute-start.14 = (bf16[128,3712]{1,0:T(8,128)(2,1)S(1)}, bf16[128,3712]{1,0:T(8,128)(2,1)}, u32[]{:S(2)}, u32[]{:S(2)}) collective-permute-start(bf16[128,3712]{1,0:T(8,128)(2,1)S(1)} %collective-permute-done.10.refs_1_.refs_2_), channel_id=1, source_target_pairs={{0,4},{4,0},{8,12},{12,8},{16,20},{20,16},{24,28},{28,24},{1,5},{5... | collective-permute-start | bytes 2850824 | tf_op jit(solution)/shard_map/ppermute | solution.py:24
  50.7 36.9 %collective-permute-start.12 = (bf16[128,3712]{1,0:T(8,128)(2,1)}, bf16[128,3712]{1,0:T(8,128)(2,1)}, u32[]{:S(2)}, u32[]{:S(2)}) collective-permute-start(bf16[128,3712]{1,0:T(8,128)(2,1)} %get-tuple-element.71), channel_id=1, source_target_pairs={{0,2},{1,3},{2,0},{3,1},{4,5},{5,4},{6,7},{7,6},{8,10},{9,11},{10,... | collective-permute-start | bytes 2850824 | tf_op jit(solution)/shard_map/ppermute | solution.py:46
  50.8 38.1 %collective-permute-start.13 = (bf16[128,3712]{1,0:T(8,128)(2,1)S(1)}, bf16[128,3712]{1,0:T(8,128)(2,1)}, u32[]{:S(2)}, u32[]{:S(2)}) collective-permute-start(bf16[128,3712]{1,0:T(8,128)(2,1)S(1)} %collective-permute-done.10.refs_1_.refs_2_), channel_id=1, source_target_pairs={{0,2},{1,3},{2,0},{3,1},{4,5},{5,4},{6,7},{7,6},{8,10},{9,11},{10,... | collective-permute-start | bytes 2850824 | tf_op jit(solution)/shard_map/ppermute | solution.py:46
  52.2 55.1 %collective-permute-start.17 = (bf16[128,5248]{1,0:T(8,128)(2,1)}, bf16[128,5248]{1,0:T(8,128)(2,1)}, u32[]{:S(2)}, u32[]{:S(2)}) collective-permute-start(bf16[128,5248]{1,0:T(8,128)(2,1)} %get-tuple-element.75), channel_id=1, source_target_pairs={{0,2},{1,3},{2,0},{3,1},{4,5},{5,4},{6,7},{7,6},{8,10},{9,11},{10,... | collective-permute-start | bytes 4030472 | tf_op jit(solution)/shard_map/ppermute | solution.py:46
  53.8 54.4 %collective-permute-start.18 = (bf16[128,5248]{1,0:T(8,128)(2,1)S(1)}, bf16[128,5248]{1,0:T(8,128)(2,1)}, u32[]{:S(2)}, u32[]{:S(2)}) collective-permute-start(bf16[128,5248]{1,0:T(8,128)(2,1)S(1)} %collective-permute-done.11.refs_8_), channel_id=1, source_target_pairs={{0,2},{1,3},{2,0},{3,1},{4,5},{5,4},{6,7},{7,6},{8,10},{9,11},{10,... | collective-permute-start | bytes 4030472 | tf_op jit(solution)/shard_map/ppermute | solution.py:46
  89.0 18.3 %all-to-all-start = ((bf16[8,256,128]{2,1,0:T(8,128)(2,1)}), bf16[8,256,128]{2,1,0:T(8,128)(2,1)S(1)}, u32[]{:S(2)}, u32[]{:S(2)}) async-start(bf16[8,256,128]{2,1,0:T(8,128)(2,1)} %get-tuple-element.65), calls=%async_computation | async-start | bytes 1048576 | tf_op jit(solution)/shard_map/all_to_all | solution.py:1170
  153.0 53.0 %collective-permute-start.24 = (bf16[2,128,5248]{2,1,0:T(8,128)(2,1)}, bf16[2,128,5248]{2,1,0:T(8,128)(2,1)S(1)}, u32[]{:S(2)}, u32[]{:S(2)}) collective-permute-start(bf16[2,128,5248]{2,1,0:T(8,128)(2,1)} %get-tuple-element.83), channel_id=1, source_target_pairs={{0,2},{1,3},{2,0},{3,1},{4,5},{5,4},{6,7},{7,6},{8,10},{9,11},{10,... | collective-permute-start | bytes 8060936 | tf_op jit(solution)/shard_map/ppermute | solution.py:46
  206.0 28.5 %collective-permute-start.27 = (bf16[2,256,1024]{2,1,0:T(8,128)(2,1)}, bf16[2,256,1024]{2,1,0:T(8,128)(2,1)}, u32[]{:S(2)}, u32[]{:S(2)}) collective-permute-start(bf16[2,256,1024]{2,1,0:T(8,128)(2,1)} %add_convert_fusion.1), channel_id=1, source_target_pairs={{0,8},{4,20},{8,0},{12,28},{16,24},{20,4},{24,16},{28,12},{1,9},{5... | collective-permute-start | bytes 3145736 | tf_op jit(solution)/shard_map/ppermute | solution.py:70
  207.5 21.6 %collective-permute-start.35 = (bf16[128,5248]{1,0:T(8,128)(2,1)}, bf16[128,5248]{1,0:T(8,128)(2,1)}, u32[]{:S(2)}, u32[]{:S(2)}) collective-permute-start(bf16[128,5248]{1,0:T(8,128)(2,1)} %fusion), channel_id=1, source_target_pairs={{0,1},{1,0},{2,3},{3,2},{4,6},{5,7},{6,4},{7,5},{8,9},{9,8},{10,11... | collective-permute-start | bytes 4030472 | tf_op jit(solution)/shard_map/ppermute | solution.py:46
  216.9 28.9 %collective-permute-start.26 = (bf16[2,4,912,128]{3,2,1,0:T(8,128)(2,1)}, bf16[2,4,912,128]{3,2,1,0:T(8,128)(2,1)}, u32[]{:S(2)}, u32[]{:S(2)}) collective-permute-start(bf16[2,4,912,128]{3,2,1,0:T(8,128)(2,1)} %get-tuple-element.96), channel_id=1, source_target_pairs={{0,2},{1,3},{2,0},{3,1},{4,5},{5,4},{6,7},{7,6},{8,10},{9,11},{10,... | collective-permute-start | bytes 5603336 | tf_op jit(solution)/shard_map/ppermute | solution.py:46
  230.4 24.2 %collective-permute-start.36 = (bf16[2,32,5248]{2,1,0:T(8,128)(2,1)S(1)}, bf16[2,32,5248]{2,1,0:T(8,128)(2,1)S(1)}, u32[]{:S(2)}, u32[]{:S(2)}) collective-permute-start(bf16[2,32,5248]{2,1,0:T(8,128)(2,1)S(1)} %fusion.1), channel_id=1, source_target_pairs={{0,8},{4,20},{8,0},{12,28},{16,24},{20,4},{24,16},{28,12},{1,9},{5... | collective-permute-start | bytes 2015240 | tf_op jit(solution)/shard_map/ppermute | solution.py:70
  236.8 32.5 %collective-permute-start.28 = (bf16[256,1024]{1,0:T(8,128)(2,1)}, bf16[256,1024]{1,0:T(8,128)(2,1)}, u32[]{:S(2)}, u32[]{:S(2)}) collective-permute-start(bf16[256,1024]{1,0:T(8,128)(2,1)} %fusion.7), channel_id=1, source_target_pairs={{0,16},{4,12},{8,24},{12,4},{16,0},{20,28},{24,8},{28,20},{1,17},{... | collective-permute-start | bytes 1572872 | tf_op jit(solution)/shard_map/ppermute | solution.py:70
  248.2 25.6 %collective-permute-start.29 = (bf16[4,912,128]{2,1,0:T(8,128)(2,1)}, bf16[4,912,128]{2,1,0:T(8,128)(2,1)}, u32[]{:S(2)}, u32[]{:S(2)}) collective-permute-start(bf16[4,912,128]{2,1,0:T(8,128)(2,1)} %fusion.2), channel_id=1, source_target_pairs={{0,1},{1,0},{2,3},{3,2},{4,6},{5,7},{6,4},{7,5},{8,9},{9,8},{10,11... | collective-permute-start | bytes 2801672 | tf_op jit(solution)/shard_map/ppermute | solution.py:46
  273.8 30.0 %collective-permute-start.30 = (bf16[2,256,384]{2,1,0:T(8,128)(2,1)S(1)}, bf16[2,256,384]{2,1,0:T(8,128)(2,1)S(1)}, u32[]{:S(2)}, u32[]{:S(2)}) collective-permute-start(bf16[2,256,384]{2,1,0:T(8,128)(2,1)S(1)} %copy-done.34), channel_id=1, source_target_pairs={{0,2},{1,3},{2,0},{3,1},{4,5},{5,4},{6,7},{7,6},{8,10},{9,11},{10,... | collective-permute-start | bytes 1179656 | tf_op jit(solution)/shard_map/ppermute | solution.py:46
  275.5 29.0 %collective-permute-start.43 = (bf16[2,912,128]{2,1,0:T(8,128)(2,1)S(1)}, bf16[2,912,128]{2,1,0:T(8,128)(2,1)S(1)}, u32[]{:S(2)}, u32[]{:S(2)}) collective-permute-start(bf16[2,912,128]{2,1,0:T(8,128)(2,1)S(1)} %fusion.3), channel_id=1, source_target_pairs={{0,8},{4,20},{8,0},{12,28},{16,24},{20,4},{24,16},{28,12},{1,9},{5... | collective-permute-start | bytes 1400840 | tf_op jit(solution)/shard_map/ppermute | solution.py:70
  276.2 45.6 %collective-permute-start.39 = (bf16[2,32,5248]{2,1,0:T(8,128)(2,1)S(1)}, bf16[2,32,5248]{2,1,0:T(8,128)(2,1)S(1)}, u32[]{:S(2)}, u32[]{:S(2)}) collective-permute-start(bf16[2,32,5248]{2,1,0:T(8,128)(2,1)S(1)} %pad_maximum_fusion.refs_0_), channel_id=1, source_target_pairs={{0,8},{4,20},{8,0},{12,28},{16,24},{20,4},{24,16},{28,12},{1,9},{5... | collective-permute-start | bytes 2015240 | tf_op jit(solution)/shard_map/ppermute | solution.py:70
  278.1 57.1 %collective-permute-start.40 = (bf16[2,32,5248]{2,1,0:T(8,128)(2,1)S(1)}, bf16[2,32,5248]{2,1,0:T(8,128)(2,1)S(1)}, u32[]{:S(2)}, u32[]{:S(2)}) collective-permute-start(bf16[2,32,5248]{2,1,0:T(8,128)(2,1)S(1)} %pad_maximum_fusion.refs_0_), channel_id=1, source_target_pairs={{0,4},{4,0},{8,12},{12,8},{16,20},{20,16},{24,28},{28,24},{1,5},{5... | collective-permute-start | bytes 2015240 | tf_op jit(solution)/shard_map/ppermute | solution.py:24
  308.8 23.8 %collective-permute-start.32 = (bf16[256,384]{1,0:T(8,128)(2,1)S(1)}, bf16[256,384]{1,0:T(8,128)(2,1)S(1)}, u32[]{:S(2)}, u32[]{:S(2)}) collective-permute-start(bf16[256,384]{1,0:T(8,128)(2,1)S(1)} %fusion.11), channel_id=1, source_target_pairs={{0,16},{4,12},{8,24},{12,4},{16,0},{20,28},{24,8},{28,20},{1,17},{... | collective-permute-start | bytes 589832 | tf_op jit(solution)/shard_map/ppermute | solution.py:70
  332.8 21.2 %collective-permute-start.46 = (bf16[2,912,128]{2,1,0:T(8,128)(2,1)S(1)}, bf16[2,912,128]{2,1,0:T(8,128)(2,1)S(1)}, u32[]{:S(2)}, u32[]{:S(2)}) collective-permute-start(bf16[2,912,128]{2,1,0:T(8,128)(2,1)S(1)} %pad_maximum_fusion.1.refs_0_), channel_id=1, source_target_pairs={{0,8},{4,20},{8,0},{12,28},{16,24},{20,4},{24,16},{28,12},{1,9},{5... | collective-permute-start | bytes 1400840 | tf_op jit(solution)/shard_map/ppermute | solution.py:70
  335.2 21.8 %collective-permute-start.34 = (bf16[2,256,384]{2,1,0:T(8,128)(2,1)S(1)}, bf16[2,256,384]{2,1,0:T(8,128)(2,1)S(1)}, u32[]{:S(2)}, u32[]{:S(2)}) collective-permute-start(bf16[2,256,384]{2,1,0:T(8,128)(2,1)S(1)} %pad_maximum_fusion.2.refs_0_), channel_id=1, source_target_pairs={{0,4},{4,0},{8,12},{12,8},{16,20},{20,16},{24,28},{28,24},{1,5},{5... | collective-permute-start | bytes 1179656 | tf_op jit(solution)/shard_map/ppermute | solution.py:24
  (65 other events, 698.5 us)

commit v5 on v4

--- a/solution.py
+++ b/solution.py
@@ -67,6 +67,10 @@
 
 
 def line_swap(value, level, seq_count):
+    return lax.ppermute(value, "seq", [(i, i ^ (2 << level)) for i in range(seq_count)])
+
+
+def mixed_swap(value, level, seq_count):
     return lax.ppermute(value, "seq", [(i, i ^ (2 << (level ^ (i & 1)))) for i in range(seq_count)])
 
 
@@ -396,10 +400,11 @@
 
 def attention_backward(
     seq_count, heads, group, low_ref, high_ref, place_ref, dout_ref, packed_ref, out_ref, lse_ref, order_ref,
-    start_ref, end_ref, cos_ref, sin_ref, w_ref, grad_ref, *refs,
+    start_ref, end_ref, cos_ref, sin_ref, w_ref, grad_hbm, *refs,
 ):
-    shares, refs = refs[:-9], refs[-9:]
-    dout_t, dpack_t, drows, qrows, krows, vrows, delta_ref, dq_t, grows = refs
+    results, refs = refs[:-13], refs[-13:]
+    dout_t, dpack_t, drows, qrows, krows, vrows, delta_ref, dq_t, grows = refs[:9]
+    grad_ref, share_ref, grad_sems, share_sems = refs[9:]
     width = heads * HD
     rows = group // seq_count
     blocks = group // BLOCK
@@ -497,24 +502,36 @@
         hot = jnp.where(here == order_ref[...], 1.0, 0.0).astype(BF16)
         grad = nn_dot(hot, grows[...]).astype(BF16)
         grad_ref[i] = grad
+        grad_out(i).start()
         return nt_dot(grad, w_ref[...]).astype(BF16)
 
-    if len(shares) == 1:
-
-        def each(i, carry):
-            shares[0][i] = arrive(i)
+    def grad_out(i):
+        return pltpu.make_async_copy(grad_ref.at[i], grad_hbm.at[i], grad_sems.at[i])
+
+    def share_out(result, first, j):
+        return pltpu.make_async_copy(share_ref.at[first + j], result.at[j], share_sems.at[first + j])
+
+    sides = [0] if len(results) == 1 else [1 - place_ref[7], place_ref[7]]
+    count = seq_count // len(results)
+    for which, (side, result) in enumerate(zip(sides, results)):
+        first = which * count
+
+        def each(j, carry, side=side, result=result, first=first):
+            if len(results) == 1:
+                source = j
+            else:
+                k = jnp.where(j == 1, 2 - side, jnp.where(j == 2, 1 + side, j))
+                source = (place_ref[8] ^ k) * 2 + side
+            share_ref[first + j] = arrive(source)
+            share_out(result, first, j).start()
             return carry
 
-        lax.fori_loop(0, seq_count, each, 0)
-    else:
-        for side, share in zip((1 - place_ref[7], place_ref[7]), shares):
-
-            def each(j, carry, side=side, share=share):
-                k = jnp.where(j == 1, 2 - side, jnp.where(j == 2, 1 + side, j))
-                share[j] = arrive((place_ref[8] ^ k) * 2 + side)
-                return carry
-
-            lax.fori_loop(0, seq_count // 2, each, 0)
+        lax.fori_loop(0, count, each, 0)
+    for i in range(seq_count):
+        grad_out(i).wait()
+    for which, result in enumerate(results):
+        for j in range(count):
+            share_out(result, which * count, j).wait()
 
 
 def run_attention_backward(place, dout, packed, out_t, lse, w_heads, layout, heads, regular):
@@ -529,7 +546,7 @@
         out_shape=[jax.ShapeDtypeStruct((seq_count, rows, 3 * width), BF16)]
         + [jax.ShapeDtypeStruct((share, rows, dim), BF16) for share in shares],
         in_specs=[smem_spec()] * 3 + [vmem_spec()] * 10,
-        out_specs=[vmem_spec()] * (1 + len(shares)),
+        out_specs=[any_spec()] * (1 + len(shares)),
         scratch_shapes=[
             pltpu.VMEM((seq_count, width, rows), BF16),
             pltpu.VMEM((width, group), BF16),
@@ -540,6 +557,10 @@
             pltpu.VMEM((heads, group), F32),
             pltpu.VMEM((width, group), F32),
             pltpu.VMEM((group, 3 * width), BF16),
+            pltpu.VMEM((seq_count, rows, 3 * width), BF16),
+            pltpu.VMEM((seq_count, rows, dim), BF16),
+            pltpu.SemaphoreType.DMA((seq_count,)),
+            pltpu.SemaphoreType.DMA((seq_count,)),
         ],
         compiler_params=params(),
         cost_estimate=cost(33e9, 15e6),
@@ -837,6 +858,9 @@
     )(place, x, att, cot, gain, grad_hidden, w_out, w_in, *first, *second)
 
 
+ORDER = (0, 2, 1, 3)
+
+
 def block_order(core):
     return (0, 2 - core, 1 + core, 3)
 
@@ -852,7 +876,7 @@
         turned[:, tokens:] = other_ref[:, 2 * hidden :].T
         core, z = place_ref[7], place_ref[8]
         for at, key in enumerate((2, 3, 1, 0)):
-            for j, k in enumerate(block_order(core)):
+            for j, k in enumerate(ORDER):
                 base = pl.multiple_of(place_ref[key] * rows + core * half + (z ^ k) * short, 16)
                 to = at * half + j * short
                 picked[to : to + short, :] = turned[pl.ds(base, short), :]
@@ -905,7 +929,7 @@
         turned[:wide, tokens:] = other_ref[:, :wide].T
         turned[wide:, :tokens] = keep_ref[:, wide + dim : wide + 2 * dim].T
         turned[wide:, tokens:] = other_ref[:, wide + dim : wide + 2 * dim].T
-        for j, k in enumerate(block_order(core)):
+        for j, k in enumerate(ORDER):
             left = pl.ds(pl.multiple_of(wide + 2 * dim + core * half + (z ^ k) * 128, 128), 128)
             picked[:tokens, j * 128 : (j + 1) * 128] = keep_ref[:, left]
             picked[tokens:, j * 128 : (j + 1) * 128] = other_ref[:, left]
@@ -916,7 +940,7 @@
     base = pl.multiple_of(owner * down_rows, 16)
     down = nn_dot(turned[pl.ds(base, down_rows), :], picked[:, :half]).astype(BF16)
     left = []
-    for k in block_order(core):
+    for k in ORDER:
         base = pl.multiple_of(wide + owner * 8 * short + core * 4 * short + (z ^ k) * short, 16)
         left.append(turned[pl.ds(base, short), :])
     out = nn_dot(jnp.concatenate(left, axis=0), picked[:, half:]).astype(BF16)
@@ -975,7 +999,7 @@
 
 def row_block(i, place_ref):
     side = jnp.where(i < 4, place_ref[7], 1 - place_ref[7])
-    order = jnp.where(i % 4 == 1, 2 - side, jnp.where(i % 4 == 2, 1 + side, i % 4))
+    order = jnp.where(i % 4 == 1, 2, jnp.where(i % 4 == 2, 1, i % 4))
     return (side * 4 + (place_ref[8] ^ order), 0)
 
 
@@ -1007,7 +1031,7 @@
     for q, ref in enumerate(pieces):
         for at in range(2):
             side = core if q < 2 else 1 - core
-            yield ref.at[at], side, z ^ block_order(side)[2 * (q % 2) + at]
+            yield ref.at[at], side, z ^ ORDER[2 * (q % 2) + at]
 
 
 def unpack_rest(place_ref, *refs):
@@ -1136,9 +1160,10 @@
     place = jnp.stack([fsdp_at, *mine, *other, core, seq_at // 2]).astype(jnp.int32)
     regular = fsdp_count == 4 and seq_count == 8 and w_down.shape[0] % 16 == 0 and dim == 1024
 
+    layout = sequence_layout(seq_lengths[0], seq_order[0], group)
     if regular:
-        chunks = [x, line_swap(x, 1, seq_count), line_swap(x, 0, seq_count)]
-        chunks.append(line_swap(after(chunks[1], chunks[2]), 0, seq_count))
+        chunks = [x, mixed_swap(x, 1, seq_count), mixed_swap(x, 0, seq_count)]
+        chunks.append(mixed_swap(after(chunks[1], chunks[2], layout[5], layout[6]), 0, seq_count))
         chunks += [swap(chunk) for chunk in chunks]
     else:
         chunks = [lax.all_gather(x, "seq", axis=0, tiled=False)]
@@ -1164,7 +1189,6 @@
     second = plane_gather_rest(second_piece, second_a, *counts, first_a)
     left = dim
 
-    layout = sequence_layout(seq_lengths[0], seq_order[0], group)
     gains, w_heads, normed, packed, att, out_t, lse = run_attention_forward(place, chunks, head_pieces, layout, heads)
     gain_one, gain_two = gains[:1], gains[1:]
     att_done = lax.all_to_all(att, "seq", split_axis=0, concat_axis=0, tiled=True)
@@ -1196,7 +1220,7 @@
         in_second = plane_swap(in_sum, 0, *counts)
         got, share = swap(shares[0]), shares[1]
         token_sum = added(share[2:], got[2:])
-        token_z1 = line_swap(token_sum, 0, seq_count)
+        token_z1 = mixed_swap(token_sum, 0, seq_count)
         rest_a, rest_b, rest_c = run_rest_grad(place, keep, after(keep_other, in_sum, token_sum), hidden)
         rest_a = plane_swap(rest_a, 1, *counts)
         gw_heads = run_qkv_weight_grad(place, normed, after(grads, rest_b), regular)
@@ -1206,7 +1230,7 @@
         rest_second = plane_swap(rest_sum, 0, *counts)
         rest_parts = (rest_c[0], rest_a[0], rest_second)
         layer_out = run_layer_result(place, middle, after(keep, rest_sum), downs, left, hidden)
-        token_z2 = line_swap(added(share[1], got[1], token_z1[1]), 1, seq_count)
+        token_z2 = mixed_swap(added(share[1], got[1], token_z1[1]), 1, seq_count)
         grad_tokens = run_input_grad(x, gmid, gain_one, [share[0], got[0], token_z1[0], token_z2])
         qkv_a, qkv_b, qkv_c = gw_heads
         qkv_a = plane_swap(after(qkv_a, rest_second), 1, *counts)

time: 371 us -> 369 us (level)
  waiting for transfers between devices: 80 us -> 96.9 us
  Pallas kernels: 163 us -> 152 us
  starting transfers between devices: 80.4 us -> 71.2 us
    ppermute x19, starting transfers between devices: 46.9 us -> 13.3 us  [core_swap(): return lax.ppermute(value, 'seq', [(i, i ^ 1) for i in range(seq_count)])]
    ppermute x15, waiting for transfers between devices: 50.2 us -> 69.7 us  [the longest x10 51.2 us: line_swap(): lax.ppermute(value, 'seq', [(i, i ^ 2 << level) for i in range(seq_count)])]
    ppermute x15, starting transfers between devices: 11.2 us -> 29.2 us  [plane_swap(): return lax.ppermute(value, AXES, pairs)]
    pallas_call x1, Pallas kernels: 38.3 us -> 31.6 us  [run_attention_backward(): pl.pallas_call(functools.partial(attention_backward, seq_count, heads, gr...]
    ppermute x15, starting transfers between devices: 15 us -> 21.4 us  [the longest x10 14.1 us: line_swap(): lax.ppermute(value, 'seq', [(i, i ^ 2 << level) for i in range(seq_count)])]
    pallas_call x1, Pallas kernels: 33.1 us -> 28.6 us  [run_attention_forward(): pl.pallas_call(functools.partial(attention_forward, seq_count, heads, gro...]
    unnamed x76 -> x72, local copies, waits for them, and re-layouts: 7.89 us -> 7.67 us
  transfers between devices with their start and end apart: 51 -> 51, of which waited for: 17 -> 19; matrix products, arithmetic and copies ran while one was open for 9% -> 10% of each run, Pallas kernels for 37% -> 34%
where the time goes in v5:
time: 369 us; the launch traced here: 367 us
  Pallas kernels  152 us (41%)
  waiting for transfers between devices  96.9 us (26%)
  starting transfers between devices  71.2 us (19%)
  other arithmetic  27.2 us (7%)
  local copies, waits for them, and re-layouts  19 us (5%)
    ppermute x10, waiting for transfers between devices, line_swap(): lax.ppermute(value, 'seq', [(i, i ^ 2 << level) for i in range(seq_count)])  51.2 us
    pallas_call x1, Pallas kernels, run_attention_backward(): pl.pallas_call(functools.partial(attention_backward, seq_count, heads, gr...  31.6 us
    ppermute x15, starting transfers between devices, plane_swap(): return lax.ppermute(value, AXES, pairs)  29.2 us
    pallas_call x1, Pallas kernels, run_attention_forward(): pl.pallas_call(functools.partial(attention_forward, seq_count, heads, gro...  28.6 us
    pallas_call x1, Pallas kernels, run_feed_forward(): pl.pallas_call(functools.partial(feed_forward, count, hidden, heads_width...  24.7 us
    ppermute x5, waiting for transfers between devices, mixed_swap(): lax.ppermute(value, 'seq', [(i, i ^ 2 << (level ^ i & 1)) for i in range(...  18.5 us
    convert_element_type x12, other arithmetic, added(): return sum((v.astype(F32) for v in values)).astype(BF16)  16.1 us
    ppermute x15, waiting for transfers between devices, plane_swap(): return lax.ppermute(value, AXES, pairs)  15.7 us
  transfers between devices with their start and end apart: 51, of which 19 were waited for; matrix products, arithmetic and copies ran while one was open for 10% of the time, Pallas kernels for 34%

profile of v5, /device:TPU:1, one launch (start us, length us, event | category | flops | bytes accessed | tf_op | source)
XLA Modules:
  0.0 367.5 jit_solution(5648529830127117129)
XLA Ops:
  23.4 5.0 %collective-permute-done.1.refs_2_ = bf16[256,1024]{1,0:T(8,128)(2,1)S(1)} collective-permute-done((bf16[256,1024]{1,0:T(8,128)(2,1)}, bf16[256,1024]{1,0:T(8,128)(2,1)S(1)}, u32[]{:S(2)}, u32[]{:S(2)}) %collective-permute-start.1) | collective-permute-done | bytes 524320 | tf_op jit(solution)/shard_map/ppermute | solution.py:74
  29.3 13.5 %collective-permute-done.2.refs_3_ = bf16[256,1024]{1,0:T(8,128)(2,1)} collective-permute-done((bf16[256,1024]{1,0:T(8,128)(2,1)S(1)}, bf16[256,1024]{1,0:T(8,128)(2,1)}, u32[]{:S(2)}, u32[]{:S(2)}) %collective-permute-start.2) | collective-permute-done | bytes 524320 | tf_op jit(solution)/shard_map/ppermute | solution.py:74
  53.5 28.6 %attention_forward.1 = (f32[2,1024]{1,0:T(2,128)}, bf16[1024,384]{1,0:T(8,128)(2,1)}, bf16[8,256,1024]{2,1,0:T(8,128)(2,1)}, bf16[384,2048]{1,0:T(8,128)(2,1)}, ...) custom-call(s32[4]{0:T(128)} %get-tuple-element.134.low_ref, s32[4]{0:T(128)} %get-tuple-element.133.high_ref, ...), custom_call_target="tpu_custom_call" | custom-call | flops 24000000000 | bytes 20000000 | tf_op jit(solution)/shard_map/attention_forward/pallas_call | solution.py:372
  87.7 9.0 %hidden_grad.1.gh_hbm = f32[256,2688]{1,0:T(8,128)} custom-call(s32[9]{0:T(128)} %stack.51.place_ref, bf16[256,1024]{1,0:T(8,128)(2,1)} %bitcast.113, bf16[656,1024]{1,0:T(8,128)(2,1)} %refs_0_.5, bf16[128,3712]{1,0:T(8,128)(2,1)} %collective-permute-done.10.refs_1_.refs_2_, bf16[128,3712]{1,0:T(8,128)(2,1)} %collective-permute-done.12.refs_2_.refs_3_, ...), custom_call_target="tpu_custom_call" | custom-call | flops 4000000000 | bytes 9000000 | tf_op jit(solution)/shard_map/hidden_grad/pallas_call | solution.py:648
  96.7 5.2 %all-to-all-done.att_ref = bf16[8,256,128]{2,1,0:T(8,128)(2,1)S(1)} async-done(((bf16[8,256,128]{2,1,0:T(8,128)(2,1)}), bf16[8,256,128]{2,1,0:T(8,128)(2,1)S(1)}, u32[]{:S(2)}, u32[]{:S(2)}) %all-to-all-start) | async-done | bytes 524320 | tf_op jit(solution)/shard_map/all_to_all | solution.py:1194
  108.7 24.7 %feed_forward.1 = (f32[256,1024]{1,0:T(8,128)}, f32[256,1024]{1,0:T(8,128)}, bf16[256,6272]{1,0:T(8,128)(2,1)}, bf16[256,5760]{1,0:T(8,128)(2,1)}, bf16[8,256,128]{2,1,0:T(8,128)(2,1)}) custom-call(s32[9]{0:T(128)} %stack.51.place_ref, bf16[256,1024]{1,0:T(8,128)(2,1)} %bitcast.99, bf16[8,256,128]{2,1,0:T(8,128)(2,1)} %copy-done.12, ...), custom_call_target="tpu_custom_call" | custom-call | flops 16000000000 | bytes 24000000 | tf_op jit(solution)/shard_map/feed_forward/pallas_call | solution.py:831
  139.6 9.0 %in_grad.1 = (bf16[2,128,5248]{2,1,0:T(8,128)(2,1)}, bf16[1,128,5248]{2,1,0:T(8,128)(2,1)}, bf16[1,128,5248]{2,1,0:T(8,128)(2,1)}) custom-call(s32[9]{0:T(128)} %stack.51.place_ref, bf16[256,6272]{1,0:T(8,128)(2,1)} %get-tuple-element.81.send_ref, bf16[256,6272]{1,0:T(8,128)(2,1)} %collective-permute-done.23.other_ref), custom_call_target="tpu_custom_call" | custom-call | flops 5502926848 | bytes 10747904 | tf_op jit(solution)/shard_map/in_grad/pallas_call | solution.py:900
  148.6 6.3 %collective-permute-start.24 = (bf16[2,128,5248]{2,1,0:T(8,128)(2,1)}, bf16[2,128,5248]{2,1,0:T(8,128)(2,1)S(1)}, u32[]{:S(2)}, u32[]{:S(2)}) collective-permute-start(bf16[2,128,5248]{2,1,0:T(8,128)(2,1)} %get-tuple-element.83), channel_id=1, source_target_pairs={{0,2},{1,3},{2,0},{3,1},{4,5},{5,4},{6,7},{7,6},{8,10},{9,11},{10,... | collective-permute-start | bytes 8060936 | tf_op jit(solution)/shard_map/ppermute | solution.py:46
  155.6 31.6 %attention_backward.1 = (bf16[8,256,384]{2,1,0:T(8,128)(2,1)}, bf16[4,256,1024]{2,1,0:T(8,128)(2,1)}, bf16[4,256,1024]{2,1,0:T(8,128)(2,1)}) custom-call(s32[8]{0:T(128)} %get-tuple-element.132.low_ref, s32[8]{0:T(128)} %get-tuple-element.131.high_ref, s32[9]{0:T(128)} %stack.51.place_ref, bf16[8,256,128]{2,1,0:T(8,128)(2,1)} %copy-done.13, ...), custom_call_target="tpu_custom_call" | custom-call | flops 32999999488 | bytes 15000000 | tf_op jit(solution)/shard_map/attention_backward/pallas_call | solution.py:543
  200.9 7.6 %collective-permute-start.35 = (bf16[128,5248]{1,0:T(8,128)(2,1)}, bf16[128,5248]{1,0:T(8,128)(2,1)}, u32[]{:S(2)}, u32[]{:S(2)}) collective-permute-start(bf16[128,5248]{1,0:T(8,128)(2,1)} %fusion), channel_id=1, source_target_pairs={{0,1},{1,0},{2,3},{3,2},{4,6},{5,7},{6,4},{7,5},{8,9},{9,8},{10,11... | collective-permute-start | bytes 4030472 | tf_op jit(solution)/shard_map/ppermute | solution.py:46
  208.6 8.8 %rest_grad.1 = (bf16[2,4,912,128]{3,2,1,0:T(8,128)(2,1)}, bf16[1,4,912,128]{3,2,1,0:T(8,128)(2,1)}, bf16[1,4,912,128]{3,2,1,0:T(8,128)(2,1)}) custom-call(s32[9]{0:T(128)} %stack.51.place_ref, bf16[256,5760]{1,0:T(8,128)(2,1)} %get-tuple-element.97.keep_ref, bf16[256,5760]{1,0:T(8,128)(2,1)} %collective-permute-done.22.other_ref), custom_call_target="tpu_custom_call" | custom-call | flops 4000000000 | bytes 10000000 | tf_op jit(solution)/shard_map/rest_grad/pallas_call | solution.py:968
  218.5 7.3 %qkv_weight_grad.1 = (bf16[2,256,384]{2,1,0:T(8,128)(2,1)}, bf16[1,256,384]{2,1,0:T(8,128)(2,1)}, bf16[1,256,384]{2,1,0:T(8,128)(2,1)}) custom-call(s32[9]{0:T(128)} %stack.51.place_ref, bf16[8,256,1024]{2,1,0:T(8,128)(2,1)} %get-tuple-element.99.normed_ref, bf16[8,256,384]{2,1,0:T(8,128)(2,1)} %get-tuple-element.100.grad_ref), custom_call_target="tpu_custom_call" | custom-call | flops 3000000000 | bytes 6000000 | tf_op jit(solution)/shard_map/qkv_weight_grad/pallas_call | solution.py:597
  233.4 12.7 %collective-permute-done.26 = bf16[2,4,912,128]{3,2,1,0:T(8,128)(2,1)} collective-permute-done((bf16[2,4,912,128]{3,2,1,0:T(8,128)(2,1)}, bf16[2,4,912,128]{3,2,1,0:T(8,128)(2,1)}, u32[]{:S(2)}, u32[]{:S(2)}) %collective-permute-start.26) | collective-permute-done | bytes 1867808 | tf_op jit(solution)/shard_map/ppermute | solution.py:46
  252.0 8.3 %layer_result.1 = bf16[256,1024]{1,0:T(8,128)(2,1)} custom-call(s32[9]{0:T(128)} %stack.51.place_ref, f32[256,1024]{1,0:T(8,128)} %get-tuple-element.79.mid_ref, bf16[256,5760]{1,0:T(8,128)(2,1)} %get-tuple-element.97.keep_ref, bf16[656,1024]{1,0:T(8,128)(2,1)} %refs_0_.5, bf16[128,3712]{1,0:T(8,128)(2,1)} %collective-permute-done.10.refs_1_.refs_2_, ...), custom_call_target="tpu_custom_call" | custom-call | flops 4000000000 | bytes 9000000 | tf_op jit(solution)/shard_map/layer_result/pallas_call | solution.py:675
  260.3 11.2 %collective-permute-done.37 = bf16[32,5248]{1,0:T(8,128)(2,1)} collective-permute-done((bf16[32,5248]{1,0:T(8,128)(2,1)S(1)}, bf16[32,5248]{1,0:T(8,128)(2,1)}, u32[]{:S(2)}, u32[]{:S(2)}) %collective-permute-start.37) | collective-permute-done | bytes 335904 | tf_op jit(solution)/shard_map/ppermute | solution.py:70
  274.8 4.5 %input_grad.1 = bf16[256,1024]{1,0:T(8,128)(2,1)} custom-call(bf16[256,1024]{1,0:T(8,128)(2,1)} %bitcast.100, f32[256,1024]{1,0:T(8,128)} %get-tuple-element.98.gmid_ref, f32[1,1024]{1,0:T(1,128)} %get-tuple-element.127.gain_ref, bf16[256,1024]{1,0:T(8,128)(2,1)} %slice_bitcast_fusion.2.refs_0_, bf16[256,1024]{1,0:T(8,128)(2,1)} %slice_bitcast_fusion.1.refs_1_, ...), custom_call_target="tpu_custom_call" | custom-call | flops 100000000 | bytes 5000000 | tf_op jit(solution)/shard_map/input_grad/pallas_call | solution.py:1110
  282.3 5.6 %collective-permute-start.43 = (bf16[2,912,128]{2,1,0:T(8,128)(2,1)S(1)}, bf16[2,912,128]{2,1,0:T(8,128)(2,1)S(1)}, u32[]{:S(2)}, u32[]{:S(2)}) collective-permute-start(bf16[2,912,128]{2,1,0:T(8,128)(2,1)S(1)} %fusion.3), channel_id=1, source_target_pairs={{0,8},{4,12},{8,0},{12,4},{16,24},{20,28},{24,16},{28,20},{1,9},{5... | collective-permute-start | bytes 1400840 | tf_op jit(solution)/shard_map/ppermute | solution.py:70
  295.0 6.1 %collective-permute-done.43 = bf16[2,912,128]{2,1,0:T(8,128)(2,1)S(1)} collective-permute-done((bf16[2,912,128]{2,1,0:T(8,128)(2,1)S(1)}, bf16[2,912,128]{2,1,0:T(8,128)(2,1)S(1)}, u32[]{:S(2)}, u32[]{:S(2)}) %collective-permute-start.43) | collective-permute-done | bytes 466976 | tf_op jit(solution)/shard_map/ppermute | solution.py:70
  304.8 13.0 %collective-permute-done.44 = bf16[912,128]{1,0:T(8,128)(2,1)S(1)} collective-permute-done((bf16[912,128]{1,0:T(8,128)(2,1)S(1)}, bf16[912,128]{1,0:T(8,128)(2,1)S(1)}, u32[]{:S(2)}, u32[]{:S(2)}) %collective-permute-start.44) | collective-permute-done | bytes 233504 | tf_op jit(solution)/shard_map/ppermute | solution.py:70
  323.4 5.4 %collective-permute-done.32 = bf16[256,384]{1,0:T(8,128)(2,1)S(1)} collective-permute-done((bf16[256,384]{1,0:T(8,128)(2,1)S(1)}, bf16[256,384]{1,0:T(8,128)(2,1)S(1)}, u32[]{:S(2)}, u32[]{:S(2)}) %collective-permute-start.32) | collective-permute-done | bytes 196640 | tf_op jit(solution)/shard_map/ppermute | solution.py:70
  328.9 4.9 %collective-permute-done.45 = bf16[912,128]{1,0:T(8,128)(2,1)S(1)} collective-permute-done((bf16[912,128]{1,0:T(8,128)(2,1)S(1)}, bf16[912,128]{1,0:T(8,128)(2,1)S(1)}, u32[]{:S(2)}, u32[]{:S(2)}) %collective-permute-start.45) | collective-permute-done | bytes 233504 | tf_op jit(solution)/shard_map/ppermute | solution.py:70
  336.8 8.4 %unpack_in.1 = (f32[256,5248]{1,0:T(8,128)}, f32[256,1]{1,0:T(8,128)}) custom-call(s32[9]{0:T(128)} %stack.51.place_ref, bf16[2,32,5248]{2,1,0:T(8,128)(2,1)} %copy-done, bf16[2,32,5248]{2,1,0:T(8,128)(2,1)} %copy-done.8, bf16[2,32,5248]{2,1,0:T(8,128)(2,1)} %copy-done.9, bf16[2,32,5248]{2,1,0:T(8,128)(2,1)} %copy-done.10, bf16[256,5248]{1,0:T(8,128)(2,1)} %refs_4_.2), custom_call_target="tpu_custom_call" | custom-call | flops 10000000 | bytes 11000000 | tf_op jit(solution)/shard_map/unpack_in/pallas_call | solution.py:1014
  345.8 6.9 %collective-permute-done.46.refs_1_ = bf16[2,912,128]{2,1,0:T(8,128)(2,1)S(1)} collective-permute-done((bf16[2,912,128]{2,1,0:T(8,128)(2,1)S(1)}, bf16[2,912,128]{2,1,0:T(8,128)(2,1)S(1)}, u32[]{:S(2)}, u32[]{:S(2)}) %collective-permute-start.46) | collective-permute-done | bytes 466976 | tf_op jit(solution)/shard_map/ppermute | solution.py:70
  356.2 4.4 %unpack_qkv.1 = (f32[256,3072]{1,0:T(8,128)}, f32[256,1]{1,0:T(8,128)}) custom-call(s32[9]{0:T(128)} %stack.51.place_ref, bf16[2,256,384]{2,1,0:T(8,128)(2,1)} %copy-done.4, bf16[2,256,384]{2,1,0:T(8,128)(2,1)} %copy-done.17, bf16[2,256,384]{2,1,0:T(8,128)(2,1)} %copy-done.18, bf16[2,256,384]{2,1,0:T(8,128)(2,1)} %collective-permute-done.42.refs_3_, ...), custom_call_target="tpu_custom_call" | custom-call | flops 10000000 | bytes 7000000 | tf_op jit(solution)/shard_map/unpack_qkv/pallas_call | solution.py:1080
  (207 shorter events, 118.4 us)
Async XLA Ops:
  0.6 22.7 %collective-permute-start = (bf16[256,1024]{1,0:T(8,128)(2,1)}, bf16[256,1024]{1,0:T(8,128)(2,1)S(1)}, u32[]{:S(2)}, u32[]{:S(2)}) collective-permute-start(bf16[256,1024]{1,0:T(8,128)(2,1)} %bitcast.96), channel_id=1, source_target_pairs={{0,16},{4,12},{8,24},{12,4},{16,0},{20,28},{24,8},{28,20},{1,17},{... | collective-permute-start | bytes 1572872 | tf_op jit(solution)/shard_map/ppermute | solution.py:74
  2.8 25.6 %collective-permute-start.1 = (bf16[256,1024]{1,0:T(8,128)(2,1)}, bf16[256,1024]{1,0:T(8,128)(2,1)S(1)}, u32[]{:S(2)}, u32[]{:S(2)}) collective-permute-start(bf16[256,1024]{1,0:T(8,128)(2,1)} %bitcast.97), channel_id=1, source_target_pairs={{0,8},{4,20},{8,0},{12,28},{16,24},{20,4},{24,16},{28,12},{1,9},{5... | collective-permute-start | bytes 1572872 | tf_op jit(solution)/shard_map/ppermute | solution.py:74
  18.9 24.7 %collective-permute-start.10 = (bf16[128,3712]{1,0:T(8,128)(2,1)}, bf16[128,3712]{1,0:T(8,128)(2,1)}, u32[]{:S(2)}, u32[]{:S(2)}) collective-permute-start(bf16[128,3712]{1,0:T(8,128)(2,1)} %get-tuple-element.71), channel_id=1, source_target_pairs={{0,1},{1,0},{2,3},{3,2},{4,6},{5,7},{6,4},{7,5},{8,9},{9,8},{10,11... | collective-permute-start | bytes 2850824 | tf_op jit(solution)/shard_map/ppermute | solution.py:46
  20.9 25.8 %collective-permute-start.11 = (bf16[128,5248]{1,0:T(8,128)(2,1)}, bf16[128,5248]{1,0:T(8,128)(2,1)S(1)}, u32[]{:S(2)}, u32[]{:S(2)}) collective-permute-start(bf16[128,5248]{1,0:T(8,128)(2,1)} %get-tuple-element.75), channel_id=1, source_target_pairs={{0,1},{1,0},{2,3},{3,2},{4,6},{5,7},{6,4},{7,5},{8,9},{9,8},{10,11... | collective-permute-start | bytes 4030472 | tf_op jit(solution)/shard_map/ppermute | solution.py:46
  28.4 22.1 %collective-permute-start.3 = (bf16[256,1024]{1,0:T(8,128)(2,1)S(1)}, bf16[256,1024]{1,0:T(8,128)(2,1)}, u32[]{:S(2)}, u32[]{:S(2)}) collective-permute-start(bf16[256,1024]{1,0:T(8,128)(2,1)S(1)} %bitcast.101), channel_id=1, source_target_pairs={{0,4},{4,0},{8,12},{12,8},{16,20},{20,16},{24,28},{28,24},{1,5},{5... | collective-permute-start | bytes 1572872 | tf_op jit(solution)/shard_map/ppermute | solution.py:24
  29.3 22.4 %collective-permute-start.4 = (bf16[256,1024]{1,0:T(8,128)(2,1)S(1)}, bf16[256,1024]{1,0:T(8,128)(2,1)}, u32[]{:S(2)}, u32[]{:S(2)}) collective-permute-start(bf16[256,1024]{1,0:T(8,128)(2,1)S(1)} %collective-permute-done.refs_1_), channel_id=1, source_target_pairs={{0,4},{4,0},{8,12},{12,8},{16,20},{20,16},{24,28},{28,24},{1,5},{5... | collective-permute-start | bytes 1572872 | tf_op jit(solution)/shard_map/ppermute | solution.py:24
  46.7 40.7 %collective-permute-start.14 = (bf16[128,3712]{1,0:T(8,128)(2,1)}, bf16[128,3712]{1,0:T(8,128)(2,1)}, u32[]{:S(2)}, u32[]{:S(2)}) collective-permute-start(bf16[128,3712]{1,0:T(8,128)(2,1)} %collective-permute-done.10.refs_1_.refs_2_), channel_id=1, source_target_pairs={{0,4},{4,0},{8,12},{12,8},{16,20},{20,16},{24,28},{28,24},{1,5},{5... | collective-permute-start | bytes 2850824 | tf_op jit(solution)/shard_map/ppermute | solution.py:24
  50.5 31.7 %collective-permute-start.12 = (bf16[128,3712]{1,0:T(8,128)(2,1)}, bf16[128,3712]{1,0:T(8,128)(2,1)}, u32[]{:S(2)}, u32[]{:S(2)}) collective-permute-start(bf16[128,3712]{1,0:T(8,128)(2,1)} %get-tuple-element.71), channel_id=1, source_target_pairs={{0,2},{1,3},{2,0},{3,1},{4,5},{5,4},{6,7},{7,6},{8,10},{9,11},{10,... | collective-permute-start | bytes 2850824 | tf_op jit(solution)/shard_map/ppermute | solution.py:46
  51.7 31.7 %collective-permute-start.13 = (bf16[128,3712]{1,0:T(8,128)(2,1)}, bf16[128,3712]{1,0:T(8,128)(2,1)}, u32[]{:S(2)}, u32[]{:S(2)}) collective-permute-start(bf16[128,3712]{1,0:T(8,128)(2,1)} %collective-permute-done.10.refs_1_.refs_2_), channel_id=1, source_target_pairs={{0,2},{1,3},{2,0},{3,1},{4,5},{5,4},{6,7},{7,6},{8,10},{9,11},{10,... | collective-permute-start | bytes 2850824 | tf_op jit(solution)/shard_map/ppermute | solution.py:46
  52.0 49.9 %collective-permute-start.17 = (bf16[128,5248]{1,0:T(8,128)(2,1)}, bf16[128,5248]{1,0:T(8,128)(2,1)S(1)}, u32[]{:S(2)}, u32[]{:S(2)}) collective-permute-start(bf16[128,5248]{1,0:T(8,128)(2,1)} %get-tuple-element.75), channel_id=1, source_target_pairs={{0,2},{1,3},{2,0},{3,1},{4,5},{5,4},{6,7},{7,6},{8,10},{9,11},{10,... | collective-permute-start | bytes 4030472 | tf_op jit(solution)/shard_map/ppermute | solution.py:46
  53.3 49.5 %collective-permute-start.18 = (bf16[128,5248]{1,0:T(8,128)(2,1)S(1)}, bf16[128,5248]{1,0:T(8,128)(2,1)}, u32[]{:S(2)}, u32[]{:S(2)}) collective-permute-start(bf16[128,5248]{1,0:T(8,128)(2,1)S(1)} %collective-permute-done.11.refs_8_), channel_id=1, source_target_pairs={{0,2},{1,3},{2,0},{3,1},{4,5},{5,4},{6,7},{7,6},{8,10},{9,11},{10,... | collective-permute-start | bytes 4030472 | tf_op jit(solution)/shard_map/ppermute | solution.py:46
  133.9 21.0 %all-to-all-start.1 = ((bf16[8,256,128]{2,1,0:T(8,128)(2,1)}), bf16[8,256,128]{2,1,0:T(8,128)(2,1)S(1)}, u32[]{:S(2)}, u32[]{:S(2)}) async-start(bf16[8,256,128]{2,1,0:T(8,128)(2,1)} %get-tuple-element.84), calls=%async_computation.1 | async-start | bytes 1048576 | tf_op jit(solution)/shard_map/all_to_all | solution.py:1206
  148.6 50.9 %collective-permute-start.24 = (bf16[2,128,5248]{2,1,0:T(8,128)(2,1)}, bf16[2,128,5248]{2,1,0:T(8,128)(2,1)S(1)}, u32[]{:S(2)}, u32[]{:S(2)}) collective-permute-start(bf16[2,128,5248]{2,1,0:T(8,128)(2,1)} %get-tuple-element.83), channel_id=1, source_target_pairs={{0,2},{1,3},{2,0},{3,1},{4,5},{5,4},{6,7},{7,6},{8,10},{9,11},{10,... | collective-permute-start | bytes 8060936 | tf_op jit(solution)/shard_map/ppermute | solution.py:46
  187.8 20.8 %collective-permute-start.22 = (bf16[256,5760]{1,0:T(8,128)(2,1)}, bf16[256,5760]{1,0:T(8,128)(2,1)}, u32[]{:S(2)}, u32[]{:S(2)}) collective-permute-start(bf16[256,5760]{1,0:T(8,128)(2,1)} %get-tuple-element.97.keep_ref), channel_id=1, source_target_pairs={{0,4},{4,0},{8,12},{12,8},{16,20},{20,16},{24,28},{28,24},{1,5},{5... | collective-permute-start | bytes 8847368 | tf_op jit(solution)/shard_map/ppermute | solution.py:24
  197.2 33.4 %collective-permute-start.27 = (bf16[2,256,1024]{2,1,0:T(8,128)(2,1)}, bf16[2,256,1024]{2,1,0:T(8,128)(2,1)}, u32[]{:S(2)}, u32[]{:S(2)}) collective-permute-start(bf16[2,256,1024]{2,1,0:T(8,128)(2,1)} %add_convert_fusion.1), channel_id=1, source_target_pairs={{0,8},{4,20},{8,0},{12,28},{16,24},{20,4},{24,16},{28,12},{1,9},{5... | collective-permute-start | bytes 3145736 | tf_op jit(solution)/shard_map/ppermute | solution.py:74
  200.9 26.4 %collective-permute-start.35 = (bf16[128,5248]{1,0:T(8,128)(2,1)}, bf16[128,5248]{1,0:T(8,128)(2,1)}, u32[]{:S(2)}, u32[]{:S(2)}) collective-permute-start(bf16[128,5248]{1,0:T(8,128)(2,1)} %fusion), channel_id=1, source_target_pairs={{0,1},{1,0},{2,3},{3,2},{4,6},{5,7},{6,4},{7,5},{8,9},{9,8},{10,11... | collective-permute-start | bytes 4030472 | tf_op jit(solution)/shard_map/ppermute | solution.py:46
  217.4 28.8 %collective-permute-start.26 = (bf16[2,4,912,128]{3,2,1,0:T(8,128)(2,1)}, bf16[2,4,912,128]{3,2,1,0:T(8,128)(2,1)}, u32[]{:S(2)}, u32[]{:S(2)}) collective-permute-start(bf16[2,4,912,128]{3,2,1,0:T(8,128)(2,1)} %get-tuple-element.96), channel_id=1, source_target_pairs={{0,2},{1,3},{2,0},{3,1},{4,5},{5,4},{6,7},{7,6},{8,10},{9,11},{10,... | collective-permute-start | bytes 5603336 | tf_op jit(solution)/shard_map/ppermute | solution.py:46
  232.8 42.0 %collective-permute-start.28 = (bf16[256,1024]{1,0:T(8,128)(2,1)}, bf16[256,1024]{1,0:T(8,128)(2,1)}, u32[]{:S(2)}, u32[]{:S(2)}) collective-permute-start(bf16[256,1024]{1,0:T(8,128)(2,1)} %fusion.7), channel_id=1, source_target_pairs={{0,16},{4,12},{8,24},{12,4},{16,0},{20,28},{24,8},{28,20},{1,17},{... | collective-permute-start | bytes 1572872 | tf_op jit(solution)/shard_map/ppermute | solution.py:74
  248.6 30.8 %collective-permute-start.29 = (bf16[4,912,128]{2,1,0:T(8,128)(2,1)}, bf16[4,912,128]{2,1,0:T(8,128)(2,1)}, u32[]{:S(2)}, u32[]{:S(2)}) collective-permute-start(bf16[4,912,128]{2,1,0:T(8,128)(2,1)} %fusion.2), channel_id=1, source_target_pairs={{0,1},{1,0},{2,3},{3,2},{4,6},{5,7},{6,4},{7,5},{8,9},{9,8},{10,11... | collective-permute-start | bytes 2801672 | tf_op jit(solution)/shard_map/ppermute | solution.py:46
  250.5 21.0 %collective-permute-start.37 = (bf16[32,5248]{1,0:T(8,128)(2,1)S(1)}, bf16[32,5248]{1,0:T(8,128)(2,1)}, u32[]{:S(2)}, u32[]{:S(2)}) collective-permute-start(bf16[32,5248]{1,0:T(8,128)(2,1)S(1)} %fusion.4), channel_id=1, source_target_pairs={{0,16},{4,20},{8,24},{12,28},{16,0},{20,4},{24,8},{28,12},{1,17},{... | collective-permute-start | bytes 1007624 | tf_op jit(solution)/shard_map/ppermute | solution.py:70
  290.9 32.2 %collective-permute-start.39 = (bf16[2,32,5248]{2,1,0:T(8,128)(2,1)S(1)}, bf16[2,32,5248]{2,1,0:T(8,128)(2,1)S(1)}, u32[]{:S(2)}, u32[]{:S(2)}) collective-permute-start(bf16[2,32,5248]{2,1,0:T(8,128)(2,1)S(1)} %pad_maximum_fusion.refs_0_), channel_id=1, source_target_pairs={{0,8},{4,12},{8,0},{12,4},{16,24},{20,28},{24,16},{28,20},{1,9},{5... | collective-permute-start | bytes 2015240 | tf_op jit(solution)/shard_map/ppermute | solution.py:70
  291.0 44.1 %collective-permute-start.40 = (bf16[2,32,5248]{2,1,0:T(8,128)(2,1)S(1)}, bf16[2,32,5248]{2,1,0:T(8,128)(2,1)S(1)}, u32[]{:S(2)}, u32[]{:S(2)}) collective-permute-start(bf16[2,32,5248]{2,1,0:T(8,128)(2,1)S(1)} %pad_maximum_fusion.refs_0_), channel_id=1, source_target_pairs={{0,4},{4,0},{8,12},{12,8},{16,20},{20,16},{24,28},{28,24},{1,5},{5... | collective-permute-start | bytes 2015240 | tf_op jit(solution)/shard_map/ppermute | solution.py:24
  302.4 26.3 %collective-permute-start.32 = (bf16[256,384]{1,0:T(8,128)(2,1)S(1)}, bf16[256,384]{1,0:T(8,128)(2,1)S(1)}, u32[]{:S(2)}, u32[]{:S(2)}) collective-permute-start(bf16[256,384]{1,0:T(8,128)(2,1)S(1)} %fusion.11), channel_id=1, source_target_pairs={{0,16},{4,20},{8,24},{12,28},{16,0},{20,4},{24,8},{28,12},{1,17},{... | collective-permute-start | bytes 589832 | tf_op jit(solution)/shard_map/ppermute | solution.py:70
  333.9 21.5 %collective-permute-start.34 = (bf16[2,256,384]{2,1,0:T(8,128)(2,1)S(1)}, bf16[2,256,384]{2,1,0:T(8,128)(2,1)S(1)}, u32[]{:S(2)}, u32[]{:S(2)}) collective-permute-start(bf16[2,256,384]{2,1,0:T(8,128)(2,1)S(1)} %pad_maximum_fusion.2.refs_0_), channel_id=1, source_target_pairs={{0,4},{4,0},{8,12},{12,8},{16,20},{20,16},{24,28},{28,24},{1,5},{5... | collective-permute-start | bytes 1179656 | tf_op jit(solution)/shard_map/ppermute | solution.py:24
  (63 other events, 724.5 us)

commit v6 on v5

--- a/solution.py
+++ b/solution.py
@@ -732,13 +732,14 @@
     wide = 2 * hidden // 128
 
     def expand(i, carry):
-        at = pl.ds(pl.multiple_of(i * 256, 256), 256)
+        at = pl.ds(pl.multiple_of(i * 512, 512), 512)
         both[:, at] = nn_dot(nt_ref[...], wi[:, at])
         return carry
 
-    lax.fori_loop(0, wide // 2, expand, 0)
-    if wide % 2:
-        both[:, pl.ds(128 * (wide - 1), 128)] = nn_dot(nt_ref[...], wi[:, pl.ds(128 * (wide - 1), 128)])
+    lax.fori_loop(0, wide // 4, expand, 0)
+    if wide % 4:
+        at = pl.ds(128 * (wide - wide % 4), 128 * (wide % 4))
+        both[:, at] = nn_dot(nt_ref[...], wi[:, at])
     both[:, pl.ds(128 * wide, 128)] = jnp.zeros((both.shape[0], 128), F32)
     tiles = padded(hidden) // 128
     whole = hidden // 128
@@ -795,11 +796,11 @@
     send_out.start()
 
     def back(i, carry):
-        at = pl.multiple_of(i * 256, 256)
-        both[:, pl.ds(at, 256)] = nt_dot(gboth_ref[:, : 2 * hidden], wi[pl.ds(at, 256), :])
-        return carry
-
-    lax.fori_loop(0, dim // 256, back, 0)
+        at = pl.multiple_of(i * 512, 512)
+        both[:, pl.ds(at, 512)] = nt_dot(gboth_ref[:, : 2 * hidden], wi[pl.ds(at, 512), :])
+        return carry
+
+    lax.fori_loop(0, dim // 512, back, 0)
     middle = mid_ref[...]
     center = middle - jnp.mean(middle, axis=-1, keepdims=True)
     spread = jnp.mean(center * center, axis=-1, keepdims=True)
@@ -813,11 +814,11 @@
     keep_out.start()
 
     def spread_out(i, carry):
-        at = pl.multiple_of(i * 256, 256)
-        both[:, pl.ds(at, 256)] = nt_dot(gbr_ref[...], wo[pl.ds(at, 256), :])
-        return carry
-
-    lax.fori_loop(0, dim // 256, spread_out, 0)
+        at = pl.multiple_of(i * 512, 512)
+        both[:, pl.ds(at, 512)] = nt_dot(gbr_ref[...], wo[pl.ds(at, 512), :])
+        return carry
+
+    lax.fori_loop(0, dim // 512, spread_out, 0)
     for s in range(att_ref.shape[0]):
         ga_ref[s] = both[:, s * heads_width : (s + 1) * heads_width].astype(BF16)
     send_out.wait()

time: 369 us -> 365 us (0.989)
  waiting for transfers between devices: 96.9 us -> 80.9 us
  starting transfers between devices: 71.2 us -> 80.7 us
    ppermute x10, waiting for transfers between devices: 51.2 us -> 36.7 us  [line_swap(): lax.ppermute(value, 'seq', [(i, i ^ 2 << level) for i in range(seq_count)])]
    ppermute x19, starting transfers between devices: 13.3 us -> 26.2 us  [core_swap(): return lax.ppermute(value, 'seq', [(i, i ^ 1) for i in range(seq_count)])]
    ppermute x15, waiting for transfers between devices: 15.7 us -> 11.2 us  [plane_swap(): return lax.ppermute(value, AXES, pairs)]
  transfers between devices with their start and end apart: 51 -> 51, of which waited for: 19 -> 20; matrix products, arithmetic and copies ran while one was open for 10% -> 11% of each run, Pallas kernels for 34% -> 35%
where the time goes in v6:
time: 365 us; the launch traced here: 360 us
  Pallas kernels  151 us (41%)
  waiting for transfers between devices  80.9 us (22%)
  starting transfers between devices  80.7 us (22%)
  other arithmetic  27.2 us (7%)
  local copies, waits for them, and re-layouts  18.8 us (5%)
    ppermute x10, waiting for transfers between devices, line_swap(): lax.ppermute(value, 'seq', [(i, i ^ 2 << level) for i in range(seq_count)])  36.7 us
    pallas_call x1, Pallas kernels, run_attention_backward(): pl.pallas_call(functools.partial(attention_backward, seq_count, heads, gr...  32.5 us
    pallas_call x1, Pallas kernels, run_attention_forward(): pl.pallas_call(functools.partial(attention_forward, seq_count, heads, gro...  29.3 us
    ppermute x15, starting transfers between devices, plane_swap(): return lax.ppermute(value, AXES, pairs)  28.1 us
    ppermute x19, starting transfers between devices, core_swap(): return lax.ppermute(value, 'seq', [(i, i ^ 1) for i in range(seq_count)])  26.2 us
    pallas_call x1, Pallas kernels, run_feed_forward(): pl.pallas_call(functools.partial(feed_forward, count, hidden, heads_width...  22.5 us
    ppermute x5, waiting for transfers between devices, mixed_swap(): lax.ppermute(value, 'seq', [(i, i ^ 2 << (level ^ i & 1)) for i in range(...  18.5 us
    convert_element_type x12, other arithmetic, added(): return sum((v.astype(F32) for v in values)).astype(BF16)  16.1 us
  transfers between devices with their start and end apart: 51, of which 20 were waited for; matrix products, arithmetic and copies ran while one was open for 11% of the time, Pallas kernels for 35%

profile of v6, /device:TPU:1, one launch (start us, length us, event | category | flops | bytes accessed | tf_op | source)
XLA Modules:
  0.0 360.0 jit_solution(5026768540537887301)
XLA Ops:
  15.0 3.8 %pack_pieces.1 = (bf16[128,3712]{1,0:T(8,128)(2,1)}, bf16[128,5248]{1,0:T(8,128)(2,1)}) custom-call(s32[9]{0:T(128)} %stack.51.place_ref, bf16[256,5248]{1,0:T(8,128)(2,1)} %refs_4_.2, bf16[256,1024]{1,0:T(8,128)(2,1)} %refs_0_.4, bf16[656,1024]{1,0:T(8,128)(2,1)} %refs_0_.5), custom_call_target="tpu_custom_call" | custom-call | flops 1000000 | bytes 5000000 | tf_op jit(solution)/shard_map/pack_pieces/pallas_call | solution.py:214
  23.4 5.0 %collective-permute-done.1.refs_2_ = bf16[256,1024]{1,0:T(8,128)(2,1)S(1)} collective-permute-done((bf16[256,1024]{1,0:T(8,128)(2,1)}, bf16[256,1024]{1,0:T(8,128)(2,1)S(1)}, u32[]{:S(2)}, u32[]{:S(2)}) %collective-permute-start.1) | collective-permute-done | bytes 524320 | tf_op jit(solution)/shard_map/ppermute | solution.py:74
  29.3 13.5 %collective-permute-done.2.refs_3_ = bf16[256,1024]{1,0:T(8,128)(2,1)} collective-permute-done((bf16[256,1024]{1,0:T(8,128)(2,1)S(1)}, bf16[256,1024]{1,0:T(8,128)(2,1)}, u32[]{:S(2)}, u32[]{:S(2)}) %collective-permute-start.2) | collective-permute-done | bytes 524320 | tf_op jit(solution)/shard_map/ppermute | solution.py:74
  53.5 29.3 %attention_forward.1 = (f32[2,1024]{1,0:T(2,128)}, bf16[1024,384]{1,0:T(8,128)(2,1)}, bf16[8,256,1024]{2,1,0:T(8,128)(2,1)}, bf16[384,2048]{1,0:T(8,128)(2,1)}, ...) custom-call(s32[4]{0:T(128)} %get-tuple-element.134.low_ref, s32[4]{0:T(128)} %get-tuple-element.133.high_ref, ...), custom_call_target="tpu_custom_call" | custom-call | flops 24000000000 | bytes 20000000 | tf_op jit(solution)/shard_map/attention_forward/pallas_call | solution.py:372
  88.4 9.0 %hidden_grad.1.gh_hbm = f32[256,2688]{1,0:T(8,128)} custom-call(s32[9]{0:T(128)} %stack.51.place_ref, bf16[256,1024]{1,0:T(8,128)(2,1)} %bitcast.113, bf16[656,1024]{1,0:T(8,128)(2,1)} %refs_0_.5, bf16[128,3712]{1,0:T(8,128)(2,1)} %collective-permute-done.10.refs_1_.refs_2_, bf16[128,3712]{1,0:T(8,128)(2,1)} %collective-permute-done.12.refs_2_.refs_3_, ...), custom_call_target="tpu_custom_call" | custom-call | flops 4000000000 | bytes 9000000 | tf_op jit(solution)/shard_map/hidden_grad/pallas_call | solution.py:648
  97.3 5.2 %all-to-all-done.att_ref = bf16[8,256,128]{2,1,0:T(8,128)(2,1)S(1)} async-done(((bf16[8,256,128]{2,1,0:T(8,128)(2,1)}), bf16[8,256,128]{2,1,0:T(8,128)(2,1)S(1)}, u32[]{:S(2)}, u32[]{:S(2)}) %all-to-all-start) | async-done | bytes 524320 | tf_op jit(solution)/shard_map/all_to_all | solution.py:1195
  109.4 22.5 %feed_forward.1 = (f32[256,1024]{1,0:T(8,128)}, f32[256,1024]{1,0:T(8,128)}, bf16[256,6272]{1,0:T(8,128)(2,1)}, bf16[256,5760]{1,0:T(8,128)(2,1)}, bf16[8,256,128]{2,1,0:T(8,128)(2,1)}) custom-call(s32[9]{0:T(128)} %stack.51.place_ref, bf16[256,1024]{1,0:T(8,128)(2,1)} %bitcast.99, bf16[8,256,128]{2,1,0:T(8,128)(2,1)} %copy-done.12, ...), custom_call_target="tpu_custom_call" | custom-call | flops 16000000000 | bytes 24000000 | tf_op jit(solution)/shard_map/feed_forward/pallas_call | solution.py:832
  138.0 9.0 %in_grad.1 = (bf16[2,128,5248]{2,1,0:T(8,128)(2,1)}, bf16[1,128,5248]{2,1,0:T(8,128)(2,1)}, bf16[1,128,5248]{2,1,0:T(8,128)(2,1)}) custom-call(s32[9]{0:T(128)} %stack.51.place_ref, bf16[256,6272]{1,0:T(8,128)(2,1)} %get-tuple-element.81.send_ref, bf16[256,6272]{1,0:T(8,128)(2,1)} %collective-permute-done.23.other_ref), custom_call_target="tpu_custom_call" | custom-call | flops 5502926848 | bytes 10747904 | tf_op jit(solution)/shard_map/in_grad/pallas_call | solution.py:901
  151.1 32.5 %attention_backward.1 = (bf16[8,256,384]{2,1,0:T(8,128)(2,1)}, bf16[4,256,1024]{2,1,0:T(8,128)(2,1)}, bf16[4,256,1024]{2,1,0:T(8,128)(2,1)}) custom-call(s32[8]{0:T(128)} %get-tuple-element.132.low_ref, s32[8]{0:T(128)} %get-tuple-element.131.high_ref, s32[9]{0:T(128)} %stack.51.place_ref, bf16[8,256,128]{2,1,0:T(8,128)(2,1)} %copy-done.13, ...), custom_call_target="tpu_custom_call" | custom-call | flops 32999999488 | bytes 15000000 | tf_op jit(solution)/shard_map/attention_backward/pallas_call | solution.py:543
  188.6 4.1 %collective-permute-done.25 = bf16[4,256,1024]{2,1,0:T(8,128)(2,1)S(1)} collective-permute-done((bf16[4,256,1024]{2,1,0:T(8,128)(2,1)}, bf16[4,256,1024]{2,1,0:T(8,128)(2,1)S(1)}, u32[]{:S(2)}, u32[]{:S(2)}) %collective-permute-start.25) | collective-permute-done | bytes 2097184 | tf_op jit(solution)/shard_map/ppermute | solution.py:24
  199.7 6.6 %collective-permute-start.35 = (bf16[128,5248]{1,0:T(8,128)(2,1)}, bf16[128,5248]{1,0:T(8,128)(2,1)}, u32[]{:S(2)}, u32[]{:S(2)}) collective-permute-start(bf16[128,5248]{1,0:T(8,128)(2,1)} %fusion), channel_id=1, source_target_pairs={{0,1},{1,0},{2,3},{3,2},{4,6},{5,7},{6,4},{7,5},{8,9},{9,8},{10,11... | collective-permute-start | bytes 4030472 | tf_op jit(solution)/shard_map/ppermute | solution.py:46
  206.3 8.8 %rest_grad.1 = (bf16[2,4,912,128]{3,2,1,0:T(8,128)(2,1)}, bf16[1,4,912,128]{3,2,1,0:T(8,128)(2,1)}, bf16[1,4,912,128]{3,2,1,0:T(8,128)(2,1)}) custom-call(s32[9]{0:T(128)} %stack.51.place_ref, bf16[256,5760]{1,0:T(8,128)(2,1)} %get-tuple-element.97.keep_ref, bf16[256,5760]{1,0:T(8,128)(2,1)} %collective-permute-done.22.other_ref), custom_call_target="tpu_custom_call" | custom-call | flops 4000000000 | bytes 10000000 | tf_op jit(solution)/shard_map/rest_grad/pallas_call | solution.py:969
  215.1 7.3 %qkv_weight_grad.1 = (bf16[2,256,384]{2,1,0:T(8,128)(2,1)}, bf16[1,256,384]{2,1,0:T(8,128)(2,1)}, bf16[1,256,384]{2,1,0:T(8,128)(2,1)}) custom-call(s32[9]{0:T(128)} %stack.51.place_ref, bf16[8,256,1024]{2,1,0:T(8,128)(2,1)} %get-tuple-element.99.normed_ref, bf16[8,256,384]{2,1,0:T(8,128)(2,1)} %get-tuple-element.100.grad_ref), custom_call_target="tpu_custom_call" | custom-call | flops 3000000000 | bytes 6000000 | tf_op jit(solution)/shard_map/qkv_weight_grad/pallas_call | solution.py:597
  233.1 5.1 %collective-permute-done.26 = bf16[2,4,912,128]{3,2,1,0:T(8,128)(2,1)} collective-permute-done((bf16[2,4,912,128]{3,2,1,0:T(8,128)(2,1)}, bf16[2,4,912,128]{3,2,1,0:T(8,128)(2,1)}, u32[]{:S(2)}, u32[]{:S(2)}) %collective-permute-start.26) | collective-permute-done | bytes 1867808 | tf_op jit(solution)/shard_map/ppermute | solution.py:46
  240.6 6.4 %collective-permute-start.29 = (bf16[4,912,128]{2,1,0:T(8,128)(2,1)}, bf16[4,912,128]{2,1,0:T(8,128)(2,1)}, u32[]{:S(2)}, u32[]{:S(2)}) collective-permute-start(bf16[4,912,128]{2,1,0:T(8,128)(2,1)} %fusion.2), channel_id=1, source_target_pairs={{0,1},{1,0},{2,3},{3,2},{4,6},{5,7},{6,4},{7,5},{8,9},{9,8},{10,11... | collective-permute-start | bytes 2801672 | tf_op jit(solution)/shard_map/ppermute | solution.py:46
  250.5 8.3 %layer_result.1 = bf16[256,1024]{1,0:T(8,128)(2,1)} custom-call(s32[9]{0:T(128)} %stack.51.place_ref, f32[256,1024]{1,0:T(8,128)} %get-tuple-element.79.mid_ref, bf16[256,5760]{1,0:T(8,128)(2,1)} %get-tuple-element.97.keep_ref, bf16[656,1024]{1,0:T(8,128)(2,1)} %refs_0_.5, bf16[128,3712]{1,0:T(8,128)(2,1)} %collective-permute-done.10.refs_1_.refs_2_, ...), custom_call_target="tpu_custom_call" | custom-call | flops 4000000000 | bytes 9000000 | tf_op jit(solution)/shard_map/layer_result/pallas_call | solution.py:675
  258.8 7.6 %collective-permute-done.37 = bf16[32,5248]{1,0:T(8,128)(2,1)} collective-permute-done((bf16[32,5248]{1,0:T(8,128)(2,1)S(1)}, bf16[32,5248]{1,0:T(8,128)(2,1)}, u32[]{:S(2)}, u32[]{:S(2)}) %collective-permute-start.37) | collective-permute-done | bytes 335904 | tf_op jit(solution)/shard_map/ppermute | solution.py:70
  269.7 4.5 %input_grad.1 = bf16[256,1024]{1,0:T(8,128)(2,1)} custom-call(bf16[256,1024]{1,0:T(8,128)(2,1)} %bitcast.100, f32[256,1024]{1,0:T(8,128)} %get-tuple-element.98.gmid_ref, f32[1,1024]{1,0:T(1,128)} %get-tuple-element.127.gain_ref, bf16[256,1024]{1,0:T(8,128)(2,1)} %slice_bitcast_fusion.2.refs_0_, bf16[256,1024]{1,0:T(8,128)(2,1)} %slice_bitcast_fusion.1.refs_1_, ...), custom_call_target="tpu_custom_call" | custom-call | flops 100000000 | bytes 5000000 | tf_op jit(solution)/shard_map/input_grad/pallas_call | solution.py:1111
  277.0 5.0 %collective-permute-start.43 = (bf16[2,912,128]{2,1,0:T(8,128)(2,1)S(1)}, bf16[2,912,128]{2,1,0:T(8,128)(2,1)S(1)}, u32[]{:S(2)}, u32[]{:S(2)}) collective-permute-start(bf16[2,912,128]{2,1,0:T(8,128)(2,1)S(1)} %fusion.3), channel_id=1, source_target_pairs={{0,8},{4,12},{8,0},{12,4},{16,24},{20,28},{24,16},{28,20},{1,9},{5... | collective-permute-start | bytes 1400840 | tf_op jit(solution)/shard_map/ppermute | solution.py:70
  295.7 12.0 %collective-permute-done.44 = bf16[912,128]{1,0:T(8,128)(2,1)S(1)} collective-permute-done((bf16[912,128]{1,0:T(8,128)(2,1)S(1)}, bf16[912,128]{1,0:T(8,128)(2,1)S(1)}, u32[]{:S(2)}, u32[]{:S(2)}) %collective-permute-start.44) | collective-permute-done | bytes 233504 | tf_op jit(solution)/shard_map/ppermute | solution.py:70
  313.6 7.2 %collective-permute-start.41 = (bf16[2,32,5248]{2,1,0:T(8,128)(2,1)S(1)}, bf16[2,32,5248]{2,1,0:T(8,128)(2,1)S(1)}, u32[]{:S(2)}, u32[]{:S(2)}) collective-permute-start(bf16[2,32,5248]{2,1,0:T(8,128)(2,1)S(1)} %collective-permute-done.39.refs_1_), channel_id=1, source_target_pairs={{0,4},{4,0},{8,12},{12,8},{16,20},{20,16},{24,28},{28,24},{1,5},{5... | collective-permute-start | bytes 2015240 | tf_op jit(solution)/shard_map/ppermute | solution.py:24
  321.0 5.6 %collective-permute-done.45 = bf16[912,128]{1,0:T(8,128)(2,1)S(1)} collective-permute-done((bf16[912,128]{1,0:T(8,128)(2,1)S(1)}, bf16[912,128]{1,0:T(8,128)(2,1)S(1)}, u32[]{:S(2)}, u32[]{:S(2)}) %collective-permute-start.45) | collective-permute-done | bytes 233504 | tf_op jit(solution)/shard_map/ppermute | solution.py:70
  331.2 8.4 %unpack_in.1 = (f32[256,5248]{1,0:T(8,128)}, f32[256,1]{1,0:T(8,128)}) custom-call(s32[9]{0:T(128)} %stack.51.place_ref, bf16[2,32,5248]{2,1,0:T(8,128)(2,1)} %copy-done, bf16[2,32,5248]{2,1,0:T(8,128)(2,1)} %copy-done.8, bf16[2,32,5248]{2,1,0:T(8,128)(2,1)} %copy-done.9, bf16[2,32,5248]{2,1,0:T(8,128)(2,1)} %copy-done.10, bf16[256,5248]{1,0:T(8,128)(2,1)} %refs_4_.2), custom_call_target="tpu_custom_call" | custom-call | flops 10000000 | bytes 11000000 | tf_op jit(solution)/shard_map/unpack_in/pallas_call | solution.py:1015
  348.7 4.4 %unpack_qkv.1 = (f32[256,3072]{1,0:T(8,128)}, f32[256,1]{1,0:T(8,128)}) custom-call(s32[9]{0:T(128)} %stack.51.place_ref, bf16[2,256,384]{2,1,0:T(8,128)(2,1)} %copy-done.4, bf16[2,256,384]{2,1,0:T(8,128)(2,1)} %copy-done.17, bf16[2,256,384]{2,1,0:T(8,128)(2,1)} %copy-done.18, bf16[2,256,384]{2,1,0:T(8,128)(2,1)} %collective-permute-done.42.refs_3_, ...), custom_call_target="tpu_custom_call" | custom-call | flops 10000000 | bytes 7000000 | tf_op jit(solution)/shard_map/unpack_qkv/pallas_call | solution.py:1081
  (207 shorter events, 127.9 us)
Async XLA Ops:
  0.6 22.7 %collective-permute-start = (bf16[256,1024]{1,0:T(8,128)(2,1)}, bf16[256,1024]{1,0:T(8,128)(2,1)S(1)}, u32[]{:S(2)}, u32[]{:S(2)}) collective-permute-start(bf16[256,1024]{1,0:T(8,128)(2,1)} %bitcast.96), channel_id=1, source_target_pairs={{0,16},{4,12},{8,24},{12,4},{16,0},{20,28},{24,8},{28,20},{1,17},{... | collective-permute-start | bytes 1572872 | tf_op jit(solution)/shard_map/ppermute | solution.py:74
  2.8 25.6 %collective-permute-start.1 = (bf16[256,1024]{1,0:T(8,128)(2,1)}, bf16[256,1024]{1,0:T(8,128)(2,1)S(1)}, u32[]{:S(2)}, u32[]{:S(2)}) collective-permute-start(bf16[256,1024]{1,0:T(8,128)(2,1)} %bitcast.97), channel_id=1, source_target_pairs={{0,8},{4,20},{8,0},{12,28},{16,24},{20,4},{24,16},{28,12},{1,9},{5... | collective-permute-start | bytes 1572872 | tf_op jit(solution)/shard_map/ppermute | solution.py:74
  18.9 24.7 %collective-permute-start.10 = (bf16[128,3712]{1,0:T(8,128)(2,1)}, bf16[128,3712]{1,0:T(8,128)(2,1)}, u32[]{:S(2)}, u32[]{:S(2)}) collective-permute-start(bf16[128,3712]{1,0:T(8,128)(2,1)} %get-tuple-element.71), channel_id=1, source_target_pairs={{0,1},{1,0},{2,3},{3,2},{4,6},{5,7},{6,4},{7,5},{8,9},{9,8},{10,11... | collective-permute-start | bytes 2850824 | tf_op jit(solution)/shard_map/ppermute | solution.py:46
  20.9 25.8 %collective-permute-start.11 = (bf16[128,5248]{1,0:T(8,128)(2,1)}, bf16[128,5248]{1,0:T(8,128)(2,1)S(1)}, u32[]{:S(2)}, u32[]{:S(2)}) collective-permute-start(bf16[128,5248]{1,0:T(8,128)(2,1)} %get-tuple-element.75), channel_id=1, source_target_pairs={{0,1},{1,0},{2,3},{3,2},{4,6},{5,7},{6,4},{7,5},{8,9},{9,8},{10,11... | collective-permute-start | bytes 4030472 | tf_op jit(solution)/shard_map/ppermute | solution.py:46
  28.4 22.1 %collective-permute-start.3 = (bf16[256,1024]{1,0:T(8,128)(2,1)S(1)}, bf16[256,1024]{1,0:T(8,128)(2,1)}, u32[]{:S(2)}, u32[]{:S(2)}) collective-permute-start(bf16[256,1024]{1,0:T(8,128)(2,1)S(1)} %bitcast.101), channel_id=1, source_target_pairs={{0,4},{4,0},{8,12},{12,8},{16,20},{20,16},{24,28},{28,24},{1,5},{5... | collective-permute-start | bytes 1572872 | tf_op jit(solution)/shard_map/ppermute | solution.py:24
  29.3 22.4 %collective-permute-start.4 = (bf16[256,1024]{1,0:T(8,128)(2,1)S(1)}, bf16[256,1024]{1,0:T(8,128)(2,1)}, u32[]{:S(2)}, u32[]{:S(2)}) collective-permute-start(bf16[256,1024]{1,0:T(8,128)(2,1)S(1)} %collective-permute-done.refs_1_), channel_id=1, source_target_pairs={{0,4},{4,0},{8,12},{12,8},{16,20},{20,16},{24,28},{28,24},{1,5},{5... | collective-permute-start | bytes 1572872 | tf_op jit(solution)/shard_map/ppermute | solution.py:24
  46.7 41.3 %collective-permute-start.14 = (bf16[128,3712]{1,0:T(8,128)(2,1)}, bf16[128,3712]{1,0:T(8,128)(2,1)}, u32[]{:S(2)}, u32[]{:S(2)}) collective-permute-start(bf16[128,3712]{1,0:T(8,128)(2,1)} %collective-permute-done.10.refs_1_.refs_2_), channel_id=1, source_target_pairs={{0,4},{4,0},{8,12},{12,8},{16,20},{20,16},{24,28},{28,24},{1,5},{5... | collective-permute-start | bytes 2850824 | tf_op jit(solution)/shard_map/ppermute | solution.py:24
  50.5 32.3 %collective-permute-start.12 = (bf16[128,3712]{1,0:T(8,128)(2,1)}, bf16[128,3712]{1,0:T(8,128)(2,1)}, u32[]{:S(2)}, u32[]{:S(2)}) collective-permute-start(bf16[128,3712]{1,0:T(8,128)(2,1)} %get-tuple-element.71), channel_id=1, source_target_pairs={{0,2},{1,3},{2,0},{3,1},{4,5},{5,4},{6,7},{7,6},{8,10},{9,11},{10,... | collective-permute-start | bytes 2850824 | tf_op jit(solution)/shard_map/ppermute | solution.py:46
  51.7 32.4 %collective-permute-start.13 = (bf16[128,3712]{1,0:T(8,128)(2,1)}, bf16[128,3712]{1,0:T(8,128)(2,1)}, u32[]{:S(2)}, u32[]{:S(2)}) collective-permute-start(bf16[128,3712]{1,0:T(8,128)(2,1)} %collective-permute-done.10.refs_1_.refs_2_), channel_id=1, source_target_pairs={{0,2},{1,3},{2,0},{3,1},{4,5},{5,4},{6,7},{7,6},{8,10},{9,11},{10,... | collective-permute-start | bytes 2850824 | tf_op jit(solution)/shard_map/ppermute | solution.py:46
  52.0 50.5 %collective-permute-start.17 = (bf16[128,5248]{1,0:T(8,128)(2,1)}, bf16[128,5248]{1,0:T(8,128)(2,1)S(1)}, u32[]{:S(2)}, u32[]{:S(2)}) collective-permute-start(bf16[128,5248]{1,0:T(8,128)(2,1)} %get-tuple-element.75), channel_id=1, source_target_pairs={{0,2},{1,3},{2,0},{3,1},{4,5},{5,4},{6,7},{7,6},{8,10},{9,11},{10,... | collective-permute-start | bytes 4030472 | tf_op jit(solution)/shard_map/ppermute | solution.py:46
  53.3 50.2 %collective-permute-start.18 = (bf16[128,5248]{1,0:T(8,128)(2,1)S(1)}, bf16[128,5248]{1,0:T(8,128)(2,1)}, u32[]{:S(2)}, u32[]{:S(2)}) collective-permute-start(bf16[128,5248]{1,0:T(8,128)(2,1)S(1)} %collective-permute-done.11.refs_8_), channel_id=1, source_target_pairs={{0,2},{1,3},{2,0},{3,1},{4,5},{5,4},{6,7},{7,6},{8,10},{9,11},{10,... | collective-permute-start | bytes 4030472 | tf_op jit(solution)/shard_map/ppermute | solution.py:46
  147.0 51.3 %collective-permute-start.24 = (bf16[2,128,5248]{2,1,0:T(8,128)(2,1)}, bf16[2,128,5248]{2,1,0:T(8,128)(2,1)S(1)}, u32[]{:S(2)}, u32[]{:S(2)}) collective-permute-start(bf16[2,128,5248]{2,1,0:T(8,128)(2,1)} %get-tuple-element.83), channel_id=1, source_target_pairs={{0,2},{1,3},{2,0},{3,1},{4,5},{5,4},{6,7},{7,6},{8,10},{9,11},{10,... | collective-permute-start | bytes 8060936 | tf_op jit(solution)/shard_map/ppermute | solution.py:46
  186.4 19.9 %collective-permute-start.22 = (bf16[256,5760]{1,0:T(8,128)(2,1)}, bf16[256,5760]{1,0:T(8,128)(2,1)}, u32[]{:S(2)}, u32[]{:S(2)}) collective-permute-start(bf16[256,5760]{1,0:T(8,128)(2,1)} %get-tuple-element.97.keep_ref), channel_id=1, source_target_pairs={{0,4},{4,0},{8,12},{12,8},{16,20},{20,16},{24,28},{28,24},{1,5},{5... | collective-permute-start | bytes 8847368 | tf_op jit(solution)/shard_map/ppermute | solution.py:24
  196.0 34.1 %collective-permute-start.27 = (bf16[2,256,1024]{2,1,0:T(8,128)(2,1)}, bf16[2,256,1024]{2,1,0:T(8,128)(2,1)}, u32[]{:S(2)}, u32[]{:S(2)}) collective-permute-start(bf16[2,256,1024]{2,1,0:T(8,128)(2,1)} %add_convert_fusion.1), channel_id=1, source_target_pairs={{0,8},{4,20},{8,0},{12,28},{16,24},{20,4},{24,16},{28,12},{1,9},{5... | collective-permute-start | bytes 3145736 | tf_op jit(solution)/shard_map/ppermute | solution.py:74
  199.7 27.5 %collective-permute-start.35 = (bf16[128,5248]{1,0:T(8,128)(2,1)}, bf16[128,5248]{1,0:T(8,128)(2,1)}, u32[]{:S(2)}, u32[]{:S(2)}) collective-permute-start(bf16[128,5248]{1,0:T(8,128)(2,1)} %fusion), channel_id=1, source_target_pairs={{0,1},{1,0},{2,3},{3,2},{4,6},{5,7},{6,4},{7,5},{8,9},{9,8},{10,11... | collective-permute-start | bytes 4030472 | tf_op jit(solution)/shard_map/ppermute | solution.py:46
  215.1 23.0 %collective-permute-start.26 = (bf16[2,4,912,128]{3,2,1,0:T(8,128)(2,1)}, bf16[2,4,912,128]{3,2,1,0:T(8,128)(2,1)}, u32[]{:S(2)}, u32[]{:S(2)}) collective-permute-start(bf16[2,4,912,128]{3,2,1,0:T(8,128)(2,1)} %get-tuple-element.96), channel_id=1, source_target_pairs={{0,2},{1,3},{2,0},{3,1},{4,5},{5,4},{6,7},{7,6},{8,10},{9,11},{10,... | collective-permute-start | bytes 5603336 | tf_op jit(solution)/shard_map/ppermute | solution.py:46
  228.5 20.6 %collective-permute-start.36 = (bf16[2,32,5248]{2,1,0:T(8,128)(2,1)S(1)}, bf16[2,32,5248]{2,1,0:T(8,128)(2,1)S(1)}, u32[]{:S(2)}, u32[]{:S(2)}) collective-permute-start(bf16[2,32,5248]{2,1,0:T(8,128)(2,1)S(1)} %fusion.1), channel_id=1, source_target_pairs={{0,8},{4,12},{8,0},{12,4},{16,24},{20,28},{24,16},{28,20},{1,9},{5... | collective-permute-start | bytes 2015240 | tf_op jit(solution)/shard_map/ppermute | solution.py:70
  232.4 37.4 %collective-permute-start.28 = (bf16[256,1024]{1,0:T(8,128)(2,1)}, bf16[256,1024]{1,0:T(8,128)(2,1)}, u32[]{:S(2)}, u32[]{:S(2)}) collective-permute-start(bf16[256,1024]{1,0:T(8,128)(2,1)} %fusion.7), channel_id=1, source_target_pairs={{0,16},{4,12},{8,24},{12,4},{16,0},{20,28},{24,8},{28,20},{1,17},{... | collective-permute-start | bytes 1572872 | tf_op jit(solution)/shard_map/ppermute | solution.py:74
  240.6 33.7 %collective-permute-start.29 = (bf16[4,912,128]{2,1,0:T(8,128)(2,1)}, bf16[4,912,128]{2,1,0:T(8,128)(2,1)}, u32[]{:S(2)}, u32[]{:S(2)}) collective-permute-start(bf16[4,912,128]{2,1,0:T(8,128)(2,1)} %fusion.2), channel_id=1, source_target_pairs={{0,1},{1,0},{2,3},{3,2},{4,6},{5,7},{6,4},{7,5},{8,9},{9,8},{10,11... | collective-permute-start | bytes 2801672 | tf_op jit(solution)/shard_map/ppermute | solution.py:46
  284.6 29.0 %collective-permute-start.39 = (bf16[2,32,5248]{2,1,0:T(8,128)(2,1)S(1)}, bf16[2,32,5248]{2,1,0:T(8,128)(2,1)S(1)}, u32[]{:S(2)}, u32[]{:S(2)}) collective-permute-start(bf16[2,32,5248]{2,1,0:T(8,128)(2,1)S(1)} %pad_maximum_fusion.refs_0_), channel_id=1, source_target_pairs={{0,8},{4,12},{8,0},{12,4},{16,24},{20,28},{24,16},{28,20},{1,9},{5... | collective-permute-start | bytes 2015240 | tf_op jit(solution)/shard_map/ppermute | solution.py:70
  284.7 44.8 %collective-permute-start.40 = (bf16[2,32,5248]{2,1,0:T(8,128)(2,1)S(1)}, bf16[2,32,5248]{2,1,0:T(8,128)(2,1)S(1)}, u32[]{:S(2)}, u32[]{:S(2)}) collective-permute-start(bf16[2,32,5248]{2,1,0:T(8,128)(2,1)S(1)} %pad_maximum_fusion.refs_0_), channel_id=1, source_target_pairs={{0,4},{4,0},{8,12},{12,8},{16,20},{20,16},{24,28},{28,24},{1,5},{5... | collective-permute-start | bytes 2015240 | tf_op jit(solution)/shard_map/ppermute | solution.py:24
  294.6 26.3 %collective-permute-start.32 = (bf16[256,384]{1,0:T(8,128)(2,1)S(1)}, bf16[256,384]{1,0:T(8,128)(2,1)S(1)}, u32[]{:S(2)}, u32[]{:S(2)}) collective-permute-start(bf16[256,384]{1,0:T(8,128)(2,1)S(1)} %fusion.11), channel_id=1, source_target_pairs={{0,16},{4,20},{8,24},{12,28},{16,0},{20,4},{24,8},{28,12},{1,17},{... | collective-permute-start | bytes 589832 | tf_op jit(solution)/shard_map/ppermute | solution.py:70
  320.9 18.7 %collective-permute-start.33 = (bf16[2,256,384]{2,1,0:T(8,128)(2,1)S(1)}, bf16[2,256,384]{2,1,0:T(8,128)(2,1)S(1)}, u32[]{:S(2)}, u32[]{:S(2)}) collective-permute-start(bf16[2,256,384]{2,1,0:T(8,128)(2,1)S(1)} %pad_maximum_fusion.2.refs_0_), channel_id=1, source_target_pairs={{0,8},{4,12},{8,0},{12,4},{16,24},{20,28},{24,16},{28,20},{1,9},{5... | collective-permute-start | bytes 1179656 | tf_op jit(solution)/shard_map/ppermute | solution.py:70
  326.7 21.3 %collective-permute-start.34 = (bf16[2,256,384]{2,1,0:T(8,128)(2,1)S(1)}, bf16[2,256,384]{2,1,0:T(8,128)(2,1)S(1)}, u32[]{:S(2)}, u32[]{:S(2)}) collective-permute-start(bf16[2,256,384]{2,1,0:T(8,128)(2,1)S(1)} %pad_maximum_fusion.2.refs_0_), channel_id=1, source_target_pairs={{0,4},{4,0},{8,12},{12,8},{16,20},{20,16},{24,28},{28,24},{1,5},{5... | collective-permute-start | bytes 1179656 | tf_op jit(solution)/shard_map/ppermute | solution.py:24
  (63 other events, 712.0 us)
